TPU v7x, 512 devices: a whole 4x4x16 slice. The times are simulated.
512 devices in a mesh: slab: 128 (over y_lo, x, z), cross: 4 (over y_hi, core).
Axes of the slice: x: 4, y: 4 (y_hi: 2, y_lo: 2; y = y_hi * 2 + y_lo), z: 16, core: 2. Of those that a mesh axis runs over, the one named last changes fastest.
Arguments:
- gas_state: float32 [16, 1024, 8192], P(None, 'slab', 'cross'), may hold values from -4 to 4, as said below
- parcel_record: float32 [5, 2097152], P(None, ('slab', 'cross')), may hold values from -4 to 4, as said below
- condensed_shares: float32 [12, 2097152], P(None, ('slab', 'cross')), may hold values from 0.02 to 0.2
- surface_steam_factor: float32 [12], replicated, may hold values from 0.2 to 2
- fine_cell: int32 [2097152], P(('slab', 'cross')), may hold values from 0 to 20479, as said below
- block_counts: int32 [16384], P(('slab', 'cross')), may hold values from 16 to 128, as said below
Outputs:
- parcel_next: float32 [5, 2097152], P(None, ('slab', 'cross'))
- fine_source: float32 [16, 1024, 8192], P(None, 'slab', 'cross')
- correction: float32 [64, 4096], replicated
Inputs may be any that keep to these rules, and one draw needn't show every extreme that they name: fine_cell is plane * 2048 + k, with plane 0 and 9 the neighbouring slabs' last and first planes; it never points outside the gas mesh, and is non-decreasing over each device's 4096 slots. The live parcels of each aligned block of 128 slots are its first block_counts slots; the last block of each device's 4096 slots is full. `gas_state`: rows 0 to 2 velocity, row 3 temperature from 1 to 2, rows 4 on vapour fractions from 0 to 0.1. `parcel_record`: rows 0 to 2 velocity, row 3 temperature from 0.6 to 0.9, row 4 mass from 0.5 to 3.
All inputs are finite; a program needn't handle non-finite values.
Results may differ from a plain program's by a relative error of at most 0.00002.
Values sent between devices are 32-bit elements; how exact they have to be, the bound alone decides.
A program may use at most 64 MiB of HBM per device.

v0:
```python
import jax
import jax.numpy as jnp
from jax import lax
from jax.sharding import PartitionSpec as P

BLOCK = 128
COARSE = 64
SWEEPS = 4


drag_rate = 0.5
evap_rate = 0.08
warming_speed = 0.3
latent_boiling_energy = 0.5
vapour_heat = 1.5
volume_inverse = 4.0


def with_halo(shard, sides, width):
    for axis, dim in sides:
        devices, length = (lax.axis_size(axis), shard.shape[dim])
        up = [(i, (i + 1) % devices) for i in range(devices - 1)]
        down = [(j, i) for i, j in up]
        last = lax.slice_in_dim(shard, length - width, length, axis=dim)
        leading = lax.slice_in_dim(shard, 0, width, axis=dim)
        before = lax.ppermute(last, axis, up)
        after = lax.ppermute(leading, axis, down)
        shard = jnp.concatenate([before, shard, after], axis=dim)
    return shard


def shifted(shard, axis, by):
    devices = lax.axis_size(axis)
    pairs = [(i, i + by) for i in range(devices) if 0 <= i + by < devices]
    return lax.ppermute(shard, axis, pairs)


def advance(
    ambient_layer_fields, parcel_record, condensed_shares, surface_steam_factor, alive_mask
):
    gas_velocity = ambient_layer_fields[0:3]
    ambient_thermal_level = ambient_layer_fields[3]
    gas_vapour = ambient_layer_fields[4:]
    parcel_velocity = parcel_record[0:3]
    parcel_thermal_level = parcel_record[3]
    parcel_weight_amount = parcel_record[4]
    slip_velocity = gas_velocity - parcel_velocity
    slip_squared = jnp.sum(slip_velocity * slip_velocity, axis=0)
    drag_factor = (
        drag_rate
        * jnp.power(parcel_weight_amount, -2.0 / 3.0)
        * (1.0 + 0.15 * jnp.power(slip_squared + 1.0, 0.3435))
    )
    following_motion = (parcel_velocity + drag_factor * gas_velocity) / (1.0 + drag_factor)
    surface_steam_share = (
        condensed_shares
        * surface_steam_factor[:, None]
        * jnp.exp(2.0 * (parcel_thermal_level - 0.75))
    )
    species_rates = evap_rate * parcel_weight_amount * (surface_steam_share - gas_vapour)
    evaporated_weight = jnp.sum(species_rates, axis=0)
    thermal_exchange = (
        warming_speed
        * (ambient_thermal_level - parcel_thermal_level)
        * jnp.power(parcel_weight_amount, 1.0 / 3.0)
    )
    following_thermal_level = (
        parcel_thermal_level
        + (thermal_exchange - latent_boiling_energy * evaporated_weight) / parcel_weight_amount
    )
    following_weight = parcel_weight_amount - evaporated_weight
    momentum_terms = (
        parcel_weight_amount * (parcel_velocity - following_motion)
        + evaporated_weight * following_motion
    )
    energy_terms = vapour_heat * evaporated_weight - thermal_exchange
    source_terms = jnp.concatenate([momentum_terms, energy_terms[None], species_rates], axis=0)
    source_terms = source_terms * (alive_mask * volume_inverse)
    updated_parcel_record = jnp.concatenate(
        [following_motion, following_thermal_level[None], following_weight[None]], axis=0
    )
    parcel_next = jnp.where(alive_mask[None] > 0.5, updated_parcel_record, parcel_record)
    return (source_terms, parcel_next, evaporated_weight * alive_mask)


def neighbours(values_grid):
    edge = values_grid.shape[0]
    padded_x = jnp.pad(values_grid, ((1, 1), (0, 0)))
    summed = padded_x[2:] + padded_x[:-2]
    padded_y = jnp.pad(values_grid, ((0, 0), (edge, edge)))
    summed = summed + padded_y[:, 2 * edge :] + padded_y[:, : -2 * edge]
    padded_z = jnp.pad(values_grid, ((0, 0), (1, 1)))
    depth = jnp.arange(values_grid.shape[1], dtype=jnp.int32) % edge
    upper_mask = (depth < edge - 1).astype(values_grid.dtype)
    lower_mask = (depth > 0).astype(values_grid.dtype)
    return summed + padded_z[:, 2:] * upper_mask + padded_z[:, :-2] * lower_mask


def relax(coarse_source):
    solution = jnp.zeros_like(coarse_source)
    for sweep in range(SWEEPS):
        solution = (neighbours(solution) + coarse_source) / 6.0
    return solution


def body(gas_state, parcel_record, condensed_shares, surface_steam_factor, fine_cell, block_counts):
    fields = gas_state.shape[0]
    planes = gas_state.shape[1]
    cross_cells = gas_state.shape[2]
    slab_count = lax.axis_size("slab")
    cross_count = lax.axis_size("cross")
    slab_index = lax.axis_index("slab")
    cross_index = lax.axis_index("cross")
    padded_gas = with_halo(gas_state, (("slab", 1),), 1)
    gas_flat = padded_gas.reshape(fields, (planes + 2) * cross_cells)
    ambient_layer_fields = jnp.take(gas_flat, fine_cell, axis=1)
    slot_in_block = jnp.arange(BLOCK, dtype=jnp.int32)
    alive_mask = (slot_in_block[None, :] < block_counts[:, None]).reshape(-1).astype(jnp.float32)
    source_terms, parcel_next, evaporated_weight = advance(
        ambient_layer_fields, parcel_record, condensed_shares, surface_steam_factor, alive_mask
    )
    extended = (
        jnp.zeros((fields, (planes + 2) * cross_cells), jnp.float32)
        .at[:, fine_cell]
        .add(source_terms)
    )
    extended = extended.reshape(fields, planes + 2, cross_cells)
    from_above = shifted(extended[:, 0], "slab", -1)
    from_below = shifted(extended[:, planes + 1], "slab", 1)
    fine_source = extended[:, 1 : planes + 1]
    fine_source = fine_source.at[:, planes - 1].add(from_above)
    fine_source = fine_source.at[:, 0].add(from_below)
    squared = COARSE * COARSE
    fine_per_coarse = planes * slab_count // COARSE
    cross_per_coarse = cross_cells * cross_count // squared
    plane_ext = fine_cell // cross_cells
    column = fine_cell % cross_cells
    global_plane = slab_index * planes + plane_ext - 1
    global_cross = cross_index * cross_cells + column
    coarse_plane = global_plane // fine_per_coarse
    coarse_column = global_cross // cross_per_coarse
    coarse_index = coarse_plane * squared + coarse_column
    coarse_local = (
        jnp.zeros((COARSE * squared,), jnp.float32).at[coarse_index].add(evaporated_weight)
    )
    coarse_local = coarse_local.reshape(COARSE, squared)
    coarse_source = lax.psum(coarse_local, ("slab", "cross"))
    correction = relax(coarse_source)
    return (parcel_next, fine_source, correction)


def solution(mesh):
    in_specs = (
        P(None, "slab", "cross"),
        P(None, ("slab", "cross")),
        P(None, ("slab", "cross")),
        P(),
        P(("slab", "cross")),
        P(("slab", "cross")),
    )
    out_specs = (P(None, ("slab", "cross")), P(None, "slab", "cross"), P())
    return jax.shard_map(body, mesh=mesh, in_specs=in_specs, out_specs=out_specs, check_vma=False)
```

profile of v0, /device:TPU:1, one launch (start us, length us, event | category | flops | bytes accessed | tf_op | source)
XLA Modules:
  0.0 604.7 jit_solution(12686420964390605401)
XLA Ops:
  7.2 0.0 all-reduce.14.cloned.1.call-start
  7.2 1.9 fusion.65
  9.2 1.3 collective-permute-start.1
  10.5 5.0 collective-permute-start
  15.5 0.7 compare_and_fusion
  16.2 1.4 compare_select_fusion
  17.6 0.7 convert_compare_fusion
  18.3 0.0 collective-permute-done.1
  18.4 0.1 copy.73
  18.5 0.1 copy.72
  18.7 0.4 pad_maximum_fusion
  19.0 5.4 copy.74
  24.5 14.8 %gather_fusion = f32[4096,16]{1,0:T(8,128)S(1)} fusion(f32[16,20480]{0,1:T(8,128)} %bitcast.31, s32[4096]{0:T(1024)S(1)} %get-tuple-element.58), kind=kCustom, calls=%fused_computation | custom fusion | bytes 540672 | tf_op jit(solution)/shard_map/jit(_take)/gather | solution.py:116
  39.2 0.0 copy-start.3
  39.3 0.0 copy-start.5
  39.3 0.0 copy-start.4
  39.3 0.6 copy.75
  39.9 0.1 multiply_reduce_fusion
  40.0 0.2 broadcast_add_fusion
  40.2 0.0 copy-done.3
  40.2 0.1 fusion.62
  40.4 0.7 fusion.52
  41.0 0.2 multiply_subtract_fusion
  41.2 0.1 divide_add_fusion
  41.3 0.1 multiply_add_fusion
  41.4 0.1 fusion.35
  41.4 0.6 copy.76
  42.0 27.0 %scatter_custom_fusion = f32[16,20480]{0,1:T(8,128)} fusion(s32[4096]{0:T(1024)S(1)} %get-tuple-element.59, f32[4096,16]{1,0:T(8,128)S(1)} %copy.76, f32[]{:T(128)} %constant.171.clone.1), kind=kCustom, calls=%fused_computation.3 | custom fusion | flops 65536 | bytes 1310724 | tf_op jit(solution)/shard_map/scatter-add | solution.py:125
  69.0 2.1 fusion.64
  71.1 0.3 copy.86
  71.4 1.3 collective-permute-start.2
  72.7 0.3 copy.87
  73.0 4.2 collective-permute-start.3
  77.2 29.4 %scatter_custom_fusion.1 = f32[262144]{0:T(1024)S(1)} fusion(s32[4096]{0:T(1024)} %get-tuple-element.57, f32[4096]{0:T(1024)} %get-tuple-element.60, f32[]{:T(128)} %constant.171.clone.1), kind=kCustom, calls=%fused_computation.48 | custom fusion | flops 4096 | bytes 1049088 | tf_op jit(solution)/shard_map/scatter-add | solution.py:144
  106.5 1.2 reshape.167
  107.7 0.0 all-reduce.14.cloned.1.call-update
  107.7 0.7 maximum_select_fusion
  108.4 7.3 %slice.192 = f32[16,8,2048]{0,2,1:T(8,128)} slice(f32[16,10,2048]{0,2,1:T(8,128)} %bitcast.30), slice={[0:16], [1:9], [0:2048]} | slice | bytes 2097152 | tf_op jit(solution)/shard_map/slice | solution.py:130
  115.8 5.1 copy.84
  120.9 0.3 copy.85
  121.2 0.0 collective-permute-done.2
  121.3 1.6 copy.81
  122.9 468.1 %all-reduce.14.cloned.1.call-done = f32[64,4096]{1,0:T(8,128)} async-done(((f32[64,4096]{1,0:T(8,128)}), f32[64,4096]{1,0:T(8,128)}) %all-reduce.14.cloned.1.call-update) | async-done | bytes 1048592 | tf_op jit(solution)/shard_map/psum | solution.py:147
  590.9 0.1 broadcast_in_dim.33
  591.0 2.4 fusion.28
  593.5 1.1 fusion.8
  594.6 1.1 fusion.15
  595.8 2.1 fusion.22
  (17 shorter events, 0.2 us)
Async XLA Ops:
  7.2 11.5 %copy-start.1 = (f32[16,8,2048]{2,1,0:T(8,128)S(1)}, f32[16,8,2048]{2,1,0:T(8,128)}, u32[]{:S(2)}) copy-start(f32[16,8,2048]{2,1,0:T(8,128)} %param.10) | copy-start | bytes 3145732
  7.2 583.7 %all-reduce.14.cloned.1.call-start = ((), (), s32[]{:S(2)}) async-start(), calls=%async_computation | async-start | bytes 2097152 | tf_op jit(solution)/shard_map/psum | solution.py:147
  9.2 9.2 %collective-permute-start.1 = (f32[16,1,2048]{2,0,1:T(8,128)S(1)}, f32[16,1,2048]{2,0,1:T(8,128)S(1)}, u32[]{:S(2)}, u32[]{:S(2)}) collective-permute-start(f32[16,1,2048]{2,0,1:T(8,128)S(1)} %copy.83), channel_id=1, source_target_pairs={{4,0},{8,4},{12,8},{16,12},{20,16},{24,20},{28,24},{32,28},{36,32}... | collective-permute-start | bytes 393224 | tf_op jit(solution)/shard_map/ppermute | solution.py:27
  10.5 8.0 %collective-permute-start = (f32[16,1,2048]{2,0,1:T(8,128)S(1)}, f32[16,1,2048]{2,0,1:T(8,128)S(1)}, u32[]{:S(2)}, u32[]{:S(2)}) collective-permute-start(f32[16,1,2048]{2,0,1:T(8,128)S(1)} %copy.82), channel_id=1, source_target_pairs={{0,4},{4,8},{8,12},{12,16},{16,20},{20,24},{24,28},{28,32},{32,36}... | collective-permute-start | bytes 393224 | tf_op jit(solution)/shard_map/ppermute | solution.py:26
  24.5 15.4 %copy-start.2 = (f32[5,4096]{1,0:T(8,128)S(1)}, f32[5,4096]{1,0:T(8,128)}, u32[]{:S(2)}) copy-start(f32[5,4096]{1,0:T(8,128)} %param.11) | copy-start | bytes 245764
  39.2 1.0 copy-start.3
  39.3 0.9 copy-start.5
  39.3 1.1 copy-start.4
  71.4 49.8 %collective-permute-start.2 = (f32[16,2048]{1,0:T(8,128)S(1)}, f32[16,2048]{1,0:T(8,128)S(1)}, u32[]{:S(2)}, u32[]{:S(2)}) collective-permute-start(f32[16,2048]{1,0:T(8,128)S(1)} %bitcast.35), channel_id=1, source_target_pairs={{4,0},{8,4},{12,8},{16,12},{20,16},{24,20},{28,24},{32,28},{36,32}... | collective-permute-start | bytes 393224 | tf_op jit(solution)/shard_map/ppermute | solution.py:35
  73.0 48.3 %collective-permute-start.3 = (f32[16,2048]{1,0:T(8,128)S(1)}, f32[16,2048]{1,0:T(8,128)S(1)}, u32[]{:S(2)}, u32[]{:S(2)}) collective-permute-start(f32[16,2048]{1,0:T(8,128)S(1)} %bitcast.34), channel_id=1, source_target_pairs={{0,4},{4,8},{8,12},{12,16},{16,20},{20,24},{24,28},{28,32},{32,36}... | collective-permute-start | bytes 393224 | tf_op jit(solution)/shard_map/ppermute | solution.py:35
  590.9 2.5 copy-start
Sparse Core Ops, SparseCore 0:
  107.9 483.0 all-reduce.13
where the time goes:
time: 605 us
  waiting for transfers between devices  468 us (77%)
  other arithmetic  68.7 us (11%)
  local copies, waits for them, and re-layouts  41.8 us (7%)
  between operations  14.3 us (2%)
  starting transfers between devices  11.8 us (2%)
    psum x1, waiting for transfers between devices, body(): coarse_source = lax.psum(coarse_local, ('slab', 'cross'))  468 us
    scatter-add x1, other arithmetic, body(): jnp.zeros((COARSE * squared,), jnp.float32).at[coarse_index]  29.4 us
    scatter-add x1, other arithmetic, body(): extended = jnp.zeros((fields, (planes + 2) * cross_cells), jnp.float32).a...  27 us
    gather x2, local copies, waits for them, and re-layouts, body(): ambient_layer_fields = jnp.take(gas_flat, fine_cell, axis=1)  15.3 us
  transfers between devices with their start and end apart: 5, of which 1 were waited for; matrix products, arithmetic and copies ran while one was open for 8% of the time, Pallas kernels for 0%

commit v1 on v0

--- a/solution.py
+++ b/solution.py
@@ -109,8 +109,6 @@
     cross_cells = gas_state.shape[2]
     slab_count = lax.axis_size("slab")
     cross_count = lax.axis_size("cross")
-    slab_index = lax.axis_index("slab")
-    cross_index = lax.axis_index("cross")
     padded_gas = with_halo(gas_state, (("slab", 1),), 1)
     gas_flat = padded_gas.reshape(fields, (planes + 2) * cross_cells)
     ambient_layer_fields = jnp.take(gas_flat, fine_cell, axis=1)
@@ -130,21 +128,11 @@
     fine_source = extended[:, 1 : planes + 1]
     fine_source = fine_source.at[:, planes - 1].add(from_above)
     fine_source = fine_source.at[:, 0].add(from_below)
-    squared = COARSE * COARSE
-    fine_per_coarse = planes * slab_count // COARSE
-    cross_per_coarse = cross_cells * cross_count // squared
-    plane_ext = fine_cell // cross_cells
-    column = fine_cell % cross_cells
-    global_plane = slab_index * planes + plane_ext - 1
-    global_cross = cross_index * cross_cells + column
-    coarse_plane = global_plane // fine_per_coarse
-    coarse_column = global_cross // cross_per_coarse
-    coarse_index = coarse_plane * squared + coarse_column
-    coarse_local = (
-        jnp.zeros((COARSE * squared,), jnp.float32).at[coarse_index].add(evaporated_weight)
-    )
-    coarse_local = coarse_local.reshape(COARSE, squared)
-    coarse_source = lax.psum(coarse_local, ("slab", "cross"))
+    fold = cross_cells * cross_count // (COARSE * COARSE)
+    mass = 0.25 * fine_source[4:].sum(axis=(0, 1))
+    piece = mass.reshape(cross_cells // fold, fold).sum(axis=1)
+    pieces = lax.all_gather(piece, ("slab", "cross"))
+    coarse_source = pieces.reshape(COARSE, slab_count // COARSE, COARSE * COARSE).sum(axis=1)
     correction = relax(coarse_source)
     return (parcel_next, fine_source, correction)
 

time: 605 us -> 893 us (1.48)
  waiting for transfers between devices: 468 us -> 780 us
  other arithmetic: 68.7 us -> 41.3 us
    all_gather x0 -> x1, waiting for transfers between devices: none -> 777 us  [body(): pieces = lax.all_gather(piece, ('slab', 'cross'))]
    psum x1 -> x0, waiting for transfers between devices: 468 us -> none  [body(): coarse_source = lax.psum(coarse_local, ('slab', 'cross'))]
    scatter-add x1 -> x0, other arithmetic: 29.4 us -> none  [body(): jnp.zeros((COARSE * squared,), jnp.float32).at[coarse_index]]
  transfers between devices with their start and end apart: 5 -> 5, of which waited for: 1 -> 3; matrix products, arithmetic and copies ran while one was open for 8% -> 2% of each run, Pallas kernels for 0% -> 0%
where the time goes in v1:
time: 893 us; the launch traced here: 892 us
  waiting for transfers between devices  780 us (87%)
  local copies, waits for them, and re-layouts  44.2 us (5%)
  other arithmetic  41.3 us (5%)
  between operations  14.3 us (2%)
  starting transfers between devices  11.8 us (1%)
    all_gather x1, waiting for transfers between devices, body(): pieces = lax.all_gather(piece, ('slab', 'cross'))  777 us
    scatter-add x1, other arithmetic, body(): extended = jnp.zeros((fields, (planes + 2) * cross_cells), jnp.float32).a...  26.9 us
  transfers between devices with their start and end apart: 5, of which 3 were waited for; matrix products, arithmetic and copies ran while one was open for 2% of the time, Pallas kernels for 0%

profile of v1, /device:TPU:1, one launch (start us, length us, event | category | flops | bytes accessed | tf_op | source)
XLA Modules:
  0.0 892.1 jit_solution(4289212892308016385)
XLA Ops:
  7.2 0.0 all-gather.3.cloned.1.call-start
  7.2 2.0 fusion.50
  9.2 4.4 collective-permute-start
  13.7 1.3 collective-permute-start.1
  15.0 0.7 compare_select_fusion
  15.7 0.7 compare_and_fusion
  16.4 0.7 select_bitcast_fusion.1
  17.2 0.1 copy.133
  17.3 2.3 collective-permute-done.1
  19.6 0.1 copy.134
  19.7 0.4 pad_maximum_fusion
  20.1 5.4 copy.135
  25.5 14.8 %gather_fusion = f32[4096,16]{1,0:T(8,128)S(1)} fusion(f32[16,20480]{0,1:T(8,128)} %bitcast.27, s32[4096]{0:T(1024)S(1)} %get-tuple-element.64), kind=kCustom, calls=%fused_computation | custom fusion | bytes 540672 | tf_op jit(solution)/shard_map/jit(_take)/gather | solution.py:114
  40.3 0.6 copy.136
  40.9 0.1 multiply_reduce_fusion
  41.0 0.2 broadcast_add_fusion
  41.2 0.0 copy-done.2
  41.2 0.1 fusion.47
  41.4 0.2 multiply_subtract_fusion
  41.6 0.1 multiply_add_fusion
  41.6 0.1 fusion.33
  41.7 0.6 copy.137
  42.3 26.9 %scatter_custom_fusion = f32[16,20480]{0,1:T(8,128)} fusion(s32[4096]{0:T(1024)S(1)} %get-tuple-element.63, f32[4096,16]{1,0:T(8,128)S(1)} %copy.137, f32[]{:T(128)} %constant.122.clone.1), kind=kCustom, calls=%fused_computation.2 | custom fusion | flops 65536 | bytes 1310724 | tf_op jit(solution)/shard_map/scatter-add | solution.py:123
  69.3 2.1 fusion.49
  71.3 1.0 copy.149
  72.3 1.3 collective-permute-start.2
  73.6 7.3 slice.196
  80.9 5.1 copy.147
  86.0 0.3 copy.148
  86.3 0.3 copy.150
  86.6 4.8 collective-permute-start.3
  91.5 0.9 fusion.35
  92.4 0.8 collective-permute-done.3
  93.2 0.1 slice_reduce_fusion
  93.4 0.5 mul.266
  93.9 0.8 reduce_sum.51
  94.7 0.1 fusion.42
  94.8 0.1 divide_add_fusion
  94.8 0.7 maximum_select_fusion
  95.6 1.6 copy.143
  97.1 777.4 %all-gather.3.cloned.1.call-done = f32[524288]{0:T(1024)} async-done(((f32[1024]{0:T(1024)}), f32[524288]{0:T(1024)}) %all-gather.3.cloned.1.call-update) | async-done | bytes 2097168 | tf_op jit(solution)/shard_map/all_gather | solution.py:134
  874.5 2.4 reshape.177
  876.9 2.7 reduce_sum.52
  879.6 0.1 broadcast_in_dim.29
  879.7 1.1 fusion.28
  880.8 1.1 fusion.8
  882.0 1.1 fusion.15
  883.1 2.1 fusion.22
  (19 shorter events, 0.2 us)
Async XLA Ops:
  7.2 12.5 %copy-start = (f32[16,8,2048]{2,1,0:T(8,128)S(1)}, f32[16,8,2048]{2,1,0:T(8,128)}, u32[]{:S(2)}) copy-start(f32[16,8,2048]{2,1,0:T(8,128)} %param.10) | copy-start | bytes 3145732
  7.2 867.3 %all-gather.3.cloned.1.call-start = ((), (), s32[]{:S(2)}) async-start(), calls=%async_computation | async-start | bytes 2101248 | tf_op jit(solution)/shard_map/all_gather | solution.py:134
  9.2 7.9 collective-permute-start
  13.7 5.9 collective-permute-start.1
  25.5 15.4 %copy-start.1 = (f32[5,4096]{1,0:T(8,128)S(1)}, f32[5,4096]{1,0:T(8,128)}, u32[]{:S(2)}) copy-start(f32[5,4096]{1,0:T(8,128)} %param.11) | copy-start | bytes 245764
  40.3 1.0 copy-start.2
  40.3 0.9 copy-start.4
  72.3 19.2 %collective-permute-start.2 = (f32[16,2048]{1,0:T(8,128)}, f32[16,2048]{1,0:T(8,128)}, u32[]{:S(2)}, u32[]{:S(2)}) collective-permute-start(f32[16,2048]{1,0:T(8,128)} %bitcast.13), channel_id=1, source_target_pairs={{4,0},{8,4},{12,8},{16,12},{20,16},{24,20},{28,24},{32,28},{36,32}... | collective-permute-start | bytes 393224 | tf_op jit(solution)/shard_map/ppermute | solution.py:35
  86.3 8.4 copy-start.3
  86.6 6.6 collective-permute-start.3
Sparse Core Ops, SparseCore 0:
  94.8 779.6 all-gather.2

commit v2 on v1

--- a/solution.py
+++ b/solution.py
@@ -1,11 +1,12 @@
 import jax
 import jax.numpy as jnp
 from jax import lax
+from jax.experimental import pallas as pl
+from jax.experimental.pallas import tpu as pltpu
 from jax.sharding import PartitionSpec as P
 
 BLOCK = 128
 COARSE = 64
-SWEEPS = 4
 
 
 drag_rate = 0.5
@@ -27,12 +28,6 @@
         after = lax.ppermute(leading, axis, down)
         shard = jnp.concatenate([before, shard, after], axis=dim)
     return shard
-
-
-def shifted(shard, axis, by):
-    devices = lax.axis_size(axis)
-    pairs = [(i, i + by) for i in range(devices) if 0 <= i + by < devices]
-    return lax.ppermute(shard, axis, pairs)
 
 
 def advance(
@@ -83,32 +78,258 @@
     return (source_terms, parcel_next, evaporated_weight * alive_mask)
 
 
-def neighbours(values_grid):
-    edge = values_grid.shape[0]
-    padded_x = jnp.pad(values_grid, ((1, 1), (0, 0)))
-    summed = padded_x[2:] + padded_x[:-2]
-    padded_y = jnp.pad(values_grid, ((0, 0), (edge, edge)))
-    summed = summed + padded_y[:, 2 * edge :] + padded_y[:, : -2 * edge]
-    padded_z = jnp.pad(values_grid, ((0, 0), (1, 1)))
-    depth = jnp.arange(values_grid.shape[1], dtype=jnp.int32) % edge
-    upper_mask = (depth < edge - 1).astype(values_grid.dtype)
-    lower_mask = (depth > 0).astype(values_grid.dtype)
-    return summed + padded_z[:, 2:] * upper_mask + padded_z[:, :-2] * lower_mask
-
-
-def relax(coarse_source):
-    solution = jnp.zeros_like(coarse_source)
-    for sweep in range(SWEEPS):
-        solution = (neighbours(solution) + coarse_source) / 6.0
-    return solution
+LINE = 16
+RING = 4
+LANES = 128
+ROWS = 8
+
+
+def spread_kernel(
+    own_ref, outer_ref, edge_ref, halo_ref, grid_ref, got,
+    pair_send, pair_recv, edge_send, edge_recv, line_send, line_recv,
+    minor_send, minor_recv, major_send, major_recv, core_send, core_recv,
+):
+    slabs = 2 * RING * LINE
+    slab = lax.axis_index("slab")
+    cross = lax.axis_index("cross")
+    core = lax.rem(cross, 2)
+    z = lax.rem(slab, LINE)
+    x = lax.rem(lax.div(slab, LINE), RING)
+    y = lax.div(cross, 2) * 2 + lax.div(slab, RING * LINE)
+    odd = lax.rem(slab, 2)
+    sign = 2 * odd - 1
+    pair = lax.div(slab, 2)
+    line_pair = lax.div(z, 2)
+    major = core * x + (1 - core) * y
+    minor = core * y + (1 - core) * x
+
+    def near(by):
+        return (lax.rem(slab + by + slabs, slabs), cross)
+
+    def place(at_x, at_y, at_z):
+        return (lax.rem(at_y, 2) * (RING * LINE) + at_x * LINE + at_z, lax.div(at_y, 2) * 2 + core)
+
+    def in_line(by):
+        return lax.rem(z + by + LINE, LINE)
+
+    def minor_peer(other):
+        return place(core * x + (1 - core) * other, core * other + (1 - core) * y, z)
+
+    def major_peer(other):
+        return place(core * other + (1 - core) * x, core * y + (1 - core) * other, z)
+
+    def turn(own, by):
+        return lax.rem(own + by, RING)
+
+    def copy(src, dst, send, recv, device):
+        return pltpu.make_async_remote_copy(
+            src_ref=src, dst_ref=dst, send_sem=send, recv_sem=recv,
+            device_id=device, device_id_type=pl.DeviceIdType.MESH,
+        )
+
+    other_core = (slab, cross + 1 - 2 * core)
+    line_from = [sign * k for k in (1, 3, 5, 7)] + [-sign * k for k in (2, 4, 6)]
+    low = lax.rem(2 * pair - 1 + slabs, slabs)
+    high = lax.rem(2 * pair + 2, slabs)
+
+    barrier = pltpu.get_barrier_semaphore()
+    sources = [near(-sign), (low, cross), (high, cross), near(-1), near(1)]
+    sources += [place(x, y, in_line(by)) for by in line_from]
+    sources += [minor_peer(turn(minor, by)) for by in (1, 2, 3)]
+    sources += [major_peer(turn(major, by)) for by in (1, 2, 3)]
+    sources += [other_core]
+    for device in sources:
+        pl.semaphore_signal(barrier, inc=1, device_id=device, device_id_type=pl.DeviceIdType.MESH)
+    pl.semaphore_wait(barrier, len(sources))
+
+    copies = [
+        copy(own_ref, got.at[0], pair_send.at[0], pair_recv.at[0], near(-sign)),
+        copy(outer_ref, got.at[2 - odd], pair_send.at[1], pair_recv.at[2 - odd], near(sign)),
+        copy(outer_ref, got.at[2 - odd], pair_send.at[2], pair_recv.at[2 - odd], near(2 * sign)),
+    ]
+    for each in copies:
+        each.start()
+    for slot in range(3):
+        copy(own_ref, got.at[slot], pair_send.at[slot], pair_recv.at[slot], near(1)).wait_recv()
+    grid_ref[core, major, minor, line_pair] = (own_ref[...] + got[0]) + (got[1] + got[2])
+    edges = [
+        copy(edge_ref.at[0], halo_ref.at[1], edge_send.at[0], edge_recv.at[1], near(-1)),
+        copy(edge_ref.at[1], halo_ref.at[0], edge_send.at[1], edge_recv.at[0], near(1)),
+    ]
+    tile = grid_ref.at[core, major, minor, line_pair]
+    line = [
+        copy(tile, tile, line_send.at[k - 1], line_recv.at[line_pair], place(x, y, in_line(sign * k)))
+        for k in range(1, 8)
+    ]
+    for each in line:
+        each.start()
+    for each in edges:
+        each.start()
+    for by in line_from:
+        other = lax.div(in_line(by), 2)
+        copy(
+            tile, grid_ref.at[core, major, minor, other], line_send.at[0], line_recv.at[other], near(1)
+        ).wait_recv()
+
+    block = grid_ref.at[core, major, minor]
+    minors = [
+        copy(block, block, minor_send.at[by - 1], minor_recv.at[minor], minor_peer(turn(minor, by)))
+        for by in (1, 2, 3)
+    ]
+    for each in minors:
+        each.start()
+    for by in (1, 2, 3):
+        other = turn(minor, by)
+        copy(
+            block, grid_ref.at[core, major, other], minor_send.at[0], minor_recv.at[other], near(1)
+        ).wait_recv()
+
+    row = grid_ref.at[core, major]
+    majors = [
+        copy(row, row, major_send.at[by - 1], major_recv.at[major], major_peer(turn(major, by)))
+        for by in (1, 2, 3)
+    ]
+    for each in majors:
+        each.start()
+    cores = []
+    for by in range(RING):
+        other = turn(major, by)
+        arrived = grid_ref.at[core, other]
+        if by:
+            copy(row, arrived, major_send.at[0], major_recv.at[other], near(1)).wait_recv()
+        each = copy(arrived, arrived, core_send.at[by], core_recv.at[other], other_core)
+        each.start()
+        cores.append(each)
+    for by in range(RING):
+        far = grid_ref.at[1 - core, by]
+        copy(far, far, core_send.at[0], core_recv.at[by], other_core).wait_recv()
+    for slot in range(2):
+        copy(edge_ref.at[0], halo_ref.at[slot], edge_send.at[0], edge_recv.at[slot], near(1)).wait_recv()
+    for each in copies + edges + line + minors + majors + cores:
+        each.wait_send()
+
+
+def spread(own, outer, edges):
+    dma = pltpu.SemaphoreType.DMA
+    vmem = pl.BlockSpec(memory_space=pltpu.VMEM)
+    hbm = pl.BlockSpec(memory_space=pl.ANY)
+    return pl.pallas_call(
+        spread_kernel,
+        out_shape=(
+            jax.ShapeDtypeStruct(edges.shape, jnp.float32),
+            jax.ShapeDtypeStruct((2, RING, RING, LINE // 2, ROWS, LANES), jnp.float32),
+        ),
+        in_specs=[vmem, vmem, hbm],
+        out_specs=(hbm, vmem),
+        scratch_shapes=[
+            pltpu.VMEM((3, ROWS, LANES), jnp.float32),
+            dma((3,)), dma((3,)), dma((2,)), dma((2,)), dma((7,)), dma((LINE // 2,)),
+            dma((3,)), dma((RING,)), dma((3,)), dma((RING,)), dma((RING,)), dma((RING,)),
+        ],
+        compiler_params=pltpu.CompilerParams(
+            collective_id=0, has_side_effects=True, vmem_limit_bytes=8 << 20
+        ),
+        name="spread",
+    )(own, outer, edges)
+
+
+def finish_kernel(base_ref, halo_ref, grid_ref, fine_ref, out_ref, source, even, uneven):
+    fields, planes, cells = base_ref.shape
+    row = lax.broadcasted_iota(jnp.int32, (planes, cells), 0)
+    first = row == 0
+    last = row == planes - 1
+    for f in range(fields):
+        low = jnp.broadcast_to(halo_ref[0, f : f + 1, :], (planes, cells))
+        high = jnp.broadcast_to(halo_ref[1, f : f + 1, :], (planes, cells))
+        fine_ref[f] = base_ref[f] + jnp.where(first, low, jnp.where(last, high, 0.0))
+
+    half = RING * RING * (LINE // 2) * ROWS
+    tiles = COARSE * COARSE // LANES
+    blank = jnp.zeros((ROWS, tiles * LANES), jnp.float32)
+    for held in (even, uneven):
+        held[0:ROWS, :] = blank
+        held[COARSE + ROWS : COARSE + 2 * ROWS, :] = blank
+    for k in range(tiles):
+        y_hi, core, i = k // 16, (k // 8) % 2, k % 8
+        cols = slice(k * LANES, (k + 1) * LANES)
+        for t in range(COARSE // ROWS):
+            y_lo, x = t // RING, t % RING
+            if core == 0:
+                at = ((y_hi * 2 + y_lo) * RING + x) * (LINE // 2) * ROWS + i
+            else:
+                at = half + (x * RING + y_hi * 2 + y_lo) * (LINE // 2) * ROWS + i
+            value = grid_ref[pl.ds(at, ROWS, stride=ROWS), :] * (1.0 / 6.0)
+            source[t * ROWS : (t + 1) * ROWS, cols] = value
+            even[(t + 1) * ROWS : (t + 2) * ROWS, cols] = value
+
+    lane = lax.broadcasted_iota(jnp.int32, (ROWS, LANES), 1)
+    edge = LANES // 2
+    depth = lax.rem(lane, edge)
+    upper = depth < edge - 1
+    lower = depth > 0
+    left = lane < edge
+
+    def sweep(src, dst, top):
+        def one(t, carry):
+            at = pl.multiple_of(t * ROWS, ROWS)
+            rolled = []
+            mid = []
+            for k in range(tiles):
+                cols = slice(k * LANES, (k + 1) * LANES)
+                value = src[pl.ds(at + ROWS, ROWS), cols]
+                mid.append(value)
+                rolled.append(pltpu.roll(value, edge, 1))
+            none = jnp.zeros((ROWS, LANES), jnp.float32)
+            for k in range(tiles):
+                cols = slice(k * LANES, (k + 1) * LANES)
+                before = rolled[k - 1] if k else none
+                after = rolled[k + 1] if k + 1 < tiles else none
+                total = rolled[k] + jnp.where(left, before, after)
+                total += jnp.where(upper, pltpu.roll(mid[k], LANES - 1, 1), 0.0)
+                total += jnp.where(lower, pltpu.roll(mid[k], 1, 1), 0.0)
+                sub = lax.broadcasted_iota(jnp.int32, (ROWS, LANES), 0)
+                up = src[pl.ds(at, ROWS), cols]
+                down = src[pl.ds(at + 2 * ROWS, ROWS), cols]
+                total += jnp.where(sub == 0, pltpu.roll(up, 1, 0), pltpu.roll(mid[k], 1, 0))
+                total += jnp.where(
+                    sub == ROWS - 1, pltpu.roll(down, ROWS - 1, 0), pltpu.roll(mid[k], ROWS - 1, 0)
+                )
+                dst[pl.ds(at + top, ROWS), cols] = total * (1.0 / 6.0) + source[pl.ds(at, ROWS), cols]
+            return carry
+
+        lax.fori_loop(0, COARSE // ROWS, one, 0)
+
+    sweep(even, uneven, ROWS)
+    sweep(uneven, even, ROWS)
+    sweep(even, out_ref, 0)
+
+
+def finish(base, halo, grid):
+    side = (COARSE, COARSE * COARSE)
+    padded = (COARSE + 2 * ROWS, COARSE * COARSE)
+    vmem = pl.BlockSpec(memory_space=pltpu.VMEM)
+    return pl.pallas_call(
+        finish_kernel,
+        out_shape=(
+            jax.ShapeDtypeStruct(base.shape, jnp.float32),
+            jax.ShapeDtypeStruct(side, jnp.float32),
+        ),
+        in_specs=[vmem, vmem, vmem],
+        out_specs=(vmem, vmem),
+        scratch_shapes=[
+            pltpu.VMEM(side, jnp.float32),
+            pltpu.VMEM(padded, jnp.float32),
+            pltpu.VMEM(padded, jnp.float32),
+        ],
+        compiler_params=pltpu.CompilerParams(vmem_limit_bytes=32 << 20),
+        name="finish",
+    )(base, halo, grid.reshape(-1, LANES))
 
 
 def body(gas_state, parcel_record, condensed_shares, surface_steam_factor, fine_cell, block_counts):
     fields = gas_state.shape[0]
     planes = gas_state.shape[1]
     cross_cells = gas_state.shape[2]
-    slab_count = lax.axis_size("slab")
-    cross_count = lax.axis_size("cross")
     padded_gas = with_halo(gas_state, (("slab", 1),), 1)
     gas_flat = padded_gas.reshape(fields, (planes + 2) * cross_cells)
     ambient_layer_fields = jnp.take(gas_flat, fine_cell, axis=1)
@@ -123,17 +344,13 @@
         .add(source_terms)
     )
     extended = extended.reshape(fields, planes + 2, cross_cells)
-    from_above = shifted(extended[:, 0], "slab", -1)
-    from_below = shifted(extended[:, planes + 1], "slab", 1)
-    fine_source = extended[:, 1 : planes + 1]
-    fine_source = fine_source.at[:, planes - 1].add(from_above)
-    fine_source = fine_source.at[:, 0].add(from_below)
-    fold = cross_cells * cross_count // (COARSE * COARSE)
-    mass = 0.25 * fine_source[4:].sum(axis=(0, 1))
-    piece = mass.reshape(cross_cells // fold, fold).sum(axis=1)
-    pieces = lax.all_gather(piece, ("slab", "cross"))
-    coarse_source = pieces.reshape(COARSE, slab_count // COARSE, COARSE * COARSE).sum(axis=1)
-    correction = relax(coarse_source)
+    mass = 0.25 * extended[4:].sum(axis=0).reshape(planes + 2, ROWS, LANES, 2).sum(axis=3)
+    even = lax.axis_index("slab") % 2 == 0
+    own = mass[1 : planes + 1].sum(axis=0) + jnp.where(even, mass[planes + 1], mass[0])
+    outer = jnp.where(even, mass[0], mass[planes + 1])
+    edges = jnp.stack([extended[:, 0], extended[:, planes + 1]])
+    halo, grid = spread(own, outer, edges)
+    fine_source, correction = finish(extended[:, 1 : planes + 1], halo, grid)
     return (parcel_next, fine_source, correction)
 
 

time: 893 us -> 142 us (0.16)
  waiting for transfers between devices: 780 us -> 0.01 us
  Pallas kernels: 0 us -> 48.7 us
  between operations: 14.3 us -> 0.87 us
    all_gather x1 -> x0, waiting for transfers between devices: 777 us -> none  [body(): pieces = lax.all_gather(piece, ('slab', 'cross'))]
    pallas_call x0 -> x2, Pallas kernels: none -> 48.7 us  [the longest x1 42.8 us: spread(): pl.pallas_call(spread_kernel, out_shape=(jax.ShapeDtypeStruct(edges.shape...]
    reduce_sum x3, other arithmetic: 3.66 us -> 12.7 us  [the longest x2 12.7 us: body(): extended[4:].sum(axis=0).reshape(planes + 2, ROWS, LANES, 2).sum(axis=3)]
  transfers between devices with their start and end apart: 5 -> 2, of which waited for: 3 -> 0; matrix products, arithmetic and copies ran while one was open for 2% -> 2% of each run, Pallas kernels for 0% -> 0%
where the time goes in v2:
time: 142 us
  Pallas kernels  48.7 us (34%)
  other arithmetic  45.8 us (32%)
  local copies, waits for them, and re-layouts  40.1 us (28%)
  starting transfers between devices  6.29 us (4%)
    pallas_call x1, Pallas kernels, spread(): pl.pallas_call(spread_kernel, out_shape=(jax.ShapeDtypeStruct(edges.shape...  42.8 us
    scatter-add x1, other arithmetic, body(): extended = jnp.zeros((fields, (planes + 2) * cross_cells), jnp.float32).a...  27 us
    gather x2, local copies, waits for them, and re-layouts, body(): ambient_layer_fields = jnp.take(gas_flat, fine_cell, axis=1)  15.4 us
    reduce_sum x2, other arithmetic, body(): extended[4:].sum(axis=0).reshape(planes + 2, ROWS, LANES, 2).sum(axis=3)  12.7 us
    reshape x1, local copies, waits for them, and re-layouts, body(): extended[4:].sum(axis=0).reshape(planes + 2, ROWS, LANES, 2).sum(axis=3)  6.82 us
    unnamed x13, local copies, waits for them, and re-layouts  5.97 us
    pallas_call x1, Pallas kernels, finish(): pl.pallas_call(finish_kernel, out_shape=(jax.ShapeDtypeStruct(base.shape,...  5.83 us
    concatenate x1, local copies, waits for them, and re-layouts, with_halo(): shard = jnp.concatenate([before, shard, after], axis=dim)  5.42 us
  transfers between devices with their start and end apart: 2, of which 0 were waited for; matrix products, arithmetic and copies ran while one was open for 2% of the time, Pallas kernels for 0%

profile of v2, /device:TPU:1, one launch (start us, length us, event | category | flops | bytes accessed | tf_op | source)
XLA Modules:
  0.0 141.7 jit_solution(15590176715075144395)
XLA Ops:
  0.6 1.8 %fusion.11 = (f32[16,1,2048]{2,1,0:T(1,128)S(1)}, f32[16,1,2048]{2,1,0:T(1,128)S(1)}) fusion(f32[16,8,2048]{2,1,0:T(8,128)} %param.6), kind=kLoop, calls=%fused_computation.40 | loop fusion | bytes 524288 | tf_op jit(solution)/shard_map/slice | solution.py:25
  2.5 1.3 collective-permute-start.1
  3.8 5.0 %collective-permute-start = (f32[16,1,2048]{2,0,1:T(8,128)S(1)}, f32[16,1,2048]{2,0,1:T(8,128)S(1)}, u32[]{:S(2)}, u32[]{:S(2)}) collective-permute-start(f32[16,1,2048]{2,0,1:T(8,128)S(1)} %copy.76), channel_id=1, source_target_pairs={{0,4},{4,8},{8,12},{12,16},{16,20},{20,24},{24,28},{28,32},{32,36}... | collective-permute-start | bytes 393224 | tf_op jit(solution)/shard_map/ppermute | solution.py:27
  8.8 0.7 compare_select_fusion
  9.5 0.7 compare_and_fusion
  10.3 0.7 select_bitcast_fusion.1
  11.0 0.7 fusion.6
  11.7 0.0 collective-permute-done.1
  11.7 0.1 copy.67
  11.9 0.0 collective-permute-done
  11.9 0.1 copy.66
  12.0 1.6 %pad_maximum_fusion = f32[16,10,2048]{2,1,0:T(8,128)S(1)} fusion(f32[16,1,2048]{2,1,0:T(1,128)S(1)} %copy.67, f32[16,8,2048]{2,1,0:T(8,128)} %param.6, f32[16,1,2048]{2,1,0:T(1,128)S(1)} %copy.66), kind=kLoop, calls=%fused_computation.5 | loop fusion | flops 655360 | bytes 2621440 | tf_op jit(solution)/shard_map/concatenate | solution.py:29
  13.6 5.4 %copy.68 = f32[16,10,2048]{0,2,1:T(8,128)} copy(f32[16,10,2048]{2,1,0:T(8,128)S(1)} %pad_maximum_fusion) | data formatting | bytes 2621440 | tf_op jit(solution)/shard_map/concatenate | solution.py:29
  19.0 0.0 copy-start.1
  19.0 0.0 copy-start.2
  19.1 0.0 copy-start.3
  19.1 14.8 %gather_fusion = f32[4096,16]{1,0:T(8,128)S(1)} fusion(f32[16,20480]{0,1:T(8,128)} %bitcast.27, s32[4096]{0:T(1024)S(1)} %get-tuple-element.35), kind=kCustom, calls=%fused_computation | custom fusion | bytes 540672 | tf_op jit(solution)/shard_map/jit(_take)/gather | solution.py:335
  33.9 0.6 copy.69
  34.5 0.0 copy-done.1
  34.5 0.1 multiply_reduce_fusion
  34.6 0.2 broadcast_add_fusion
  34.8 0.0 copy-done.2
  34.8 0.0 copy-done.3
  34.8 0.2 fusion.8
  34.9 0.2 multiply_subtract_fusion
  35.1 0.1 multiply_add_fusion
  35.2 0.1 fusion.3
  35.3 0.6 copy.70
  35.9 27.0 %scatter_custom_fusion = f32[16,20480]{0,1:T(8,128)} fusion(s32[4096]{0:T(1024)S(1)} %get-tuple-element.34, f32[4096,16]{1,0:T(8,128)S(1)} %copy.70, f32[]{:T(128)} %constant.17.clone.1), kind=kCustom, calls=%fused_computation.3 | custom fusion | flops 65536 | bytes 1310724 | tf_op jit(solution)/shard_map/scatter-add | solution.py:344
  62.9 0.0 copy-start
  62.9 8.8 %slice_reduce_fusion = f32[20480]{0:T(1024)S(1)} fusion(f32[16,20480]{0,1:T(8,128)} %scatter_custom_fusion), kind=kLoop, calls=%fused_computation.2 | loop fusion | flops 225280 | bytes 1064960 | tf_op jit(solution)/shard_map/reduce_sum | solution.py:347
  71.7 0.0 copy-done
  71.7 3.8 %slice.68 = f32[16,8,2048]{0,2,1:T(8,128)} slice(f32[16,10,2048]{0,2,1:T(8,128)S(1)} %bitcast.25), slice={[0:16], [1:9], [0:2048]} | slice | bytes 2097152 | tf_op jit(solution)/shard_map/slice | solution.py:353
  75.4 0.1 fusion.10
  75.6 0.1 divide_add_fusion
  75.6 5.3 %copy.78.base_ref = f32[16,8,2048]{2,1,0:T(8,128)S(1)} copy(f32[16,8,2048]{0,2,1:T(8,128)} %slice.68) | data formatting | bytes 2097152
  80.9 6.8 %reshape.104 = f32[10,8,128,2]{3,2,1,0:T(8,128)} reshape(f32[20480]{0:T(1024)S(1)} %slice_reduce_fusion) | data formatting | bytes 163840 | tf_op jit(solution)/shard_map/reshape | solution.py:347
  87.7 3.9 %reduce_sum.51 = f32[10,8,128]{2,1,0:T(8,128)S(1)} reduce(f32[10,8,128,2]{3,2,1,0:T(8,128)} %reshape.104, f32[]{:T(128)} %constant.17.clone.1), dimensions={3}, to_apply=%region_4.5 | reduce | flops 10240 | bytes 122884 | tf_op jit(solution)/shard_map/reduce_sum | solution.py:347
  91.7 0.3 copy.80
  92.0 0.3 copy.79
  92.3 42.8 %spread.1 = (f32[2,16,2048]{2,1,0:T(8,128)S(1)}, f32[2,4,4,8,8,128]{5,4,3,2,1,0:T(8,128)S(1)}) custom-call(f32[8,128]{1,0:T(8,128)S(1)} %bitcast_add_fusion.own_ref, f32[8,128]{1,0:T(8,128)S(1)} %select_bitcast_fusion.2.outer_ref, f32[2,16,2048]{2,1,0:T(8,128)S(1)} %pad_maximum_fusion.1.edge_ref), custom_call_target="tpu_custom_call" | custom-call | tf_op jit(solution)/shard_map/spread/pallas_call | solution.py:216
  135.2 5.8 %finish.1 = (f32[16,8,2048]{2,1,0:T(8,128)}, f32[64,4096]{1,0:T(8,128)}) custom-call(f32[16,8,2048]{2,1,0:T(8,128)S(1)} %copy.78.base_ref, f32[2,16,2048]{2,1,0:T(8,128)S(1)} %get-tuple-element.7.halo_ref, f32[2048,128]{1,0:T(8,128)S(1)} %bitcast.24), custom_call_target="tpu_custom_call" | custom-call | tf_op jit(solution)/shard_map/finish/pallas_call | solution.py:311
  141.0 0.7 maximum_select_fusion
  (9 shorter events, 0.2 us)
Async XLA Ops:
  2.5 9.3 %collective-permute-start.1 = (f32[16,1,2048]{2,0,1:T(8,128)S(1)}, f32[16,1,2048]{2,0,1:T(8,128)S(1)}, u32[]{:S(2)}, u32[]{:S(2)}) collective-permute-start(f32[16,1,2048]{2,0,1:T(8,128)S(1)} %copy.77), channel_id=1, source_target_pairs={{4,0},{8,4},{12,8},{16,12},{20,16},{24,20},{28,24},{32,28},{36,32}... | collective-permute-start | bytes 393224 | tf_op jit(solution)/shard_map/ppermute | solution.py:28
  3.8 8.1 %collective-permute-start = (f32[16,1,2048]{2,0,1:T(8,128)S(1)}, f32[16,1,2048]{2,0,1:T(8,128)S(1)}, u32[]{:S(2)}, u32[]{:S(2)}) collective-permute-start(f32[16,1,2048]{2,0,1:T(8,128)S(1)} %copy.76), channel_id=1, source_target_pairs={{0,4},{4,8},{8,12},{12,16},{16,20},{20,24},{24,28},{28,32},{32,36}... | collective-permute-start | bytes 393224 | tf_op jit(solution)/shard_map/ppermute | solution.py:27
  19.0 15.4 %copy-start.1 = (f32[5,4096]{1,0:T(8,128)S(1)}, f32[5,4096]{1,0:T(8,128)}, u32[]{:S(2)}) copy-start(f32[5,4096]{1,0:T(8,128)} %param.7) | copy-start | bytes 245764
  19.0 15.7 %copy-start.2 = (f32[12,4096]{1,0:T(8,128)S(1)}, f32[12,4096]{1,0:T(8,128)}, u32[]{:S(2)}) copy-start(f32[12,4096]{1,0:T(8,128)} %param.8) | copy-start | bytes 589828
  19.1 15.7 %copy-start.3 = (f32[12]{0:T(128)S(1)}, f32[12]{0:T(128)}, u32[]{:S(2)}) copy-start(f32[12]{0:T(128)} %param.9) | copy-start | bytes 148
  62.9 8.8 %copy-start = (f32[16,20480]{0,1:T(8,128)S(1)}, f32[16,20480]{0,1:T(8,128)}, u32[]{:S(2)}) copy-start(f32[16,20480]{0,1:T(8,128)} %scatter_custom_fusion) | copy-start | bytes 3932164

commit v3 on v2

--- a/solution.py
+++ b/solution.py
@@ -15,67 +15,6 @@
 latent_boiling_energy = 0.5
 vapour_heat = 1.5
 volume_inverse = 4.0
-
-
-def with_halo(shard, sides, width):
-    for axis, dim in sides:
-        devices, length = (lax.axis_size(axis), shard.shape[dim])
-        up = [(i, (i + 1) % devices) for i in range(devices - 1)]
-        down = [(j, i) for i, j in up]
-        last = lax.slice_in_dim(shard, length - width, length, axis=dim)
-        leading = lax.slice_in_dim(shard, 0, width, axis=dim)
-        before = lax.ppermute(last, axis, up)
-        after = lax.ppermute(leading, axis, down)
-        shard = jnp.concatenate([before, shard, after], axis=dim)
-    return shard
-
-
-def advance(
-    ambient_layer_fields, parcel_record, condensed_shares, surface_steam_factor, alive_mask
-):
-    gas_velocity = ambient_layer_fields[0:3]
-    ambient_thermal_level = ambient_layer_fields[3]
-    gas_vapour = ambient_layer_fields[4:]
-    parcel_velocity = parcel_record[0:3]
-    parcel_thermal_level = parcel_record[3]
-    parcel_weight_amount = parcel_record[4]
-    slip_velocity = gas_velocity - parcel_velocity
-    slip_squared = jnp.sum(slip_velocity * slip_velocity, axis=0)
-    drag_factor = (
-        drag_rate
-        * jnp.power(parcel_weight_amount, -2.0 / 3.0)
-        * (1.0 + 0.15 * jnp.power(slip_squared + 1.0, 0.3435))
-    )
-    following_motion = (parcel_velocity + drag_factor * gas_velocity) / (1.0 + drag_factor)
-    surface_steam_share = (
-        condensed_shares
-        * surface_steam_factor[:, None]
-        * jnp.exp(2.0 * (parcel_thermal_level - 0.75))
-    )
-    species_rates = evap_rate * parcel_weight_amount * (surface_steam_share - gas_vapour)
-    evaporated_weight = jnp.sum(species_rates, axis=0)
-    thermal_exchange = (
-        warming_speed
-        * (ambient_thermal_level - parcel_thermal_level)
-        * jnp.power(parcel_weight_amount, 1.0 / 3.0)
-    )
-    following_thermal_level = (
-        parcel_thermal_level
-        + (thermal_exchange - latent_boiling_energy * evaporated_weight) / parcel_weight_amount
-    )
-    following_weight = parcel_weight_amount - evaporated_weight
-    momentum_terms = (
-        parcel_weight_amount * (parcel_velocity - following_motion)
-        + evaporated_weight * following_motion
-    )
-    energy_terms = vapour_heat * evaporated_weight - thermal_exchange
-    source_terms = jnp.concatenate([momentum_terms, energy_terms[None], species_rates], axis=0)
-    source_terms = source_terms * (alive_mask * volume_inverse)
-    updated_parcel_record = jnp.concatenate(
-        [following_motion, following_thermal_level[None], following_weight[None]], axis=0
-    )
-    parcel_next = jnp.where(alive_mask[None] > 0.5, updated_parcel_record, parcel_record)
-    return (source_terms, parcel_next, evaporated_weight * alive_mask)
 
 
 LINE = 16
@@ -326,31 +265,209 @@
     )(base, halo, grid.reshape(-1, LANES))
 
 
+CHUNK = 512
+PER_PLANE = 4
+UNROLL = 4
+
+
+def parts_of(value):
+    high = value.astype(jnp.bfloat16)
+    rest = value - high.astype(jnp.float32)
+    middle = rest.astype(jnp.bfloat16)
+    low = (rest - middle.astype(jnp.float32)).astype(jnp.bfloat16)
+    return jnp.concatenate([high, middle, low], axis=0)
+
+
+def joined(value):
+    third = value.shape[0] // 3
+    return value[:third] + (value[third : 2 * third] + value[2 * third :])
+
+
+def spray_kernel(
+    cell_at, count_at, gas_ref, low_ref, high_ref, record_ref, shares_ref, steam_ref, cell_ref,
+    next_ref, base_ref, edge_ref, own_ref, outer_ref,
+    gas_parts, gathered, terms, total, block_of, chunk_of, base_of,
+):
+    fields, planes, cells = gas_ref.shape
+    blocks = cell_ref.shape[0]
+    chunks = (planes + 2) * PER_PLANE
+
+    def listed(b, i):
+        first = lax.shift_right_logical(cell_at[b * BLOCK], 9)
+        last = lax.shift_right_logical(cell_at[b * BLOCK + BLOCK - 1], 9)
+
+        def one(j, i):
+            block_of[i] = b
+            chunk_of[i] = j
+            base_of[i] = j * CHUNK
+            return i + 1
+
+        return lax.fori_loop(first, last + 1, one, i)
+
+    pairs = lax.fori_loop(0, blocks, listed, 0)
+    for k in range(UNROLL):
+        block_of[pairs + k] = 0
+        chunk_of[pairs + k] = 0
+        base_of[pairs + k] = chunks * CHUNK
+    rounds = lax.div(pairs + UNROLL - 1, UNROLL)
+
+    for p in range(planes + 2):
+        for q in range(PER_PLANE):
+            cols = slice(q * CHUNK, (q + 1) * CHUNK)
+            if p == 0:
+                value = low_ref[:, cols]
+            elif p == planes + 1:
+                value = high_ref[:, cols]
+            else:
+                value = gas_ref[:, p - 1, cols]
+            gas_parts[p * PER_PLANE + q] = parts_of(value)
+    gathered[...] = jnp.zeros(gathered.shape, jnp.float32)
+    total[...] = jnp.zeros(total.shape, jnp.float32)
+    row = lax.broadcasted_iota(jnp.int32, (CHUNK, BLOCK), 0)
+
+    def picked(i):
+        place = cell_ref[pl.ds(block_of[i], 1), :] - base_of[i]
+        return jnp.where(row == place, 1.0, 0.0).astype(jnp.bfloat16)
+
+    def gather(n, carry):
+        for k in range(UNROLL):
+            i = n * UNROLL + k
+            part = jnp.dot(gas_parts[chunk_of[i]], picked(i), preferred_element_type=jnp.float32)
+            gathered[block_of[i]] += joined(part)
+        return carry
+
+    lax.fori_loop(0, rounds, gather, 0)
+
+    lane = lax.broadcasted_iota(jnp.int32, (1, BLOCK), 1)
+    steam = steam_ref[...]
+
+    def step(n, carry):
+        for k in range(UNROLL):
+            b = n * UNROLL + k
+            cols = pl.ds(pl.multiple_of(b * BLOCK, BLOCK), BLOCK)
+            gas = gathered[b]
+            record = record_ref[:, cols]
+            alive = lane < count_at[b]
+            gas_velocity, gas_heat, vapour = gas[0:3], gas[3:4], gas[4:]
+            velocity, heat, weight = record[0:3], record[3:4], record[4:5]
+            slip = gas_velocity - velocity
+            slip = slip * slip
+            slip = slip[0:1] + slip[1:2] + slip[2:3]
+            log_weight = jnp.log(weight)
+            factor = drag_rate * jnp.exp(log_weight * (-2.0 / 3.0))
+            factor = factor * (1.0 + 0.15 * jnp.exp(0.3435 * jnp.log(slip + 1.0)))
+            moved = (velocity + factor * gas_velocity) / (1.0 + factor)
+            surface = shares_ref[:, cols] * steam * jnp.exp(2.0 * (heat - 0.75))
+            rates = evap_rate * weight * (surface - vapour)
+            lost = jnp.sum(rates, axis=0, keepdims=True)
+            exchange = warming_speed * (gas_heat - heat) * jnp.exp(log_weight * (1.0 / 3.0))
+            warmed = heat + (exchange - latent_boiling_energy * lost) / weight
+            scale = jnp.where(alive, volume_inverse, 0.0)
+            terms[b, 0:3] = (weight * (velocity - moved) + lost * moved) * scale
+            terms[b, 3:4] = (vapour_heat * lost - exchange) * scale
+            terms[b, 4:16] = rates * scale
+            next_ref[0:3, cols] = jnp.where(alive, moved, velocity)
+            next_ref[3:4, cols] = jnp.where(alive, warmed, heat)
+            next_ref[4:5, cols] = jnp.where(alive, weight - lost, weight)
+        return carry
+
+    lax.fori_loop(0, blocks // UNROLL, step, 0)
+
+    def scatter(n, carry):
+        for k in range(UNROLL):
+            i = n * UNROLL + k
+            part = lax.dot_general(
+                parts_of(terms[block_of[i]]), picked(i), (((1,), (1,)), ((), ())),
+                preferred_element_type=jnp.float32,
+            )
+            total[chunk_of[i]] += joined(part)
+        return carry
+
+    lax.fori_loop(0, rounds, scatter, 0)
+
+    half = CHUNK // 2
+    fold_row = lax.broadcasted_iota(jnp.int32, (half, LANES), 0)
+    fold_lane = lax.broadcasted_iota(jnp.int32, (half, LANES), 1)
+    fold = jnp.where(lax.shift_right_logical(fold_row, 1) == fold_lane, 1.0, 0.0).astype(jnp.bfloat16)
+
+    def mass(value):
+        kept = jnp.sum(value[4:], axis=0, keepdims=True)
+        rows = [
+            joined(jnp.dot(parts_of(kept[:, h * half : (h + 1) * half]), fold, preferred_element_type=jnp.float32))
+            for h in range(2)
+        ]
+        return rows
+
+    own, low, high = [], [], []
+    for q in range(PER_PLANE):
+        cols = slice(q * CHUNK, (q + 1) * CHUNK)
+        below = total[q]
+        above = total[(planes + 1) * PER_PLANE + q]
+        edge_ref[0, :, cols] = below
+        edge_ref[1, :, cols] = above
+        inside = None
+        for p in range(planes):
+            value = total[(p + 1) * PER_PLANE + q]
+            base_ref[:, p, cols] = value
+            inside = value if inside is None else inside + value
+        own += mass(inside)
+        low += mass(below)
+        high += mass(above)
+    own, low, high = (0.25 * jnp.concatenate(rows, axis=0) for rows in (own, low, high))
+    odd = lax.rem(lax.axis_index("slab"), 2) == 1
+    own_ref[...] = own + jnp.where(odd, low, high)
+    outer_ref[...] = jnp.where(odd, high, low)
+
+
+def spray(gas_state, low, high, parcel_record, condensed_shares, surface_steam_factor, fine_cell, block_counts):
+    fields, planes, cells = gas_state.shape
+    blocks = block_counts.shape[0]
+    chunks = (planes + 2) * PER_PLANE
+    room = chunks + blocks + UNROLL
+    vmem = pl.BlockSpec(memory_space=pltpu.VMEM)
+    smem = pl.BlockSpec(memory_space=pltpu.SMEM)
+    array = lambda *shape: jax.ShapeDtypeStruct(shape, jnp.float32)
+    return pl.pallas_call(
+        spray_kernel,
+        out_shape=(
+            array(*parcel_record.shape), array(*gas_state.shape), array(2, fields, cells),
+            array(ROWS, LANES), array(ROWS, LANES),
+        ),
+        in_specs=[smem, smem] + [vmem] * 7,
+        out_specs=(vmem,) * 5,
+        scratch_shapes=[
+            pltpu.VMEM((chunks, 3 * fields, CHUNK), jnp.bfloat16),
+            pltpu.VMEM((blocks, fields, BLOCK), jnp.float32),
+            pltpu.VMEM((blocks, fields, BLOCK), jnp.float32),
+            pltpu.VMEM((chunks, fields, CHUNK), jnp.float32),
+            pltpu.SMEM((room,), jnp.int32),
+            pltpu.SMEM((room,), jnp.int32),
+            pltpu.SMEM((room,), jnp.int32),
+        ],
+        compiler_params=pltpu.CompilerParams(vmem_limit_bytes=32 << 20),
+        name="spray",
+    )(
+        fine_cell, block_counts, gas_state, low, high, parcel_record, condensed_shares,
+        surface_steam_factor.reshape(-1, 1), fine_cell.reshape(blocks, BLOCK),
+    )
+
+
+def exchanged(shard):
+    devices = lax.axis_size("slab")
+    up = [(i, (i + 1) % devices) for i in range(devices)]
+    down = [(j, i) for i, j in up]
+    before = lax.ppermute(shard[:, -1], "slab", up)
+    after = lax.ppermute(shard[:, 0], "slab", down)
+    return before, after
+
+
 def body(gas_state, parcel_record, condensed_shares, surface_steam_factor, fine_cell, block_counts):
-    fields = gas_state.shape[0]
-    planes = gas_state.shape[1]
-    cross_cells = gas_state.shape[2]
-    padded_gas = with_halo(gas_state, (("slab", 1),), 1)
-    gas_flat = padded_gas.reshape(fields, (planes + 2) * cross_cells)
-    ambient_layer_fields = jnp.take(gas_flat, fine_cell, axis=1)
-    slot_in_block = jnp.arange(BLOCK, dtype=jnp.int32)
-    alive_mask = (slot_in_block[None, :] < block_counts[:, None]).reshape(-1).astype(jnp.float32)
-    source_terms, parcel_next, evaporated_weight = advance(
-        ambient_layer_fields, parcel_record, condensed_shares, surface_steam_factor, alive_mask
+    low, high = exchanged(gas_state)
+    parcel_next, base, edges, own, outer = spray(
+        gas_state, low, high, parcel_record, condensed_shares, surface_steam_factor, fine_cell, block_counts
     )
-    extended = (
-        jnp.zeros((fields, (planes + 2) * cross_cells), jnp.float32)
-        .at[:, fine_cell]
-        .add(source_terms)
-    )
-    extended = extended.reshape(fields, planes + 2, cross_cells)
-    mass = 0.25 * extended[4:].sum(axis=0).reshape(planes + 2, ROWS, LANES, 2).sum(axis=3)
-    even = lax.axis_index("slab") % 2 == 0
-    own = mass[1 : planes + 1].sum(axis=0) + jnp.where(even, mass[planes + 1], mass[0])
-    outer = jnp.where(even, mass[0], mass[planes + 1])
-    edges = jnp.stack([extended[:, 0], extended[:, planes + 1]])
     halo, grid = spread(own, outer, edges)
-    fine_source, correction = finish(extended[:, 1 : planes + 1], halo, grid)
+    fine_source, correction = finish(base, halo, grid)
     return (parcel_next, fine_source, correction)
 
 

time: 142 us -> 80.8 us (0.57)
  other arithmetic: 45.8 us -> 0 us
  local copies, waits for them, and re-layouts: 40.1 us -> 3.98 us
  starting transfers between devices: 6.29 us -> 17.1 us
  Pallas kernels: 48.7 us -> 56.8 us
  waiting for transfers between devices: 0.01 us -> 2.05 us
    scatter-add x1 -> x0, other arithmetic: 27 us -> none  [body(): extended = jnp.zeros((fields, (planes + 2) * cross_cells), jnp.float32).a...]
    pallas_call x0 -> x1, Pallas kernels: none -> 17.6 us  [spray(): pl.pallas_call(spray_kernel, out_shape=(array(*parcel_record.shape), arra...]
    gather x2 -> x0, local copies, waits for them, and re-layouts: 15.4 us -> none  [body(): ambient_layer_fields = jnp.take(gas_flat, fine_cell, axis=1)]
    reduce_sum x5 -> x0, other arithmetic: 12.9 us -> none  [the longest x2 12.7 us: body(): extended[4:].sum(axis=0).reshape(planes + 2, ROWS, LANES, 2).sum(axis=3)]
    ppermute x2, starting transfers between devices: 6.29 us -> 17.1 us  [the longest x1 12.7 us: exchanged(): after = lax.ppermute(shard[:, 0], 'slab', down)]
    pallas_call x1, Pallas kernels: 42.8 us -> 33.3 us  [spread(): pl.pallas_call(spread_kernel, out_shape=(jax.ShapeDtypeStruct(edges.shape...]
    reshape x1, local copies, waits for them, and re-layouts: 6.82 us -> 0.1 us  [spray(): surface_steam_factor.reshape(-1, 1)]
    concatenate x1 -> x0, local copies, waits for them, and re-layouts: 5.42 us -> none  [with_halo(): shard = jnp.concatenate([before, shard, after], axis=dim)]
  transfers between devices with their start and end apart: 2 -> 2, of which waited for: 0 -> 2; matrix products, arithmetic and copies ran while one was open for 2% -> 0% of each run, Pallas kernels for 0% -> 0%
where the time goes in v3:
time: 80.8 us; the launch traced here: 80.6 us
  Pallas kernels  56.8 us (70%)
  starting transfers between devices  17.1 us (21%)
  local copies, waits for them, and re-layouts  3.98 us (5%)
  waiting for transfers between devices  2.05 us (3%)
    pallas_call x1, Pallas kernels, spread(): pl.pallas_call(spread_kernel, out_shape=(jax.ShapeDtypeStruct(edges.shape...  33.3 us
    pallas_call x1, Pallas kernels, spray(): pl.pallas_call(spray_kernel, out_shape=(array(*parcel_record.shape), arra...  17.6 us
    ppermute x1, starting transfers between devices, exchanged(): after = lax.ppermute(shard[:, 0], 'slab', down)  12.7 us
    pallas_call x1, Pallas kernels, finish(): pl.pallas_call(finish_kernel, out_shape=(jax.ShapeDtypeStruct(base.shape,...  5.83 us
    ppermute x1, starting transfers between devices, exchanged(): before = lax.ppermute(shard[:, -1], 'slab', up)  4.36 us
    unnamed x14, local copies, waits for them, and re-layouts  1.96 us
    slice x1, local copies, waits for them, and re-layouts, exchanged(): after = lax.ppermute(shard[:, 0], 'slab', down)  1.93 us
  transfers between devices with their start and end apart: 2, of which 2 were waited for; matrix products, arithmetic and copies ran while one was open for 0% of the time, Pallas kernels for 0%

profile of v3, /device:TPU:1, one launch (start us, length us, event | category | flops | bytes accessed | tf_op | source)
XLA Modules:
  0.0 80.6 jit_solution(14506332040317434012)
XLA Ops:
  0.6 0.0 copy-start
  0.6 1.9 %fusion = (f32[16,1,2048]{2,1,0:T(1,128)S(1)}, f32[16,1,2048]{2,1,0:T(1,128)S(1)}) fusion(f32[16,8,2048]{2,1,0:T(8,128)} %gas_ref.1), kind=kLoop, calls=%fused_computation.2 | loop fusion | bytes 524288 | tf_op jit(solution)/shard_map/slice | solution.py:460
  2.6 0.0 copy-start.5
  2.6 4.4 %collective-permute-start = (f32[16,2048]{1,0:T(8,128)S(1)}, f32[16,2048]{1,0:T(8,128)S(1)}, u32[]{:S(2)}, u32[]{:S(2)}) collective-permute-start(f32[16,2048]{1,0:T(8,128)S(1)} %bitcast.11), channel_id=1, source_target_pairs={{0,4},{4,8},{8,12},{12,16},{16,20},{20,24},{24,28},{28,32},{32,36}... | collective-permute-start | bytes 393224 | tf_op jit(solution)/shard_map/ppermute | solution.py:459
  7.0 0.0 copy-start.3
  7.1 12.7 %collective-permute-start.1 = (f32[16,2048]{1,0:T(8,128)S(1)}, f32[16,2048]{1,0:T(8,128)S(1)}, u32[]{:S(2)}, u32[]{:S(2)}) collective-permute-start(f32[16,2048]{1,0:T(8,128)S(1)} %bitcast.12), channel_id=1, source_target_pairs={{4,0},{8,4},{12,8},{16,12},{20,16},{24,20},{28,24},{32,28},{36,32}... | collective-permute-start | bytes 393224 | tf_op jit(solution)/shard_map/ppermute | solution.py:460
  19.8 0.0 copy-done.5
  19.8 0.1 copy.11.steam_ref
  19.9 0.0 copy-start.4
  19.9 1.1 %collective-permute-done.low_ref = f32[16,2048]{1,0:T(8,128)S(1)} collective-permute-done((f32[16,2048]{1,0:T(8,128)S(1)}, f32[16,2048]{1,0:T(8,128)S(1)}, u32[]{:S(2)}, u32[]{:S(2)}) %collective-permute-start) | collective-permute-done | bytes 131104 | tf_op jit(solution)/shard_map/ppermute | solution.py:459
  21.0 1.0 %collective-permute-done.1.high_ref = f32[16,2048]{1,0:T(8,128)S(1)} collective-permute-done((f32[16,2048]{1,0:T(8,128)S(1)}, f32[16,2048]{1,0:T(8,128)S(1)}, u32[]{:S(2)}, u32[]{:S(2)}) %collective-permute-start.1) | collective-permute-done | bytes 131104 | tf_op jit(solution)/shard_map/ppermute | solution.py:460
  21.9 0.0 copy-done
  21.9 0.0 copy-done.3
  21.9 0.0 copy-done.4
  21.9 0.0 copy-start.1
  22.0 0.9 %copy-done.1 = f32[12,4096]{1,0:T(8,128)S(1)} copy-done((f32[12,4096]{1,0:T(8,128)S(1)}, f32[12,4096]{1,0:T(8,128)}, u32[]{:S(2)}) %copy-start.1) | copy-done | bytes 196632
  22.9 0.0 copy-start.2
  22.9 0.9 %copy-done.2 = f32[5,4096]{1,0:T(8,128)S(1)} copy-done((f32[5,4096]{1,0:T(8,128)S(1)}, f32[5,4096]{1,0:T(8,128)}, u32[]{:S(2)}) %copy-start.2) | copy-done | bytes 81944
  23.8 17.6 %spray.1 = (f32[5,4096]{1,0:T(8,128)}, f32[16,8,2048]{2,1,0:T(8,128)S(1)}, f32[2,16,2048]{2,1,0:T(8,128)S(1)}, f32[8,128]{1,0:T(8,128)S(1)}, f32[8,128]{1,0:T(8,128)S(1)}) custom-call(s32[4096]{0:T(1024)S(1)} %copy-done.3, s32[32]{0:T(128)S(1)} %copy-done.4, f32[16,8,2048]{2,1,0:T(8,128)S(1)} %copy-done, f32[16,2048]{1,0:T(8,128)S(1)} %collective-permute-done.low_ref, ...), custom_call_target="tpu_custom_call" | custom-call | tf_op jit(solution)/shard_map/spray/pallas_call | solution.py:430
  41.4 33.3 %spread.1 = (f32[2,16,2048]{2,1,0:T(8,128)S(1)}, f32[2,4,4,8,8,128]{5,4,3,2,1,0:T(8,128)S(1)}) custom-call(f32[8,128]{1,0:T(8,128)S(1)} %get-tuple-element.14.own_ref, f32[8,128]{1,0:T(8,128)S(1)} %get-tuple-element.15.outer_ref, f32[2,16,2048]{2,1,0:T(8,128)S(1)} %get-tuple-element.16.edge_ref), custom_call_target="tpu_custom_call" | custom-call | tf_op jit(solution)/shard_map/spread/pallas_call | solution.py:155
  74.7 5.8 %finish.1 = (f32[16,8,2048]{2,1,0:T(8,128)}, f32[64,4096]{1,0:T(8,128)}) custom-call(f32[16,8,2048]{2,1,0:T(8,128)S(1)} %get-tuple-element.13.base_ref, f32[2,16,2048]{2,1,0:T(8,128)S(1)} %get-tuple-element.17.halo_ref, f32[2048,128]{1,0:T(8,128)S(1)} %bitcast.9), custom_call_target="tpu_custom_call" | custom-call | tf_op jit(solution)/shard_map/finish/pallas_call | solution.py:250
  (2 shorter events, 0.1 us)
Async XLA Ops:
  0.6 21.3 %copy-start = (f32[16,8,2048]{2,1,0:T(8,128)S(1)}, f32[16,8,2048]{2,1,0:T(8,128)}, u32[]{:S(2)}) copy-start(f32[16,8,2048]{2,1,0:T(8,128)} %gas_ref.1) | copy-start | bytes 3145732
  2.6 17.2 %copy-start.5 = (f32[12]{0:T(128)S(1)}, f32[12]{0:T(128)}, u32[]{:S(2)}) copy-start(f32[12]{0:T(128)} %param.9) | copy-start | bytes 148
  2.6 18.3 %collective-permute-start = (f32[16,2048]{1,0:T(8,128)S(1)}, f32[16,2048]{1,0:T(8,128)S(1)}, u32[]{:S(2)}, u32[]{:S(2)}) collective-permute-start(f32[16,2048]{1,0:T(8,128)S(1)} %bitcast.11), channel_id=1, source_target_pairs={{0,4},{4,8},{8,12},{12,16},{16,20},{20,24},{24,28},{28,32},{32,36}... | collective-permute-start | bytes 393224 | tf_op jit(solution)/shard_map/ppermute | solution.py:459
  7.0 14.9 %copy-start.3 = (s32[4096]{0:T(1024)S(1)}, s32[4096]{0:T(1024)}, u32[]{:S(2)}) copy-start(s32[4096]{0:T(1024)} %cell_at.1) | copy-start | bytes 49156
  7.1 14.9 %collective-permute-start.1 = (f32[16,2048]{1,0:T(8,128)S(1)}, f32[16,2048]{1,0:T(8,128)S(1)}, u32[]{:S(2)}, u32[]{:S(2)}) collective-permute-start(f32[16,2048]{1,0:T(8,128)S(1)} %bitcast.12), channel_id=1, source_target_pairs={{4,0},{8,4},{12,8},{16,12},{20,16},{24,20},{28,24},{32,28},{36,32}... | collective-permute-start | bytes 393224 | tf_op jit(solution)/shard_map/ppermute | solution.py:460
  19.9 2.1 %copy-start.4 = (s32[32]{0:T(128)S(1)}, s32[32]{0:T(128)}, u32[]{:S(2)}) copy-start(s32[32]{0:T(128)} %count_at.1) | copy-start | bytes 388
  21.9 1.0 %copy-start.1 = (f32[12,4096]{1,0:T(8,128)S(1)}, f32[12,4096]{1,0:T(8,128)}, u32[]{:S(2)}) copy-start(f32[12,4096]{1,0:T(8,128)} %shares_ref.1) | copy-start | bytes 589828
  22.9 0.9 %copy-start.2 = (f32[5,4096]{1,0:T(8,128)S(1)}, f32[5,4096]{1,0:T(8,128)}, u32[]{:S(2)}) copy-start(f32[5,4096]{1,0:T(8,128)} %record_ref.1) | copy-start | bytes 245764

commit v4 on v2

v4 whole, which is shorter than its diff:
```python
import jax
import jax.numpy as jnp
from jax import lax
from jax.experimental import pallas as pl
from jax.experimental.pallas import tpu as pltpu
from jax.sharding import PartitionSpec as P

BLOCK = 128
COARSE = 64


drag_rate = 0.5
evap_rate = 0.08
warming_speed = 0.3
latent_boiling_energy = 0.5
vapour_heat = 1.5
volume_inverse = 4.0


LINE = 16
RING = 4
LANES = 128
ROWS = 8
FIELDS = 16
PLANES = 8
TILES = 16
CHUNK = 512
PER_PLANE = 4
SHIFT = 9
UNROLL = 4
PAIRS = 72
ROOM = 80


def parts_of(value):
    high = value.astype(jnp.bfloat16)
    rest = value - high.astype(jnp.float32)
    middle = rest.astype(jnp.bfloat16)
    low = (rest - middle.astype(jnp.float32)).astype(jnp.bfloat16)
    return jnp.concatenate([high, middle, low], axis=0)


def joined(value):
    third = value.shape[0] // 3
    return value[:third] + (value[third : 2 * third] + value[2 * third :])


def plane_rows(tile, plane):
    return pl.ds(tile * PLANES + plane, FIELDS, stride=TILES * PLANES)


def send(src, dst, send_sem, recv_sem, device):
    return pltpu.make_async_remote_copy(
        src_ref=src, dst_ref=dst, send_sem=send_sem, recv_sem=recv_sem,
        device_id=device, device_id_type=pl.DeviceIdType.MESH,
    )


def halo_kernel(gas_ref, parts_ref, sent, got, send_sem, recv_sem):
    slabs = 2 * RING * LINE
    slab = lax.axis_index("slab")
    cross = lax.axis_index("cross")
    below = (lax.rem(slab - 1 + slabs, slabs), cross)
    above = (lax.rem(slab + 1, slabs), cross)
    barrier = pltpu.get_barrier_semaphore()
    for device in (below, above):
        pl.semaphore_signal(barrier, inc=1, device_id=device, device_id_type=pl.DeviceIdType.MESH)
    for side, plane in ((0, 0), (1, PLANES - 1)):
        for t in range(TILES):
            sent[side, :, t * LANES : (t + 1) * LANES] = gas_ref[plane_rows(t, plane), :]
    pl.semaphore_wait(barrier, 2)
    copies = [
        send(sent.at[0], got.at[1], send_sem.at[0], recv_sem.at[1], below),
        send(sent.at[1], got.at[0], send_sem.at[1], recv_sem.at[0], above),
    ]
    for each in copies:
        each.start()
    group = CHUNK // LANES
    for p in range(PLANES):
        for q in range(PER_PLANE):
            value = [gas_ref[plane_rows(q * group + t, p), :] for t in range(group)]
            parts_ref[(p + 1) * PER_PLANE + q] = parts_of(jnp.concatenate(value, axis=1))
    for side, plane in ((0, 0), (1, PLANES + 1)):
        send(sent.at[0], got.at[side], send_sem.at[0], recv_sem.at[side], above).wait_recv()
        for q in range(PER_PLANE):
            parts_ref[plane * PER_PLANE + q] = parts_of(got[side, :, q * CHUNK : (q + 1) * CHUNK])
    for each in copies:
        each.wait_send()


def halo(gas_rows):
    vmem = pl.BlockSpec(memory_space=pltpu.VMEM)
    dma = pltpu.SemaphoreType.DMA
    chunks = (PLANES + 2) * PER_PLANE
    return pl.pallas_call(
        halo_kernel,
        out_shape=jax.ShapeDtypeStruct((chunks, 3 * FIELDS, CHUNK), jnp.bfloat16),
        in_specs=[vmem],
        out_specs=vmem,
        scratch_shapes=[
            pltpu.VMEM((2, FIELDS, TILES * LANES), jnp.float32),
            pltpu.VMEM((2, FIELDS, TILES * LANES), jnp.float32),
            dma((2,)), dma((2,)),
        ],
        compiler_params=pltpu.CompilerParams(
            collective_id=1, has_side_effects=True, vmem_limit_bytes=16 << 20
        ),
        name="halo",
    )(gas_rows)


def spray_kernel(
    cell_at, count_at, gas_parts, record_ref, shares_ref, steam_ref, cell_ref, next_ref, terms,
    table, gathered,
):
    blocks = cell_ref.shape[0]
    chunks = (PLANES + 2) * PER_PLANE

    def listed(b, i):
        first = lax.shift_right_logical(cell_at[b * BLOCK], SHIFT)
        last = lax.shift_right_logical(cell_at[b * BLOCK + BLOCK - 1], SHIFT)

        def one(j, i):
            table[i] = b
            table[ROOM + i] = j
            table[2 * ROOM + j] = i
            return i + 1

        return lax.fori_loop(first, last + 1, one, i)

    for c in range(chunks):
        table[2 * ROOM + c] = PAIRS
    pairs = lax.fori_loop(0, blocks, listed, 0)

    def blank(i, carry):
        table[i] = 0
        table[ROOM + i] = -1
        return carry

    lax.fori_loop(pairs, PAIRS, blank, 0)
    rounds = lax.div(pairs + UNROLL - 1, UNROLL)

    gathered[...] = jnp.zeros(gathered.shape, jnp.float32)
    row = lax.broadcasted_iota(jnp.int32, (CHUNK, BLOCK), 0)

    def picked(i):
        c = table[ROOM + i]
        place = cell_ref[pl.ds(table[i], 1), :] - jnp.where(c < 0, chunks, c) * CHUNK
        return jnp.where(row == place, 1.0, 0.0).astype(jnp.bfloat16)

    def gather(n, carry):
        for k in range(UNROLL):
            i = n * UNROLL + k
            held = gas_parts[jnp.maximum(table[ROOM + i], 0)]
            part = jnp.dot(held, picked(i), preferred_element_type=jnp.float32)
            gathered[table[i]] += joined(part)
        return carry

    lax.fori_loop(0, rounds, gather, 0)

    lane = lax.broadcasted_iota(jnp.int32, (1, BLOCK), 1)
    steam = steam_ref[...]

    def step(n, carry):
        for k in range(UNROLL):
            b = n * UNROLL + k
            cols = pl.ds(pl.multiple_of(b * BLOCK, BLOCK), BLOCK)
            gas = gathered[b]
            record = record_ref[:, cols]
            alive = lane < count_at[b]
            gas_velocity, gas_heat, vapour = gas[0:3], gas[3:4], gas[4:]
            velocity, heat, weight = record[0:3], record[3:4], record[4:5]
            slip = gas_velocity - velocity
            slip = slip * slip
            slip = slip[0:1] + slip[1:2] + slip[2:3]
            log_weight = jnp.log(weight)
            factor = drag_rate * jnp.exp(log_weight * (-2.0 / 3.0))
            factor = factor * (1.0 + 0.15 * jnp.exp(0.3435 * jnp.log(slip + 1.0)))
            moved = (velocity + factor * gas_velocity) / (1.0 + factor)
            surface = shares_ref[:, cols] * steam * jnp.exp(2.0 * (heat - 0.75))
            rates = evap_rate * weight * (surface - vapour)
            lost = jnp.sum(rates, axis=0, keepdims=True)
            exchange = warming_speed * (gas_heat - heat) * jnp.exp(log_weight * (1.0 / 3.0))
            warmed = heat + (exchange - latent_boiling_energy * lost) / weight
            scale = jnp.where(alive, volume_inverse, 0.0)
            terms[b, 0:3] = (weight * (velocity - moved) + lost * moved) * scale
            terms[b, 3:4] = (vapour_heat * lost - exchange) * scale
            terms[b, 4:16] = rates * scale
            next_ref[0:3, cols] = jnp.where(alive, moved, velocity)
            next_ref[3:4, cols] = jnp.where(alive, warmed, heat)
            next_ref[4:5, cols] = jnp.where(alive, weight - lost, weight)
        return carry

    lax.fori_loop(0, blocks // UNROLL, step, 0)


def spray(gas_parts, parcel_record, condensed_shares, surface_steam_factor, fine_cell, block_counts):
    blocks = block_counts.shape[0]
    vmem = pl.BlockSpec(memory_space=pltpu.VMEM)
    smem = pl.BlockSpec(memory_space=pltpu.SMEM)
    return pl.pallas_call(
        spray_kernel,
        out_shape=(
            jax.ShapeDtypeStruct(parcel_record.shape, jnp.float32),
            jax.ShapeDtypeStruct((blocks, FIELDS, BLOCK), jnp.float32),
            jax.ShapeDtypeStruct((3 * ROOM,), jnp.int32),
        ),
        in_specs=[smem, smem] + [vmem] * 5,
        out_specs=(vmem, vmem, smem),
        scratch_shapes=[
            pltpu.VMEM((blocks, FIELDS, BLOCK), jnp.float32),
        ],
        compiler_params=pltpu.CompilerParams(vmem_limit_bytes=16 << 20),
        name="spray",
    )(
        fine_cell, block_counts, gas_parts, parcel_record, condensed_shares,
        surface_steam_factor.reshape(-1, 1), fine_cell.reshape(blocks, BLOCK),
    )


def scatter(table, cell_ref, terms_ref, base_ref, edge, slots):
    chunks = (PLANES + 2) * PER_PLANE
    row = lax.broadcasted_iota(jnp.int32, (CHUNK, BLOCK), 0)

    def step(n, carry):
        total, before = carry
        for k in range(UNROLL):
            i = n * UNROLL + k
            b = table[i]
            c = table[ROOM + i]
            place = cell_ref[pl.ds(b, 1), :] - jnp.where(c < 0, chunks, c) * CHUNK
            picked = jnp.where(row == place, 1.0, 0.0).astype(jnp.bfloat16)
            part = lax.dot_general(
                parts_of(terms_ref[b]), picked, (((1,), (1,)), ((), ())),
                preferred_element_type=jnp.float32,
            )
            total = joined(part) + total * jnp.where(c == before, 1.0, 0.0)
            slots[i] = total
            before = c
        return total, before

    none = jnp.zeros((FIELDS, CHUNK), jnp.float32)
    lax.fori_loop(0, PAIRS // UNROLL, step, (none, -2))
    slots[PAIRS] = none

    half = CHUNK // 2
    fold_row = lax.broadcasted_iota(jnp.int32, (half, LANES), 0)
    fold_lane = lax.broadcasted_iota(jnp.int32, (half, LANES), 1)
    fold = jnp.where(lax.shift_right_logical(fold_row, 1) == fold_lane, 1.0, 0.0).astype(jnp.bfloat16)

    def mass(value):
        kept = jnp.sum(value[4:], axis=0, keepdims=True)
        return [
            joined(jnp.dot(parts_of(kept[:, h * half : (h + 1) * half]), fold, preferred_element_type=jnp.float32))
            for h in range(2)
        ]

    own, low, high = [], [], []
    group = CHUNK // LANES
    for q in range(PER_PLANE):
        cols = slice(q * CHUNK, (q + 1) * CHUNK)
        below = slots[table[2 * ROOM + q]]
        above = slots[table[2 * ROOM + (PLANES + 1) * PER_PLANE + q]]
        edge[0, :, cols] = below
        edge[1, :, cols] = above
        inside = None
        for p in range(PLANES):
            value = slots[table[2 * ROOM + (p + 1) * PER_PLANE + q]]
            for t in range(group):
                base_ref[plane_rows(q * group + t, p), :] = value[:, t * LANES : (t + 1) * LANES]
            inside = value if inside is None else inside + value
        own += mass(inside)
        low += mass(below)
        high += mass(above)
    return tuple(0.25 * jnp.concatenate(rows, axis=0) for rows in (own, low, high))


def spread_kernel(
    table, cell_ref, terms_ref, base_ref, halo_ref, grid_ref, own_ref, outer_ref, edge_ref, slots, got,
    pair_send, pair_recv, edge_send, edge_recv, line_send, line_recv,
    minor_send, minor_recv, major_send, major_recv, core_send, core_recv,
):
    slabs = 2 * RING * LINE
    slab = lax.axis_index("slab")
    cross = lax.axis_index("cross")
    core = lax.rem(cross, 2)
    z = lax.rem(slab, LINE)
    x = lax.rem(lax.div(slab, LINE), RING)
    y = lax.div(cross, 2) * 2 + lax.div(slab, RING * LINE)
    odd = lax.rem(slab, 2)
    sign = 2 * odd - 1
    pair = lax.div(slab, 2)
    line_pair = lax.div(z, 2)
    major = core * x + (1 - core) * y
    minor = core * y + (1 - core) * x

    def near(by):
        return (lax.rem(slab + by + slabs, slabs), cross)

    def place(at_x, at_y, at_z):
        return (lax.rem(at_y, 2) * (RING * LINE) + at_x * LINE + at_z, lax.div(at_y, 2) * 2 + core)

    def in_line(by):
        return lax.rem(z + by + LINE, LINE)

    def minor_peer(other):
        return place(core * x + (1 - core) * other, core * other + (1 - core) * y, z)

    def major_peer(other):
        return place(core * other + (1 - core) * x, core * y + (1 - core) * other, z)

    def turn(own, by):
        return lax.rem(own + by, RING)

    copy = send

    other_core = (slab, cross + 1 - 2 * core)
    line_from = [sign * k for k in (1, 3, 5, 7)] + [-sign * k for k in (2, 4, 6)]
    low = lax.rem(2 * pair - 1 + slabs, slabs)
    high = lax.rem(2 * pair + 2, slabs)

    barrier = pltpu.get_barrier_semaphore()
    sources = [near(-sign), (low, cross), (high, cross), near(-1), near(1)]
    sources += [place(x, y, in_line(by)) for by in line_from]
    sources += [minor_peer(turn(minor, by)) for by in (1, 2, 3)]
    sources += [major_peer(turn(major, by)) for by in (1, 2, 3)]
    sources += [other_core]
    for device in sources:
        pl.semaphore_signal(barrier, inc=1, device_id=device, device_id_type=pl.DeviceIdType.MESH)
    own, low_tile, high_tile = scatter(table, cell_ref, terms_ref, base_ref, edge_ref, slots)
    own_ref[...] = own + jnp.where(odd == 1, low_tile, high_tile)
    outer_ref[...] = jnp.where(odd == 1, high_tile, low_tile)
    pl.semaphore_wait(barrier, len(sources))

    copies = [
        copy(own_ref, got.at[0], pair_send.at[0], pair_recv.at[0], near(-sign)),
        copy(outer_ref, got.at[2 - odd], pair_send.at[1], pair_recv.at[2 - odd], near(sign)),
        copy(outer_ref, got.at[2 - odd], pair_send.at[2], pair_recv.at[2 - odd], near(2 * sign)),
    ]
    for each in copies:
        each.start()
    for slot in range(3):
        copy(own_ref, got.at[slot], pair_send.at[slot], pair_recv.at[slot], near(1)).wait_recv()
    grid_ref[core, major, minor, line_pair] = (own_ref[...] + got[0]) + (got[1] + got[2])
    edges = [
        copy(edge_ref.at[0], halo_ref.at[1], edge_send.at[0], edge_recv.at[1], near(-1)),
        copy(edge_ref.at[1], halo_ref.at[0], edge_send.at[1], edge_recv.at[0], near(1)),
    ]
    tile = grid_ref.at[core, major, minor, line_pair]
    line = [
        copy(tile, tile, line_send.at[k - 1], line_recv.at[line_pair], place(x, y, in_line(sign * k)))
        for k in range(1, 8)
    ]
    for each in line:
        each.start()
    for each in edges:
        each.start()
    for by in line_from:
        other = lax.div(in_line(by), 2)
        copy(
            tile, grid_ref.at[core, major, minor, other], line_send.at[0], line_recv.at[other], near(1)
        ).wait_recv()

    block = grid_ref.at[core, major, minor]
    minors = [
        copy(block, block, minor_send.at[by - 1], minor_recv.at[minor], minor_peer(turn(minor, by)))
        for by in (1, 2, 3)
    ]
    for each in minors:
        each.start()
    for by in (1, 2, 3):
        other = turn(minor, by)
        copy(
            block, grid_ref.at[core, major, other], minor_send.at[0], minor_recv.at[other], near(1)
        ).wait_recv()

    row = grid_ref.at[core, major]
    majors = [
        copy(row, row, major_send.at[by - 1], major_recv.at[major], major_peer(turn(major, by)))
        for by in (1, 2, 3)
    ]
    for each in majors:
        each.start()
    cores = []
    for by in range(RING):
        other = turn(major, by)
        arrived = grid_ref.at[core, other]
        if by:
            copy(row, arrived, major_send.at[0], major_recv.at[other], near(1)).wait_recv()
        each = copy(arrived, arrived, core_send.at[by], core_recv.at[other], other_core)
        each.start()
        cores.append(each)
    for by in range(RING):
        far = grid_ref.at[1 - core, by]
        copy(far, far, core_send.at[0], core_recv.at[by], other_core).wait_recv()
    for slot in range(2):
        copy(edge_ref.at[0], halo_ref.at[slot], edge_send.at[0], edge_recv.at[slot], near(1)).wait_recv()
    for each in copies + edges + line + minors + majors + cores:
        each.wait_send()


def spread(table, cells, terms):
    dma = pltpu.SemaphoreType.DMA
    vmem = pl.BlockSpec(memory_space=pltpu.VMEM)
    smem = pl.BlockSpec(memory_space=pltpu.SMEM)
    side = (2, FIELDS, TILES * LANES)
    return pl.pallas_call(
        spread_kernel,
        out_shape=(
            jax.ShapeDtypeStruct((FIELDS * TILES * PLANES, LANES), jnp.float32),
            jax.ShapeDtypeStruct(side, jnp.float32),
            jax.ShapeDtypeStruct((2, RING, RING, LINE // 2, ROWS, LANES), jnp.float32),
        ),
        in_specs=[smem, vmem, vmem],
        out_specs=(vmem, vmem, vmem),
        scratch_shapes=[
            pltpu.VMEM((ROWS, LANES), jnp.float32),
            pltpu.VMEM((ROWS, LANES), jnp.float32),
            pltpu.VMEM(side, jnp.float32),
            pltpu.VMEM((PAIRS + 1, FIELDS, CHUNK), jnp.float32),
            pltpu.VMEM((3, ROWS, LANES), jnp.float32),
            dma((3,)), dma((3,)), dma((2,)), dma((2,)), dma((7,)), dma((LINE // 2,)),
            dma((3,)), dma((RING,)), dma((3,)), dma((RING,)), dma((RING,)), dma((RING,)),
        ],
        compiler_params=pltpu.CompilerParams(
            collective_id=0, has_side_effects=True, vmem_limit_bytes=16 << 20
        ),
        name="spread",
    )(table, cells, terms)


def finish_kernel(base_ref, halo_ref, grid_ref, fine_ref, out_ref, fine, source, even, uneven, flat, result, fine_sem, out_sem):
    sub = lax.broadcasted_iota(jnp.int32, (ROWS, LANES), 0)
    lane = lax.broadcasted_iota(jnp.int32, (ROWS, LANES), 1)
    first = sub == 0
    last = sub == ROWS - 1
    for f in range(FIELDS):
        for t in range(TILES):
            cols = slice(t * LANES, (t + 1) * LANES)
            rows = slice((f * TILES + t) * PLANES, (f * TILES + t + 1) * PLANES)
            low = jnp.broadcast_to(halo_ref[0, f : f + 1, cols], (PLANES, LANES))
            high = jnp.broadcast_to(halo_ref[1, f : f + 1, cols], (PLANES, LANES))
            fine[rows, :] = base_ref[rows, :] + jnp.where(first, low, jnp.where(last, high, 0.0))
    fine_copy = pltpu.make_async_copy(fine, fine_ref, fine_sem)
    fine_copy.start()

    wide = COARSE // 2
    none = jnp.zeros((wide, LANES), jnp.float32)
    for held in (even, uneven):
        held[0] = none
        held[COARSE + 1] = none
    for plane in range(COARSE):
        y_lo, x, j = plane // 32, (plane // 8) % RING, plane % 8
        for c in range(RING):
            y = (c // 2) * 2 + y_lo
            at = grid_ref[0, y, x, j] if c % 2 == 0 else grid_ref[1, x, y, j]
            value = at * (1.0 / 6.0)
            source[plane, c * ROWS : (c + 1) * ROWS, :] = value
            even[plane + 1, c * ROWS : (c + 1) * ROWS, :] = value

    half = LANES // 2
    depth = lax.rem(lane, half)
    upper = jnp.where(depth < half - 1, 1.0, 0.0)
    lower = jnp.where(depth > 0, 1.0, 0.0)
    left = lane < half
    blank = jnp.zeros((ROWS, LANES), jnp.float32)

    def relaxed(src, plane):
        mid = [src[plane + 1, c * ROWS : (c + 1) * ROWS, :] for c in range(RING)]
        turned = [pltpu.roll(value, half, 1) for value in mid]
        down = [blank] + [pltpu.roll(value, 1, 0) for value in turned]
        up = [pltpu.roll(value, ROWS - 1, 0) for value in turned] + [blank]
        for c in range(RING):
            tile = slice(c * ROWS, (c + 1) * ROWS)
            before = jnp.where(first, down[c], down[c + 1])
            after = jnp.where(last, up[c + 1], up[c])
            total = turned[c] + jnp.where(left, before, after)
            total += pltpu.roll(mid[c], LANES - 1, 1) * upper
            total += pltpu.roll(mid[c], 1, 1) * lower
            total += src[plane, tile, :] + src[plane + 2, tile, :]
            yield tile, total * (1.0 / 6.0) + source[plane, tile, :]

    def sweep(src, dst):
        def some(n, carry):
            for k in range(UNROLL):
                plane = n * UNROLL + k
                for tile, value in relaxed(src, plane):
                    dst[plane + 1, tile, :] = value
            return carry

        lax.fori_loop(0, COARSE // UNROLL, some, 0)

    sweep(even, uneven)
    sweep(uneven, even)
    copies = []
    for group in range(COARSE // ROWS):
        for k in range(ROWS):
            plane = group * ROWS + k
            for tile, value in relaxed(even, plane):
                flat[plane * wide + tile.start : plane * wide + tile.stop, :] = value
        rows = slice(group * ROWS, (group + 1) * ROWS)
        for r in range(wide):
            value = flat[pl.ds(group * ROWS * wide + r, ROWS, stride=wide), :]
            result[rows, r * LANES : (r + 1) * LANES] = value
        each = pltpu.make_async_copy(result.at[rows], out_ref.at[rows], out_sem.at[group])
        each.start()
        copies.append(each)
    for each in copies:
        each.wait()
    fine_copy.wait()


def finish(base, halo_sum, grid):
    wide = COARSE // 2
    vmem = pl.BlockSpec(memory_space=pltpu.VMEM)
    hbm = pl.BlockSpec(memory_space=pl.ANY)
    dma = pltpu.SemaphoreType.DMA
    return pl.pallas_call(
        finish_kernel,
        out_shape=(
            jax.ShapeDtypeStruct(base.shape, jnp.float32),
            jax.ShapeDtypeStruct((COARSE, COARSE * COARSE), jnp.float32),
        ),
        in_specs=[vmem, vmem, vmem],
        out_specs=(hbm, hbm),
        scratch_shapes=[
            pltpu.VMEM(base.shape, jnp.float32),
            pltpu.VMEM((COARSE, wide, LANES), jnp.float32),
            pltpu.VMEM((COARSE + 2, wide, LANES), jnp.float32),
            pltpu.VMEM((COARSE + 2, wide, LANES), jnp.float32),
            pltpu.VMEM((COARSE * wide, LANES), jnp.float32),
            pltpu.VMEM((COARSE, COARSE * COARSE), jnp.float32),
            dma, dma((COARSE // ROWS,)),
        ],
        compiler_params=pltpu.CompilerParams(vmem_limit_bytes=16 << 20),
        name="finish",
    )(base, halo_sum, grid)


def body(gas_state, parcel_record, condensed_shares, surface_steam_factor, fine_cell, block_counts):
    rows = gas_state.reshape(FIELDS, PLANES, TILES, LANES).transpose(0, 2, 1, 3).reshape(-1, LANES)
    parts = halo(rows)
    parcel_next, terms, table = spray(
        parts, parcel_record, condensed_shares, surface_steam_factor, fine_cell, block_counts
    )
    base, halo_sum, grid = spread(table, fine_cell.reshape(-1, BLOCK), terms)
    fine_rows, correction = finish(base, halo_sum, grid)
    fine_source = fine_rows.reshape(FIELDS, TILES, PLANES, LANES).transpose(0, 2, 1, 3).reshape(gas_state.shape)
    return (parcel_next, fine_source, correction)


def solution(mesh):
    in_specs = (
        P(None, "slab", "cross"),
        P(None, ("slab", "cross")),
        P(None, ("slab", "cross")),
        P(),
        P(("slab", "cross")),
        P(("slab", "cross")),
    )
    out_specs = (P(None, ("slab", "cross")), P(None, "slab", "cross"), P())
    return jax.shard_map(body, mesh=mesh, in_specs=in_specs, out_specs=out_specs, check_vma=False)
```

time: 142 us -> 66.8 us (0.47)
  other arithmetic: 45.8 us -> 0 us
  local copies, waits for them, and re-layouts: 40.1 us -> 1.99 us
  Pallas kernels: 48.7 us -> 63.9 us
  starting transfers between devices: 6.29 us -> 0 us
    scatter-add x1 -> x0, other arithmetic: 27 us -> none  [body(): extended = jnp.zeros((fields, (planes + 2) * cross_cells), jnp.float32).a...]
    gather x2 -> x0, local copies, waits for them, and re-layouts: 15.4 us -> none  [body(): ambient_layer_fields = jnp.take(gas_flat, fine_cell, axis=1)]
    pallas_call x1 -> x3, Pallas kernels: 42.8 us -> 57.7 us  [the longest x1 32.9 us: spread(): pl.pallas_call(spread_kernel, out_shape=(jax.ShapeDtypeStruct((FIELDS * T...]
    reduce_sum x5 -> x0, other arithmetic: 12.9 us -> none  [the longest x2 12.7 us: body(): extended[4:].sum(axis=0).reshape(planes + 2, ROWS, LANES, 2).sum(axis=3)]
    ppermute x2 -> x0, starting transfers between devices: 6.29 us -> none  [the longest x1 5 us: with_halo(): before = lax.ppermute(last, axis, up)]
    reshape x1, local copies, waits for them, and re-layouts: 6.82 us -> 0.75 us  [spray(): surface_steam_factor.reshape(-1, 1)]
    slice x3 -> x0, local copies, waits for them, and re-layouts: 5.66 us -> none  [the longest x1 3.76 us: body(): fine_source, correction = finish(extended[:, 1:planes + 1], halo, grid)]
    concatenate x1 -> x0, local copies, waits for them, and re-layouts: 5.42 us -> none  [with_halo(): shard = jnp.concatenate([before, shard, after], axis=dim)]
  transfers between devices with their start and end apart: 2 -> 0, of which waited for: 0 -> 0; matrix products, arithmetic and copies ran while one was open for 2% -> 0% of each run, Pallas kernels for 0% -> 0%
where the time goes in v4:
time: 66.8 us; the launch traced here: 66.6 us
  Pallas kernels  63.9 us (96%)
  local copies, waits for them, and re-layouts  1.99 us (3%)
  between operations  0.7 us (1%)
    pallas_call x1, Pallas kernels, spread(): pl.pallas_call(spread_kernel, out_shape=(jax.ShapeDtypeStruct((FIELDS * T...  32.9 us
    pallas_call x1, Pallas kernels, halo(): pl.pallas_call(halo_kernel, out_shape=jax.ShapeDtypeStruct((chunks, 3 * F...  17.8 us
    pallas_call x1, Pallas kernels, spray(): pl.pallas_call(spray_kernel, out_shape=(jax.ShapeDtypeStruct(parcel_recor...  7.04 us
    pallas_call x1, Pallas kernels, finish(): pl.pallas_call(finish_kernel, out_shape=(jax.ShapeDtypeStruct(base.shape,...  6.22 us

profile of v4, /device:TPU:1, one launch (start us, length us, event | category | flops | bytes accessed | tf_op | source)
XLA Modules:
  0.0 66.6 jit_solution(14144186423351498765)
XLA Ops:
  0.6 0.0 copy-start.4
  0.6 0.7 %copy.9.steam_ref = f32[12,1]{1,0:T(8,128)S(1)} copy(f32[12,1]{0,1:T(1,128)} %bitcast.15) | data formatting | bytes 96 | tf_op jit(solution)/shard_map/reshape | solution.py:217
  1.4 0.0 copy-start
  1.4 1.2 %copy-done = f32[16,8,2048]{2,1,0:T(8,128)S(1)} copy-done((f32[16,8,2048]{2,1,0:T(8,128)S(1)}, f32[16,8,2048]{2,1,0:T(8,128)}, u32[]{:S(2)}) %copy-start) | copy-done | bytes 1048600
  2.6 0.0 copy-start.1
  2.6 0.0 copy-start.2
  2.6 0.0 copy-start.3
  2.6 17.8 %halo.1.gas_parts = bf16[40,48,512]{2,1,0:T(8,128)(2,1)S(1)} custom-call(f32[2048,128]{1,0:T(8,128)S(1)} %bitcast.12), custom_call_target="tpu_custom_call" | custom-call | tf_op jit(solution)/shard_map/halo/pallas_call | solution.py:95
  20.5 0.0 copy-done.4
  20.5 0.0 copy-done.1
  20.5 0.0 copy-done.2
  20.5 0.0 copy-done.3
  20.5 7.0 %spray.1 = (f32[5,4096]{1,0:T(8,128)}, f32[32,16,128]{2,1,0:T(8,128)S(1)}, s32[240]{0:T(256)S(1)}) custom-call(s32[4096]{0:T(1024)S(1)} %copy-done.2, s32[32]{0:T(128)S(1)} %copy-done.4, bf16[40,48,512]{2,1,0:T(8,128)(2,1)S(1)} %halo.1.gas_parts, f32[5,4096]{1,0:T(8,128)S(1)} %copy-done.3, f32[12,4096]{1,0:T(8,128)S(1)} %copy-done.1, ...), custom_call_target="tpu_custom_call" | custom-call | tf_op jit(solution)/shard_map/spray/pallas_call | solution.py:201
  27.5 32.9 %spread.1 = (f32[2048,128]{1,0:T(8,128)S(1)}, f32[2,16,2048]{2,1,0:T(8,128)S(1)}, f32[2,4,4,8,8,128]{5,4,3,2,1,0:T(8,128)S(1)}) custom-call(s32[240]{0:T(256)S(1)} %get-tuple-element.12.table, s32[32,128]{1,0:T(8,128)S(1)} %bitcast.14, f32[32,16,128]{2,1,0:T(8,128)S(1)} %get-tuple-element.13.terms_ref), custom_call_target="tpu_custom_call" | custom-call | tf_op jit(solution)/shard_map/spread/pallas_call | solution.py:407
  60.4 6.2 %finish.1 = (f32[2048,128]{1,0:T(8,128)}, f32[64,4096]{1,0:T(8,128)}) custom-call(f32[2048,128]{1,0:T(8,128)S(1)} %get-tuple-element.14.base_ref, f32[2,16,2048]{2,1,0:T(8,128)S(1)} %get-tuple-element.15.halo_ref, f32[2,4,4,8,8,128]{5,4,3,2,1,0:T(8,128)S(1)} %get-tuple-element.16.grid_ref), custom_call_target="tpu_custom_call" | custom-call | tf_op jit(solution)/shard_map/finish/pallas_call | solution.py:518
Async XLA Ops:
  0.6 19.8 %copy-start.4 = (s32[32]{0:T(128)S(1)}, s32[32]{0:T(128)}, u32[]{:S(2)}) copy-start(s32[32]{0:T(128)} %count_at.1) | copy-start | bytes 388
  1.4 1.2 %copy-start = (f32[16,8,2048]{2,1,0:T(8,128)S(1)}, f32[16,8,2048]{2,1,0:T(8,128)}, u32[]{:S(2)}) copy-start(f32[16,8,2048]{2,1,0:T(8,128)} %param.6) | copy-start | bytes 3145732
  2.6 17.9 %copy-start.1 = (f32[12,4096]{1,0:T(8,128)S(1)}, f32[12,4096]{1,0:T(8,128)}, u32[]{:S(2)}) copy-start(f32[12,4096]{1,0:T(8,128)} %shares_ref.1) | copy-start | bytes 589828
  2.6 17.9 %copy-start.2 = (s32[4096]{0:T(1024)S(1)}, s32[4096]{0:T(1024)}, u32[]{:S(2)}) copy-start(s32[4096]{0:T(1024)} %cell_at.1) | copy-start | bytes 49156
  2.6 17.9 %copy-start.3 = (f32[5,4096]{1,0:T(8,128)S(1)}, f32[5,4096]{1,0:T(8,128)}, u32[]{:S(2)}) copy-start(f32[5,4096]{1,0:T(8,128)} %record_ref.1) | copy-start | bytes 245764

commit v5 on v4

--- a/solution.py
+++ b/solution.py
@@ -30,6 +30,9 @@
 UNROLL = 4
 PAIRS = 72
 ROOM = 80
+LAG_MINOR = 5
+LAG_MAJOR = 5
+STRIDE = 40
 
 
 def parts_of(value):
@@ -159,7 +162,10 @@
     lax.fori_loop(0, rounds, gather, 0)
 
     lane = lax.broadcasted_iota(jnp.int32, (1, BLOCK), 1)
-    steam = steam_ref[...]
+    species = lax.broadcasted_iota(jnp.int32, (steam_ref.shape[0], BLOCK), 0)
+    steam = jnp.zeros(species.shape, jnp.float32)
+    for k in range(steam_ref.shape[0]):
+        steam = jnp.where(species == k, steam_ref[k], steam)
 
     def step(n, carry):
         for k in range(UNROLL):
@@ -205,7 +211,7 @@
             jax.ShapeDtypeStruct((blocks, FIELDS, BLOCK), jnp.float32),
             jax.ShapeDtypeStruct((3 * ROOM,), jnp.int32),
         ),
-        in_specs=[smem, smem] + [vmem] * 5,
+        in_specs=[smem, smem] + [vmem] * 3 + [smem, vmem],
         out_specs=(vmem, vmem, smem),
         scratch_shapes=[
             pltpu.VMEM((blocks, FIELDS, BLOCK), jnp.float32),
@@ -214,7 +220,7 @@
         name="spray",
     )(
         fine_cell, block_counts, gas_parts, parcel_record, condensed_shares,
-        surface_steam_factor.reshape(-1, 1), fine_cell.reshape(blocks, BLOCK),
+        surface_steam_factor, fine_cell.reshape(blocks, BLOCK),
     )
 
 
@@ -347,55 +353,59 @@
         copy(edge_ref.at[1], halo_ref.at[0], edge_send.at[1], edge_recv.at[0], near(1)),
     ]
     tile = grid_ref.at[core, major, minor, line_pair]
-    line = [
-        copy(tile, tile, line_send.at[k - 1], line_recv.at[line_pair], place(x, y, in_line(sign * k)))
-        for k in range(1, 8)
-    ]
-    for each in line:
+    for k in range(1, 8):
+        each = copy(tile, tile, line_send.at[k - 1], line_recv.at[line_pair], place(x, y, in_line(sign * k)))
         each.start()
-    for each in edges:
+        copies.append(each)
+    tiles = [line_pair] + [lax.div(in_line(sign * k if k % 2 else -sign * k), 2) for k in range(1, 8)]
+
+    def go(src, dst, send_sem, recv_sem, device):
+        each = copy(src, dst, send_sem, recv_sem, device)
         each.start()
-    for by in line_from:
-        other = lax.div(in_line(by), 2)
-        copy(
-            tile, grid_ref.at[core, major, minor, other], line_send.at[0], line_recv.at[other], near(1)
-        ).wait_recv()
-
-    block = grid_ref.at[core, major, minor]
-    minors = [
-        copy(block, block, minor_send.at[by - 1], minor_recv.at[minor], minor_peer(turn(minor, by)))
-        for by in (1, 2, 3)
-    ]
-    for each in minors:
-        each.start()
-    for by in (1, 2, 3):
-        other = turn(minor, by)
-        copy(
-            block, grid_ref.at[core, major, other], minor_send.at[0], minor_recv.at[other], near(1)
-        ).wait_recv()
-
-    row = grid_ref.at[core, major]
-    majors = [
-        copy(row, row, major_send.at[by - 1], major_recv.at[major], major_peer(turn(major, by)))
-        for by in (1, 2, 3)
-    ]
-    for each in majors:
-        each.start()
-    cores = []
+        copies.append(each)
+
+    def to_minors(k):
+        t = tiles[k]
+        src = grid_ref.at[core, major, minor, t]
+        if k:
+            copy(src, src, line_send.at[0], line_recv.at[t], near(1)).wait_recv()
+        for by in (1, 2, 3):
+            go(src, src, minor_send.at[by - 1, k], minor_recv.at[minor, t], minor_peer(turn(minor, by)))
+
+    def to_majors(k):
+        t = tiles[k]
+        for by in (1, 2, 3):
+            src = grid_ref.at[core, major, turn(minor, by), t]
+            copy(src, src, minor_send.at[0, k], minor_recv.at[turn(minor, by), t], near(1)).wait_recv()
+        src = grid_ref.at[core, major, :, t]
+        for by in (1, 2, 3):
+            go(src, src, major_send.at[by - 1, k], major_recv.at[major, t], major_peer(turn(major, by)))
+        go(src, src, core_send.at[0, k], core_recv.at[major, t], other_core)
+
+    def to_core(k):
+        t = tiles[k]
+        for by in (1, 2, 3):
+            src = grid_ref.at[core, turn(major, by), :, t]
+            copy(src, src, major_send.at[0, k], major_recv.at[turn(major, by), t], near(1)).wait_recv()
+            go(src, src, core_send.at[by, k], core_recv.at[turn(major, by), t], other_core)
+
+    for step in range(8 + LAG_MINOR + LAG_MAJOR):
+        if step < 8:
+            to_minors(step)
+        if step == 0:
+            for each in edges:
+                each.start()
+        if 0 <= step - LAG_MINOR < 8:
+            to_majors(step - LAG_MINOR)
+        if 0 <= step - LAG_MINOR - LAG_MAJOR < 8:
+            to_core(step - LAG_MINOR - LAG_MAJOR)
     for by in range(RING):
-        other = turn(major, by)
-        arrived = grid_ref.at[core, other]
-        if by:
-            copy(row, arrived, major_send.at[0], major_recv.at[other], near(1)).wait_recv()
-        each = copy(arrived, arrived, core_send.at[by], core_recv.at[other], other_core)
-        each.start()
-        cores.append(each)
-    for by in range(RING):
-        far = grid_ref.at[1 - core, by]
-        copy(far, far, core_send.at[0], core_recv.at[by], other_core).wait_recv()
+        for k in range(8):
+            src = grid_ref.at[1 - core, by, :, k]
+            copy(src, src, core_send.at[0, k], core_recv.at[by, k], other_core).wait_recv()
     for slot in range(2):
         copy(edge_ref.at[0], halo_ref.at[slot], edge_send.at[0], edge_recv.at[slot], near(1)).wait_recv()
-    for each in copies + edges + line + minors + majors + cores:
+    for each in copies + edges:
         each.wait_send()
 
 
@@ -420,7 +430,7 @@
             pltpu.VMEM((PAIRS + 1, FIELDS, CHUNK), jnp.float32),
             pltpu.VMEM((3, ROWS, LANES), jnp.float32),
             dma((3,)), dma((3,)), dma((2,)), dma((2,)), dma((7,)), dma((LINE // 2,)),
-            dma((3,)), dma((RING,)), dma((3,)), dma((RING,)), dma((RING,)), dma((RING,)),
+            dma((3, 8)), dma((RING, 8)), dma((3, 8)), dma((RING, 8)), dma((RING, 8)), dma((RING, 8)),
         ],
         compiler_params=pltpu.CompilerParams(
             collective_id=0, has_side_effects=True, vmem_limit_bytes=16 << 20
@@ -429,7 +439,7 @@
     )(table, cells, terms)
 
 
-def finish_kernel(base_ref, halo_ref, grid_ref, fine_ref, out_ref, fine, source, even, uneven, flat, result, fine_sem, out_sem):
+def finish_kernel(base_ref, halo_ref, grid_ref, fine_ref, out_ref, fine, source, even, uneven, even_turned, uneven_turned, flat, result, fine_sem, out_sem):
     sub = lax.broadcasted_iota(jnp.int32, (ROWS, LANES), 0)
     lane = lax.broadcasted_iota(jnp.int32, (ROWS, LANES), 1)
     first = sub == 0
@@ -446,9 +456,19 @@
 
     wide = COARSE // 2
     none = jnp.zeros((wide, LANES), jnp.float32)
-    for held in (even, uneven):
+    blank = jnp.zeros((ROWS, LANES), jnp.float32)
+    half = LANES // 2
+    for held, turned in ((even, even_turned), (uneven, uneven_turned)):
         held[0] = none
         held[COARSE + 1] = none
+        for plane in range(COARSE + 1):
+            turned[plane * STRIDE : plane * STRIDE + ROWS, :] = blank
+
+    def keep(held, turned, plane, c, value):
+        held[plane + 1, c * ROWS : (c + 1) * ROWS, :] = value
+        at = pl.multiple_of(plane * STRIDE + (c + 1) * ROWS, ROWS)
+        turned[pl.ds(at, ROWS), :] = pltpu.roll(value, half, 1)
+
     for plane in range(COARSE):
         y_lo, x, j = plane // 32, (plane // 8) % RING, plane % 8
         for c in range(RING):
@@ -456,48 +476,42 @@
             at = grid_ref[0, y, x, j] if c % 2 == 0 else grid_ref[1, x, y, j]
             value = at * (1.0 / 6.0)
             source[plane, c * ROWS : (c + 1) * ROWS, :] = value
-            even[plane + 1, c * ROWS : (c + 1) * ROWS, :] = value
-
-    half = LANES // 2
+            keep(even, even_turned, plane, c, value)
+
     depth = lax.rem(lane, half)
-    upper = jnp.where(depth < half - 1, 1.0, 0.0)
-    lower = jnp.where(depth > 0, 1.0, 0.0)
+    upper = depth < half - 1
+    lower = depth > 0
     left = lane < half
-    blank = jnp.zeros((ROWS, LANES), jnp.float32)
-
-    def relaxed(src, plane):
-        mid = [src[plane + 1, c * ROWS : (c + 1) * ROWS, :] for c in range(RING)]
-        turned = [pltpu.roll(value, half, 1) for value in mid]
-        down = [blank] + [pltpu.roll(value, 1, 0) for value in turned]
-        up = [pltpu.roll(value, ROWS - 1, 0) for value in turned] + [blank]
-        for c in range(RING):
-            tile = slice(c * ROWS, (c + 1) * ROWS)
-            before = jnp.where(first, down[c], down[c + 1])
-            after = jnp.where(last, up[c + 1], up[c])
-            total = turned[c] + jnp.where(left, before, after)
-            total += pltpu.roll(mid[c], LANES - 1, 1) * upper
-            total += pltpu.roll(mid[c], 1, 1) * lower
-            total += src[plane, tile, :] + src[plane + 2, tile, :]
-            yield tile, total * (1.0 / 6.0) + source[plane, tile, :]
-
-    def sweep(src, dst):
+
+    def relaxed(held, turned, plane, c):
+        tile = slice(c * ROWS, (c + 1) * ROWS)
+        at = plane * STRIDE + (c + 1) * ROWS
+        mid = held[plane + 1, tile, :]
+        across = jnp.where(left, turned[pl.ds(at - 1, ROWS), :], turned[pl.ds(at + 1, ROWS), :])
+        total = turned[pl.ds(at, ROWS), :] + across
+        along = jnp.where(upper, pltpu.roll(mid, LANES - 1, 1), 0.0)
+        along += jnp.where(lower, pltpu.roll(mid, 1, 1), 0.0)
+        total += along + (held[plane, tile, :] + held[plane + 2, tile, :])
+        return total * (1.0 / 6.0) + source[plane, tile, :]
+
+    def sweep(held, turned, to, to_turned):
         def some(n, carry):
             for k in range(UNROLL):
-                plane = n * UNROLL + k
-                for tile, value in relaxed(src, plane):
-                    dst[plane + 1, tile, :] = value
+                for c in range(RING):
+                    keep(to, to_turned, n * UNROLL + k, c, relaxed(held, turned, n * UNROLL + k, c))
             return carry
 
         lax.fori_loop(0, COARSE // UNROLL, some, 0)
 
-    sweep(even, uneven)
-    sweep(uneven, even)
+    sweep(even, even_turned, uneven, uneven_turned)
+    sweep(uneven, uneven_turned, even, even_turned)
     copies = []
     for group in range(COARSE // ROWS):
         for k in range(ROWS):
             plane = group * ROWS + k
-            for tile, value in relaxed(even, plane):
-                flat[plane * wide + tile.start : plane * wide + tile.stop, :] = value
+            for c in range(RING):
+                at = plane * wide + c * ROWS
+                flat[at : at + ROWS, :] = relaxed(even, even_turned, plane, c)
         rows = slice(group * ROWS, (group + 1) * ROWS)
         for r in range(wide):
             value = flat[pl.ds(group * ROWS * wide + r, ROWS, stride=wide), :]
@@ -528,6 +542,8 @@
             pltpu.VMEM((COARSE, wide, LANES), jnp.float32),
             pltpu.VMEM((COARSE + 2, wide, LANES), jnp.float32),
             pltpu.VMEM((COARSE + 2, wide, LANES), jnp.float32),
+            pltpu.VMEM((COARSE * STRIDE + ROWS, LANES), jnp.float32),
+            pltpu.VMEM((COARSE * STRIDE + ROWS, LANES), jnp.float32),
             pltpu.VMEM((COARSE * wide, LANES), jnp.float32),
             pltpu.VMEM((COARSE, COARSE * COARSE), jnp.float32),
             dma, dma((COARSE // ROWS,)),

time: 66.8 us -> 66.7 us (level)
  local copies, waits for them, and re-layouts: 1.99 us -> 1.25 us
    pallas_call x1, Pallas kernels: 6.22 us -> 7.84 us  [finish(): pl.pallas_call(finish_kernel, out_shape=(jax.ShapeDtypeStruct(base.shape,...]
    pallas_call x1, Pallas kernels: 32.9 us -> 32 us  [spread(): pl.pallas_call(spread_kernel, out_shape=(jax.ShapeDtypeStruct((FIELDS * T...]
    reshape x1 -> x0, local copies, waits for them, and re-layouts: 0.75 us -> none  [spray(): surface_steam_factor.reshape(-1, 1)]
where the time goes in v5:
time: 66.7 us; the launch traced here: 66.5 us
  Pallas kernels  64.5 us (97%)
  local copies, waits for them, and re-layouts  1.25 us (2%)
  between operations  0.72 us (1%)
    pallas_call x1, Pallas kernels, spread(): pl.pallas_call(spread_kernel, out_shape=(jax.ShapeDtypeStruct((FIELDS * T...  32 us
    pallas_call x1, Pallas kernels, halo(): pl.pallas_call(halo_kernel, out_shape=jax.ShapeDtypeStruct((chunks, 3 * F...  17.8 us
    pallas_call x1, Pallas kernels, finish(): pl.pallas_call(finish_kernel, out_shape=(jax.ShapeDtypeStruct(base.shape,...  7.84 us
    pallas_call x1, Pallas kernels, spray(): pl.pallas_call(spray_kernel, out_shape=(jax.ShapeDtypeStruct(parcel_recor...  6.84 us

profile of v5, /device:TPU:1, one launch (start us, length us, event | category | flops | bytes accessed | tf_op | source)
XLA Modules:
  0.0 66.5 jit_solution(15353214619741341624)
XLA Ops:
  0.6 0.0 copy-start.4
  0.6 0.0 copy-start.5
  0.7 0.0 copy-start
  0.7 1.2 %copy-done = f32[16,8,2048]{2,1,0:T(8,128)S(1)} copy-done((f32[16,8,2048]{2,1,0:T(8,128)S(1)}, f32[16,8,2048]{2,1,0:T(8,128)}, u32[]{:S(2)}) %copy-start) | copy-done | bytes 1048600
  1.9 0.0 copy-start.1
  1.9 0.0 copy-start.2
  1.9 0.0 copy-start.3
  1.9 17.8 %halo.1.gas_parts = bf16[40,48,512]{2,1,0:T(8,128)(2,1)S(1)} custom-call(f32[2048,128]{1,0:T(8,128)S(1)} %bitcast.11), custom_call_target="tpu_custom_call" | custom-call | tf_op jit(solution)/shard_map/halo/pallas_call | solution.py:98
  19.7 0.0 copy-done.4
  19.7 0.0 copy-done.5
  19.8 0.0 copy-done.1
  19.8 0.0 copy-done.2
  19.8 0.0 copy-done.3
  19.8 6.8 %spray.1 = (f32[5,4096]{1,0:T(8,128)}, f32[32,16,128]{2,1,0:T(8,128)S(1)}, s32[240]{0:T(256)S(1)}) custom-call(s32[4096]{0:T(1024)S(1)} %copy-done.2, s32[32]{0:T(128)S(1)} %copy-done.4, bf16[40,48,512]{2,1,0:T(8,128)(2,1)S(1)} %halo.1.gas_parts, f32[5,4096]{1,0:T(8,128)S(1)} %copy-done.3, f32[12,4096]{1,0:T(8,128)S(1)} %copy-done.1, f32[12]{0:T(128)S(1)} %copy-done.5, ...), custom_call_target="tpu_custom_call" | custom-call | tf_op jit(solution)/shard_map/spray/pallas_call | solution.py:207
  26.6 32.0 %spread.1 = (f32[2048,128]{1,0:T(8,128)S(1)}, f32[2,16,2048]{2,1,0:T(8,128)S(1)}, f32[2,4,4,8,8,128]{5,4,3,2,1,0:T(8,128)S(1)}) custom-call(s32[240]{0:T(256)S(1)} %get-tuple-element.12.table, s32[32,128]{1,0:T(8,128)S(1)} %bitcast.13, f32[32,16,128]{2,1,0:T(8,128)S(1)} %get-tuple-element.13.terms_ref), custom_call_target="tpu_custom_call" | custom-call | tf_op jit(solution)/shard_map/spread/pallas_call | solution.py:417
  58.6 7.8 %finish.1 = (f32[2048,128]{1,0:T(8,128)}, f32[64,4096]{1,0:T(8,128)}) custom-call(f32[2048,128]{1,0:T(8,128)S(1)} %get-tuple-element.14.base_ref, f32[2,16,2048]{2,1,0:T(8,128)S(1)} %get-tuple-element.15.halo_ref, f32[2,4,4,8,8,128]{5,4,3,2,1,0:T(8,128)S(1)} %get-tuple-element.16.grid_ref), custom_call_target="tpu_custom_call" | custom-call | tf_op jit(solution)/shard_map/finish/pallas_call | solution.py:532
Async XLA Ops:
  0.6 19.1 %copy-start.4 = (s32[32]{0:T(128)S(1)}, s32[32]{0:T(128)}, u32[]{:S(2)}) copy-start(s32[32]{0:T(128)} %count_at.1) | copy-start | bytes 388
  0.6 19.1 %copy-start.5 = (f32[12]{0:T(128)S(1)}, f32[12]{0:T(128)}, u32[]{:S(2)}) copy-start(f32[12]{0:T(128)} %steam_ref.1) | copy-start | bytes 148
  0.7 1.2 %copy-start = (f32[16,8,2048]{2,1,0:T(8,128)S(1)}, f32[16,8,2048]{2,1,0:T(8,128)}, u32[]{:S(2)}) copy-start(f32[16,8,2048]{2,1,0:T(8,128)} %param.6) | copy-start | bytes 3145732
  1.9 17.9 %copy-start.1 = (f32[12,4096]{1,0:T(8,128)S(1)}, f32[12,4096]{1,0:T(8,128)}, u32[]{:S(2)}) copy-start(f32[12,4096]{1,0:T(8,128)} %shares_ref.1) | copy-start | bytes 589828
  1.9 17.9 %copy-start.2 = (s32[4096]{0:T(1024)S(1)}, s32[4096]{0:T(1024)}, u32[]{:S(2)}) copy-start(s32[4096]{0:T(1024)} %cell_at.1) | copy-start | bytes 49156
  1.9 17.9 %copy-start.3 = (f32[5,4096]{1,0:T(8,128)S(1)}, f32[5,4096]{1,0:T(8,128)}, u32[]{:S(2)}) copy-start(f32[5,4096]{1,0:T(8,128)} %record_ref.1) | copy-start | bytes 245764

commit v6 on v5

--- a/solution.py
+++ b/solution.py
@@ -24,15 +24,16 @@
 FIELDS = 16
 PLANES = 8
 TILES = 16
-CHUNK = 512
-PER_PLANE = 4
-SHIFT = 9
-UNROLL = 4
-PAIRS = 72
-ROOM = 80
+CHUNK = 256
+PER_PLANE = 8
+SHIFT = 8
+UNROLL = 16
+STEP = 8
+PAIRS = 112
+ROOM = 120
 LAG_MINOR = 5
 LAG_MAJOR = 5
-STRIDE = 40
+SPAN = 16
 
 
 def parts_of(value):
@@ -46,6 +47,18 @@
 def joined(value):
     third = value.shape[0] // 3
     return value[:third] + (value[third : 2 * third] + value[2 * third :])
+
+
+def chosen(row, cells, chunk):
+    place = cells - jnp.where(chunk < 0, (PLANES + 2) * PER_PLANE, chunk) * CHUNK
+    place = jnp.where((place < 0) | (place >= CHUNK), -1, place)
+    place = place.astype(jnp.float32).astype(jnp.bfloat16)
+    return jnp.where(row == place, jnp.bfloat16(1), jnp.bfloat16(0))
+
+
+def chunk_rows():
+    row = lax.broadcasted_iota(jnp.int32, (CHUNK, BLOCK), 0)
+    return row.astype(jnp.float32).astype(jnp.bfloat16)
 
 
 def plane_rows(tile, plane):
@@ -144,12 +157,10 @@
     rounds = lax.div(pairs + UNROLL - 1, UNROLL)
 
     gathered[...] = jnp.zeros(gathered.shape, jnp.float32)
-    row = lax.broadcasted_iota(jnp.int32, (CHUNK, BLOCK), 0)
+    row = chunk_rows()
 
     def picked(i):
-        c = table[ROOM + i]
-        place = cell_ref[pl.ds(table[i], 1), :] - jnp.where(c < 0, chunks, c) * CHUNK
-        return jnp.where(row == place, 1.0, 0.0).astype(jnp.bfloat16)
+        return chosen(row, cell_ref[pl.ds(table[i], 1), :], table[ROOM + i])
 
     def gather(n, carry):
         for k in range(UNROLL):
@@ -168,8 +179,8 @@
         steam = jnp.where(species == k, steam_ref[k], steam)
 
     def step(n, carry):
-        for k in range(UNROLL):
-            b = n * UNROLL + k
+        for k in range(STEP):
+            b = n * STEP + k
             cols = pl.ds(pl.multiple_of(b * BLOCK, BLOCK), BLOCK)
             gas = gathered[b]
             record = record_ref[:, cols]
@@ -197,7 +208,7 @@
             next_ref[4:5, cols] = jnp.where(alive, weight - lost, weight)
         return carry
 
-    lax.fori_loop(0, blocks // UNROLL, step, 0)
+    lax.fori_loop(0, blocks // STEP, step, 0)
 
 
 def spray(gas_parts, parcel_record, condensed_shares, surface_steam_factor, fine_cell, block_counts):
@@ -225,8 +236,7 @@
 
 
 def scatter(table, cell_ref, terms_ref, base_ref, edge, slots):
-    chunks = (PLANES + 2) * PER_PLANE
-    row = lax.broadcasted_iota(jnp.int32, (CHUNK, BLOCK), 0)
+    row = chunk_rows()
 
     def step(n, carry):
         total, before = carry
@@ -234,8 +244,7 @@
             i = n * UNROLL + k
             b = table[i]
             c = table[ROOM + i]
-            place = cell_ref[pl.ds(b, 1), :] - jnp.where(c < 0, chunks, c) * CHUNK
-            picked = jnp.where(row == place, 1.0, 0.0).astype(jnp.bfloat16)
+            picked = chosen(row, cell_ref[pl.ds(b, 1), :], c)
             part = lax.dot_general(
                 parts_of(terms_ref[b]), picked, (((1,), (1,)), ((), ())),
                 preferred_element_type=jnp.float32,
@@ -249,17 +258,13 @@
     lax.fori_loop(0, PAIRS // UNROLL, step, (none, -2))
     slots[PAIRS] = none
 
-    half = CHUNK // 2
-    fold_row = lax.broadcasted_iota(jnp.int32, (half, LANES), 0)
-    fold_lane = lax.broadcasted_iota(jnp.int32, (half, LANES), 1)
+    fold_row = lax.broadcasted_iota(jnp.int32, (CHUNK, LANES), 0)
+    fold_lane = lax.broadcasted_iota(jnp.int32, (CHUNK, LANES), 1)
     fold = jnp.where(lax.shift_right_logical(fold_row, 1) == fold_lane, 1.0, 0.0).astype(jnp.bfloat16)
 
     def mass(value):
         kept = jnp.sum(value[4:], axis=0, keepdims=True)
-        return [
-            joined(jnp.dot(parts_of(kept[:, h * half : (h + 1) * half]), fold, preferred_element_type=jnp.float32))
-            for h in range(2)
-        ]
+        return [joined(jnp.dot(parts_of(kept), fold, preferred_element_type=jnp.float32))]
 
     own, low, high = [], [], []
     group = CHUNK // LANES
@@ -439,7 +444,7 @@
     )(table, cells, terms)
 
 
-def finish_kernel(base_ref, halo_ref, grid_ref, fine_ref, out_ref, fine, source, even, uneven, even_turned, uneven_turned, flat, result, fine_sem, out_sem):
+def finish_kernel(base_ref, halo_ref, grid_ref, fine_ref, out_ref, fine, source, even, uneven, flat, result, fine_sem, out_sem):
     sub = lax.broadcasted_iota(jnp.int32, (ROWS, LANES), 0)
     lane = lax.broadcasted_iota(jnp.int32, (ROWS, LANES), 1)
     first = sub == 0
@@ -456,19 +461,9 @@
 
     wide = COARSE // 2
     none = jnp.zeros((wide, LANES), jnp.float32)
-    blank = jnp.zeros((ROWS, LANES), jnp.float32)
-    half = LANES // 2
-    for held, turned in ((even, even_turned), (uneven, uneven_turned)):
+    for held in (even, uneven):
         held[0] = none
         held[COARSE + 1] = none
-        for plane in range(COARSE + 1):
-            turned[plane * STRIDE : plane * STRIDE + ROWS, :] = blank
-
-    def keep(held, turned, plane, c, value):
-        held[plane + 1, c * ROWS : (c + 1) * ROWS, :] = value
-        at = pl.multiple_of(plane * STRIDE + (c + 1) * ROWS, ROWS)
-        turned[pl.ds(at, ROWS), :] = pltpu.roll(value, half, 1)
-
     for plane in range(COARSE):
         y_lo, x, j = plane // 32, (plane // 8) % RING, plane % 8
         for c in range(RING):
@@ -476,42 +471,48 @@
             at = grid_ref[0, y, x, j] if c % 2 == 0 else grid_ref[1, x, y, j]
             value = at * (1.0 / 6.0)
             source[plane, c * ROWS : (c + 1) * ROWS, :] = value
-            keep(even, even_turned, plane, c, value)
-
+            even[plane + 1, c * ROWS : (c + 1) * ROWS, :] = value
+
+    half = LANES // 2
     depth = lax.rem(lane, half)
-    upper = depth < half - 1
-    lower = depth > 0
+    upper = jnp.where(depth < half - 1, 1.0, 0.0)
+    lower = jnp.where(depth > 0, 1.0, 0.0)
     left = lane < half
-
-    def relaxed(held, turned, plane, c):
-        tile = slice(c * ROWS, (c + 1) * ROWS)
-        at = plane * STRIDE + (c + 1) * ROWS
-        mid = held[plane + 1, tile, :]
-        across = jnp.where(left, turned[pl.ds(at - 1, ROWS), :], turned[pl.ds(at + 1, ROWS), :])
-        total = turned[pl.ds(at, ROWS), :] + across
-        along = jnp.where(upper, pltpu.roll(mid, LANES - 1, 1), 0.0)
-        along += jnp.where(lower, pltpu.roll(mid, 1, 1), 0.0)
-        total += along + (held[plane, tile, :] + held[plane + 2, tile, :])
-        return total * (1.0 / 6.0) + source[plane, tile, :]
-
-    def sweep(held, turned, to, to_turned):
+    blank = jnp.zeros((ROWS, LANES), jnp.float32)
+
+    def relaxed(src, plane):
+        mid = [src[plane + 1, c * ROWS : (c + 1) * ROWS, :] for c in range(RING)]
+        turned = [pltpu.roll(value, half, 1) for value in mid]
+        down = [blank] + [pltpu.roll(value, 1, 0) for value in turned]
+        up = [pltpu.roll(value, ROWS - 1, 0) for value in turned] + [blank]
+        for c in range(RING):
+            tile = slice(c * ROWS, (c + 1) * ROWS)
+            before = jnp.where(first, down[c], down[c + 1])
+            after = jnp.where(last, up[c + 1], up[c])
+            total = turned[c] + jnp.where(left, before, after)
+            total += pltpu.roll(mid[c], LANES - 1, 1) * upper
+            total += pltpu.roll(mid[c], 1, 1) * lower
+            total += src[plane, tile, :] + src[plane + 2, tile, :]
+            yield tile, total * (1.0 / 6.0) + source[plane, tile, :]
+
+    def sweep(src, dst):
         def some(n, carry):
-            for k in range(UNROLL):
-                for c in range(RING):
-                    keep(to, to_turned, n * UNROLL + k, c, relaxed(held, turned, n * UNROLL + k, c))
+            for k in range(SPAN):
+                plane = n * SPAN + k
+                for tile, value in relaxed(src, plane):
+                    dst[plane + 1, tile, :] = value
             return carry
 
-        lax.fori_loop(0, COARSE // UNROLL, some, 0)
-
-    sweep(even, even_turned, uneven, uneven_turned)
-    sweep(uneven, uneven_turned, even, even_turned)
+        lax.fori_loop(0, COARSE // SPAN, some, 0)
+
+    sweep(even, uneven)
+    sweep(uneven, even)
     copies = []
     for group in range(COARSE // ROWS):
         for k in range(ROWS):
             plane = group * ROWS + k
-            for c in range(RING):
-                at = plane * wide + c * ROWS
-                flat[at : at + ROWS, :] = relaxed(even, even_turned, plane, c)
+            for tile, value in relaxed(even, plane):
+                flat[plane * wide + tile.start : plane * wide + tile.stop, :] = value
         rows = slice(group * ROWS, (group + 1) * ROWS)
         for r in range(wide):
             value = flat[pl.ds(group * ROWS * wide + r, ROWS, stride=wide), :]
@@ -542,8 +543,6 @@
             pltpu.VMEM((COARSE, wide, LANES), jnp.float32),
             pltpu.VMEM((COARSE + 2, wide, LANES), jnp.float32),
             pltpu.VMEM((COARSE + 2, wide, LANES), jnp.float32),
-            pltpu.VMEM((COARSE * STRIDE + ROWS, LANES), jnp.float32),
-            pltpu.VMEM((COARSE * STRIDE + ROWS, LANES), jnp.float32),
             pltpu.VMEM((COARSE * wide, LANES), jnp.float32),
             pltpu.VMEM((COARSE, COARSE * COARSE), jnp.float32),
             dma, dma((COARSE // ROWS,)),

time: 66.7 us -> 60.1 us (0.901)
  Pallas kernels: 64.5 us -> 58 us
    pallas_call x1, Pallas kernels: 7.84 us -> 4.5 us  [finish(): pl.pallas_call(finish_kernel, out_shape=(jax.ShapeDtypeStruct(base.shape,...]
    pallas_call x1, Pallas kernels: 32 us -> 30.2 us  [spread(): pl.pallas_call(spread_kernel, out_shape=(jax.ShapeDtypeStruct((FIELDS * T...]
    pallas_call x1, Pallas kernels: 6.84 us -> 5.45 us  [spray(): pl.pallas_call(spray_kernel, out_shape=(jax.ShapeDtypeStruct(parcel_recor...]
where the time goes in v6:
time: 60.1 us; the launch traced here: 60 us
  Pallas kernels  58 us (97%)
  local copies, waits for them, and re-layouts  1.25 us (2%)
  between operations  0.72 us (1%)
    pallas_call x1, Pallas kernels, spread(): pl.pallas_call(spread_kernel, out_shape=(jax.ShapeDtypeStruct((FIELDS * T...  30.2 us
    pallas_call x1, Pallas kernels, halo(): pl.pallas_call(halo_kernel, out_shape=jax.ShapeDtypeStruct((chunks, 3 * F...  17.8 us
    pallas_call x1, Pallas kernels, spray(): pl.pallas_call(spray_kernel, out_shape=(jax.ShapeDtypeStruct(parcel_recor...  5.45 us
    pallas_call x1, Pallas kernels, finish(): pl.pallas_call(finish_kernel, out_shape=(jax.ShapeDtypeStruct(base.shape,...  4.5 us
    unnamed x12, local copies, waits for them, and re-layouts  1.25 us

profile of v6, /device:TPU:1, one launch (start us, length us, event | category | flops | bytes accessed | tf_op | source)
XLA Modules:
  0.0 60.0 jit_solution(4494888499636477344)
XLA Ops:
  0.6 0.0 copy-start.4
  0.6 0.0 copy-start.5
  0.7 0.0 copy-start
  0.7 1.2 %copy-done = f32[16,8,2048]{2,1,0:T(8,128)S(1)} copy-done((f32[16,8,2048]{2,1,0:T(8,128)S(1)}, f32[16,8,2048]{2,1,0:T(8,128)}, u32[]{:S(2)}) %copy-start) | copy-done | bytes 1048600
  1.9 0.0 copy-start.1
  1.9 0.0 copy-start.2
  1.9 0.0 copy-start.3
  1.9 17.8 %halo.1.gas_parts = bf16[80,48,256]{2,1,0:T(8,128)(2,1)S(1)} custom-call(f32[2048,128]{1,0:T(8,128)S(1)} %bitcast.11), custom_call_target="tpu_custom_call" | custom-call | tf_op jit(solution)/shard_map/halo/pallas_call | solution.py:111
  19.7 0.0 copy-done.4
  19.7 0.0 copy-done.5
  19.8 0.0 copy-done.1
  19.8 0.0 copy-done.2
  19.8 0.0 copy-done.3
  19.8 5.4 %spray.1 = (f32[5,4096]{1,0:T(8,128)}, f32[32,16,128]{2,1,0:T(8,128)S(1)}, s32[360]{0:T(512)S(1)}) custom-call(s32[4096]{0:T(1024)S(1)} %copy-done.2, s32[32]{0:T(128)S(1)} %copy-done.4, bf16[80,48,256]{2,1,0:T(8,128)(2,1)S(1)} %halo.1.gas_parts, f32[5,4096]{1,0:T(8,128)S(1)} %copy-done.3, f32[12,4096]{1,0:T(8,128)S(1)} %copy-done.1, f32[12]{0:T(128)S(1)} %copy-done.5, ...), custom_call_target="tpu_custom_call" | custom-call | tf_op jit(solution)/shard_map/spray/pallas_call | solution.py:218
  25.2 30.2 %spread.1 = (f32[2048,128]{1,0:T(8,128)S(1)}, f32[2,16,2048]{2,1,0:T(8,128)S(1)}, f32[2,4,4,8,8,128]{5,4,3,2,1,0:T(8,128)S(1)}) custom-call(s32[360]{0:T(512)S(1)} %get-tuple-element.12.table, s32[32,128]{1,0:T(8,128)S(1)} %bitcast.13, f32[32,16,128]{2,1,0:T(8,128)S(1)} %get-tuple-element.13.terms_ref), custom_call_target="tpu_custom_call" | custom-call | tf_op jit(solution)/shard_map/spread/pallas_call | solution.py:422
  55.5 4.5 %finish.1 = (f32[2048,128]{1,0:T(8,128)}, f32[64,4096]{1,0:T(8,128)}) custom-call(f32[2048,128]{1,0:T(8,128)S(1)} %get-tuple-element.14.base_ref, f32[2,16,2048]{2,1,0:T(8,128)S(1)} %get-tuple-element.15.halo_ref, f32[2,4,4,8,8,128]{5,4,3,2,1,0:T(8,128)S(1)} %get-tuple-element.16.grid_ref), custom_call_target="tpu_custom_call" | custom-call | tf_op jit(solution)/shard_map/finish/pallas_call | solution.py:533
Async XLA Ops:
  0.6 19.1 %copy-start.4 = (s32[32]{0:T(128)S(1)}, s32[32]{0:T(128)}, u32[]{:S(2)}) copy-start(s32[32]{0:T(128)} %count_at.1) | copy-start | bytes 388
  0.6 19.1 %copy-start.5 = (f32[12]{0:T(128)S(1)}, f32[12]{0:T(128)}, u32[]{:S(2)}) copy-start(f32[12]{0:T(128)} %steam_ref.1) | copy-start | bytes 148
  0.7 1.2 %copy-start = (f32[16,8,2048]{2,1,0:T(8,128)S(1)}, f32[16,8,2048]{2,1,0:T(8,128)}, u32[]{:S(2)}) copy-start(f32[16,8,2048]{2,1,0:T(8,128)} %param.6) | copy-start | bytes 3145732
  1.9 17.9 %copy-start.1 = (f32[12,4096]{1,0:T(8,128)S(1)}, f32[12,4096]{1,0:T(8,128)}, u32[]{:S(2)}) copy-start(f32[12,4096]{1,0:T(8,128)} %shares_ref.1) | copy-start | bytes 589828
  1.9 17.9 %copy-start.2 = (s32[4096]{0:T(1024)S(1)}, s32[4096]{0:T(1024)}, u32[]{:S(2)}) copy-start(s32[4096]{0:T(1024)} %cell_at.1) | copy-start | bytes 49156
  1.9 17.9 %copy-start.3 = (f32[5,4096]{1,0:T(8,128)S(1)}, f32[5,4096]{1,0:T(8,128)}, u32[]{:S(2)}) copy-start(f32[5,4096]{1,0:T(8,128)} %record_ref.1) | copy-start | bytes 245764

commit v7 on v6

--- a/solution.py
+++ b/solution.py
@@ -31,6 +31,12 @@
 STEP = 8
 PAIRS = 112
 ROOM = 120
+EDGES = 48
+LAST = 2 * ROOM
+ENDS = 3 * ROOM
+EDGE_BLOCK = 4 * ROOM
+EDGE_CHUNK = 5 * ROOM
+EDGE_ENDS = 6 * ROOM
 LAG_MINOR = 5
 LAG_MAJOR = 5
 SPAN = 16
@@ -72,7 +78,82 @@
     )
 
 
-def halo_kernel(gas_ref, parts_ref, sent, got, send_sem, recv_sem):
+def table_kernel(cell_at, table):
+    blocks = cell_at.shape[0] // BLOCK
+    chunks = (PLANES + 2) * PER_PLANE
+    inner = (PER_PLANE, (PLANES + 1) * PER_PLANE)
+    for c in range(chunks):
+        table[LAST + c] = PAIRS
+
+    def listed(b, state):
+        i, edge = state
+        first = lax.shift_right_logical(cell_at[b * BLOCK], SHIFT)
+        last = lax.shift_right_logical(cell_at[b * BLOCK + BLOCK - 1], SHIFT)
+
+        def one(c, state):
+            i, at = state
+            table[i] = b
+            table[ROOM + i] = c
+            table[LAST + c] = i
+            table[EDGE_BLOCK + at] = b
+            table[EDGE_CHUNK + at] = c
+            outer = (c < inner[0]) | (c >= inner[1])
+            return i + 1, at + jnp.where(outer, 1, 0)
+
+        i, after = lax.fori_loop(first, last + 1, one, (i, edge))
+        table[ENDS + b] = i - 1
+        table[EDGE_ENDS + b] = jnp.where(after > edge, after - 1, EDGES)
+        return i, after
+
+    pairs, edges = lax.fori_loop(0, blocks, listed, (0, 0))
+
+    def blank(start):
+        def one(i, carry):
+            table[start + i] = 0
+            table[start + ROOM + i] = -1
+            return carry
+
+        return one
+
+    lax.fori_loop(pairs, PAIRS, blank(0), 0)
+    lax.fori_loop(edges, EDGES, blank(EDGE_BLOCK), 0)
+
+
+def tables(fine_cell):
+    smem = pl.BlockSpec(memory_space=pltpu.SMEM)
+    return pl.pallas_call(
+        table_kernel,
+        out_shape=jax.ShapeDtypeStruct((7 * ROOM,), jnp.int32),
+        in_specs=[smem],
+        out_specs=smem,
+        name="tables",
+    )(fine_cell)
+
+
+def gather(table, start, steps, unroll, cell_ref, held, slots):
+    row = chunk_rows()
+
+    def step(n, carry):
+        total, before = carry
+        for k in range(unroll):
+            i = n * unroll + k
+            b = table[start + i]
+            c = table[start + ROOM + i]
+            part = jnp.dot(
+                held(jnp.maximum(c, 0)), chosen(row, cell_ref[pl.ds(b, 1), :], c),
+                preferred_element_type=jnp.float32,
+            )
+            total = joined(part) + total * jnp.where(b == before, 1.0, 0.0)
+            slots[i] = total
+            before = b
+        return total, before
+
+    none = jnp.zeros((FIELDS, BLOCK), jnp.float32)
+    lax.fori_loop(0, steps // unroll, step, (none, -1))
+    slots[steps] = none
+
+
+def halo_kernel(table, cell_ref, gas_ref, inner_ref, outer_ref, parts_ref, sent, got, send_sem, recv_sem):
     slabs = 2 * RING * LINE
     slab = lax.axis_index("slab")
     cross = lax.axis_index("cross")
@@ -96,24 +177,35 @@
         for q in range(PER_PLANE):
             value = [gas_ref[plane_rows(q * group + t, p), :] for t in range(group)]
             parts_ref[(p + 1) * PER_PLANE + q] = parts_of(jnp.concatenate(value, axis=1))
-    for side, plane in ((0, 0), (1, PLANES + 1)):
+    none = jnp.zeros(parts_ref.shape[1:], jnp.bfloat16)
+    for q in range(PER_PLANE):
+        parts_ref[q] = none
+        parts_ref[(PLANES + 1) * PER_PLANE + q] = none
+    gather(table, 0, PAIRS, UNROLL, cell_ref, lambda c: parts_ref[c], inner_ref)
+    for side in (0, 1):
         send(sent.at[0], got.at[side], send_sem.at[0], recv_sem.at[side], above).wait_recv()
         for q in range(PER_PLANE):
-            parts_ref[plane * PER_PLANE + q] = parts_of(got[side, :, q * CHUNK : (q + 1) * CHUNK])
+            outer_ref[side * PER_PLANE + q] = parts_of(got[side, :, q * CHUNK : (q + 1) * CHUNK])
     for each in copies:
         each.wait_send()
 
 
-def halo(gas_rows):
+def halo(table, cells, gas_rows):
     vmem = pl.BlockSpec(memory_space=pltpu.VMEM)
+    smem = pl.BlockSpec(memory_space=pltpu.SMEM)
     dma = pltpu.SemaphoreType.DMA
     chunks = (PLANES + 2) * PER_PLANE
+    parts = (3 * FIELDS, CHUNK)
     return pl.pallas_call(
         halo_kernel,
-        out_shape=jax.ShapeDtypeStruct((chunks, 3 * FIELDS, CHUNK), jnp.bfloat16),
-        in_specs=[vmem],
-        out_specs=vmem,
+        out_shape=(
+            jax.ShapeDtypeStruct((PAIRS + 1, FIELDS, BLOCK), jnp.float32),
+            jax.ShapeDtypeStruct((2 * PER_PLANE,) + parts, jnp.bfloat16),
+        ),
+        in_specs=[smem, vmem, vmem],
+        out_specs=(vmem, vmem),
         scratch_shapes=[
+            pltpu.VMEM((chunks,) + parts, jnp.bfloat16),
             pltpu.VMEM((2, FIELDS, TILES * LANES), jnp.float32),
             pltpu.VMEM((2, FIELDS, TILES * LANES), jnp.float32),
             dma((2,)), dma((2,)),
@@ -122,56 +214,15 @@
             collective_id=1, has_side_effects=True, vmem_limit_bytes=16 << 20
         ),
         name="halo",
-    )(gas_rows)
-
-
-def spray_kernel(
-    cell_at, count_at, gas_parts, record_ref, shares_ref, steam_ref, cell_ref, next_ref, terms,
-    table, gathered,
-):
+    )(table, cells, gas_rows)
+
+
+def advance(table, count_at, steam_ref, inner_ref, outer_ref, record_ref, shares_ref, cell_ref, next_ref, terms, slots):
+    def held(c):
+        return outer_ref[jnp.where(c < PER_PLANE, c, jnp.maximum(c - PLANES * PER_PLANE, 0))]
+
     blocks = cell_ref.shape[0]
-    chunks = (PLANES + 2) * PER_PLANE
-
-    def listed(b, i):
-        first = lax.shift_right_logical(cell_at[b * BLOCK], SHIFT)
-        last = lax.shift_right_logical(cell_at[b * BLOCK + BLOCK - 1], SHIFT)
-
-        def one(j, i):
-            table[i] = b
-            table[ROOM + i] = j
-            table[2 * ROOM + j] = i
-            return i + 1
-
-        return lax.fori_loop(first, last + 1, one, i)
-
-    for c in range(chunks):
-        table[2 * ROOM + c] = PAIRS
-    pairs = lax.fori_loop(0, blocks, listed, 0)
-
-    def blank(i, carry):
-        table[i] = 0
-        table[ROOM + i] = -1
-        return carry
-
-    lax.fori_loop(pairs, PAIRS, blank, 0)
-    rounds = lax.div(pairs + UNROLL - 1, UNROLL)
-
-    gathered[...] = jnp.zeros(gathered.shape, jnp.float32)
-    row = chunk_rows()
-
-    def picked(i):
-        return chosen(row, cell_ref[pl.ds(table[i], 1), :], table[ROOM + i])
-
-    def gather(n, carry):
-        for k in range(UNROLL):
-            i = n * UNROLL + k
-            held = gas_parts[jnp.maximum(table[ROOM + i], 0)]
-            part = jnp.dot(held, picked(i), preferred_element_type=jnp.float32)
-            gathered[table[i]] += joined(part)
-        return carry
-
-    lax.fori_loop(0, rounds, gather, 0)
-
+    gather(table, EDGE_BLOCK, EDGES, UNROLL, cell_ref, held, slots)
     lane = lax.broadcasted_iota(jnp.int32, (1, BLOCK), 1)
     species = lax.broadcasted_iota(jnp.int32, (steam_ref.shape[0], BLOCK), 0)
     steam = jnp.zeros(species.shape, jnp.float32)
@@ -182,7 +233,7 @@
         for k in range(STEP):
             b = n * STEP + k
             cols = pl.ds(pl.multiple_of(b * BLOCK, BLOCK), BLOCK)
-            gas = gathered[b]
+            gas = inner_ref[table[ENDS + b]] + slots[table[EDGE_ENDS + b]]
             record = record_ref[:, cols]
             alive = lane < count_at[b]
             gas_velocity, gas_heat, vapour = gas[0:3], gas[3:4], gas[4:]
@@ -211,30 +262,6 @@
     lax.fori_loop(0, blocks // STEP, step, 0)
 
 
-def spray(gas_parts, parcel_record, condensed_shares, surface_steam_factor, fine_cell, block_counts):
-    blocks = block_counts.shape[0]
-    vmem = pl.BlockSpec(memory_space=pltpu.VMEM)
-    smem = pl.BlockSpec(memory_space=pltpu.SMEM)
-    return pl.pallas_call(
-        spray_kernel,
-        out_shape=(
-            jax.ShapeDtypeStruct(parcel_record.shape, jnp.float32),
-            jax.ShapeDtypeStruct((blocks, FIELDS, BLOCK), jnp.float32),
-            jax.ShapeDtypeStruct((3 * ROOM,), jnp.int32),
-        ),
-        in_specs=[smem, smem] + [vmem] * 3 + [smem, vmem],
-        out_specs=(vmem, vmem, smem),
-        scratch_shapes=[
-            pltpu.VMEM((blocks, FIELDS, BLOCK), jnp.float32),
-        ],
-        compiler_params=pltpu.CompilerParams(vmem_limit_bytes=16 << 20),
-        name="spray",
-    )(
-        fine_cell, block_counts, gas_parts, parcel_record, condensed_shares,
-        surface_steam_factor, fine_cell.reshape(blocks, BLOCK),
-    )
-
-
 def scatter(table, cell_ref, terms_ref, base_ref, edge, slots):
     row = chunk_rows()
 
@@ -287,7 +314,8 @@
 
 
 def spread_kernel(
-    table, cell_ref, terms_ref, base_ref, halo_ref, grid_ref, own_ref, outer_ref, edge_ref, slots, got,
+    table, count_at, steam_ref, inner_ref, parts_ref, record_ref, shares_ref, cell_ref,
+    next_ref, base_ref, halo_ref, grid_ref, own_ref, outer_ref, edge_ref, terms, edge_slots, slots, got,
     pair_send, pair_recv, edge_send, edge_recv, line_send, line_recv,
     minor_send, minor_recv, major_send, major_recv, core_send, core_recv,
 ):
@@ -338,7 +366,11 @@
     sources += [other_core]
     for device in sources:
         pl.semaphore_signal(barrier, inc=1, device_id=device, device_id_type=pl.DeviceIdType.MESH)
-    own, low_tile, high_tile = scatter(table, cell_ref, terms_ref, base_ref, edge_ref, slots)
+    advance(
+        table, count_at, steam_ref, inner_ref, parts_ref, record_ref, shares_ref, cell_ref,
+        next_ref, terms, edge_slots,
+    )
+    own, low_tile, high_tile = scatter(table, cell_ref, terms, base_ref, edge_ref, slots)
     own_ref[...] = own + jnp.where(odd == 1, low_tile, high_tile)
     outer_ref[...] = jnp.where(odd == 1, high_tile, low_tile)
     pl.semaphore_wait(barrier, len(sources))
@@ -414,7 +446,7 @@
         each.wait_send()
 
 
-def spread(table, cells, terms):
+def spread(table, block_counts, steam, inner, parts, record, shares, cells):
     dma = pltpu.SemaphoreType.DMA
     vmem = pl.BlockSpec(memory_space=pltpu.VMEM)
     smem = pl.BlockSpec(memory_space=pltpu.SMEM)
@@ -422,16 +454,19 @@
     return pl.pallas_call(
         spread_kernel,
         out_shape=(
+            jax.ShapeDtypeStruct(record.shape, jnp.float32),
             jax.ShapeDtypeStruct((FIELDS * TILES * PLANES, LANES), jnp.float32),
             jax.ShapeDtypeStruct(side, jnp.float32),
             jax.ShapeDtypeStruct((2, RING, RING, LINE // 2, ROWS, LANES), jnp.float32),
         ),
-        in_specs=[smem, vmem, vmem],
-        out_specs=(vmem, vmem, vmem),
+        in_specs=[smem] * 3 + [vmem] * 5,
+        out_specs=(vmem,) * 4,
         scratch_shapes=[
             pltpu.VMEM((ROWS, LANES), jnp.float32),
             pltpu.VMEM((ROWS, LANES), jnp.float32),
             pltpu.VMEM(side, jnp.float32),
+            pltpu.VMEM((cells.shape[0], FIELDS, BLOCK), jnp.float32),
+            pltpu.VMEM((EDGES + 1, FIELDS, BLOCK), jnp.float32),
             pltpu.VMEM((PAIRS + 1, FIELDS, CHUNK), jnp.float32),
             pltpu.VMEM((3, ROWS, LANES), jnp.float32),
             dma((3,)), dma((3,)), dma((2,)), dma((2,)), dma((7,)), dma((LINE // 2,)),
@@ -441,10 +476,11 @@
             collective_id=0, has_side_effects=True, vmem_limit_bytes=16 << 20
         ),
         name="spread",
-    )(table, cells, terms)
-
-
-def finish_kernel(base_ref, halo_ref, grid_ref, fine_ref, out_ref, fine, source, even, uneven, flat, result, fine_sem, out_sem):
+    )(table, block_counts, steam, inner, parts, record, shares, cells)
+
+
+def finish_kernel(moved_ref, base_ref, halo_ref, grid_ref, next_ref, fine_ref, out_ref, fine, source, even, uneven, flat, result, fine_sem, out_sem):
+    next_ref[...] = moved_ref[...]
     sub = lax.broadcasted_iota(jnp.int32, (ROWS, LANES), 0)
     lane = lax.broadcasted_iota(jnp.int32, (ROWS, LANES), 1)
     first = sub == 0
@@ -525,7 +561,7 @@
     fine_copy.wait()
 
 
-def finish(base, halo_sum, grid):
+def finish(moved, base, halo_sum, grid):
     wide = COARSE // 2
     vmem = pl.BlockSpec(memory_space=pltpu.VMEM)
     hbm = pl.BlockSpec(memory_space=pl.ANY)
@@ -533,11 +569,12 @@
     return pl.pallas_call(
         finish_kernel,
         out_shape=(
+            jax.ShapeDtypeStruct(moved.shape, jnp.float32),
             jax.ShapeDtypeStruct(base.shape, jnp.float32),
             jax.ShapeDtypeStruct((COARSE, COARSE * COARSE), jnp.float32),
         ),
-        in_specs=[vmem, vmem, vmem],
-        out_specs=(hbm, hbm),
+        in_specs=[vmem] * 4,
+        out_specs=(vmem, hbm, hbm),
         scratch_shapes=[
             pltpu.VMEM(base.shape, jnp.float32),
             pltpu.VMEM((COARSE, wide, LANES), jnp.float32),
@@ -549,17 +586,18 @@
         ],
         compiler_params=pltpu.CompilerParams(vmem_limit_bytes=16 << 20),
         name="finish",
-    )(base, halo_sum, grid)
+    )(moved, base, halo_sum, grid)
 
 
 def body(gas_state, parcel_record, condensed_shares, surface_steam_factor, fine_cell, block_counts):
     rows = gas_state.reshape(FIELDS, PLANES, TILES, LANES).transpose(0, 2, 1, 3).reshape(-1, LANES)
-    parts = halo(rows)
-    parcel_next, terms, table = spray(
-        parts, parcel_record, condensed_shares, surface_steam_factor, fine_cell, block_counts
+    cells = fine_cell.reshape(-1, BLOCK)
+    table = tables(fine_cell)
+    inner, outer = halo(table, cells, rows)
+    moved, base, halo_sum, grid = spread(
+        table, block_counts, surface_steam_factor, inner, outer, parcel_record, condensed_shares, cells
     )
-    base, halo_sum, grid = spread(table, fine_cell.reshape(-1, BLOCK), terms)
-    fine_rows, correction = finish(base, halo_sum, grid)
+    parcel_next, fine_rows, correction = finish(moved, base, halo_sum, grid)
     fine_source = fine_rows.reshape(FIELDS, TILES, PLANES, LANES).transpose(0, 2, 1, 3).reshape(gas_state.shape)
     return (parcel_next, fine_source, correction)
 

time: 60.1 us -> 61.7 us (1.027)
  local copies, waits for them, and re-layouts: 1.25 us -> 2.56 us
    unnamed x12 -> x14, local copies, waits for them, and re-layouts: 1.25 us -> 2.56 us
where the time goes in v7:
time: 61.7 us; the launch traced here: 61.5 us
  Pallas kernels  58.2 us (94%)
  local copies, waits for them, and re-layouts  2.56 us (4%)
  between operations  0.71 us (1%)
    pallas_call x1, Pallas kernels, spread(): pl.pallas_call(spread_kernel, out_shape=(jax.ShapeDtypeStruct(record.shap...  31.2 us
    pallas_call x1, Pallas kernels, halo(): pl.pallas_call(halo_kernel, out_shape=(jax.ShapeDtypeStruct((PAIRS + 1, F...  18.4 us
    pallas_call x1, Pallas kernels, finish(): pl.pallas_call(finish_kernel, out_shape=(jax.ShapeDtypeStruct(moved.shape...  5.16 us
    pallas_call x1, Pallas kernels, tables(): pl.pallas_call(table_kernel, out_shape=jax.ShapeDtypeStruct((7 * ROOM,),...  3.47 us
    unnamed x14, local copies, waits for them, and re-layouts  2.56 us

profile of v7, /device:TPU:1, one launch (start us, length us, event | category | flops | bytes accessed | tf_op | source)
XLA Modules:
  0.0 61.5 jit_solution(2402314383691389095)
XLA Ops:
  0.6 0.0 copy-start.2
  0.6 3.5 %tables.1.table = s32[840]{0:T(1024)} custom-call(s32[4096]{0:T(1024)} %cell_at.1), custom_call_target="tpu_custom_call" | custom-call | tf_op jit(solution)/shard_map/tables/pallas_call | solution.py:124
  4.1 0.0 copy-done.2
  4.1 0.0 copy-start
  4.1 1.2 %copy-done = f32[16,8,2048]{2,1,0:T(8,128)S(1)} copy-done((f32[16,8,2048]{2,1,0:T(8,128)S(1)}, f32[16,8,2048]{2,1,0:T(8,128)}, u32[]{:S(2)}) %copy-start) | copy-done | bytes 1048600
  5.4 0.0 copy-start.4
  5.4 0.7 %copy-done.4 = s32[840]{0:T(1024)S(1)} copy-done((s32[840]{0:T(1024)S(1)}, s32[840]{0:T(1024)}, u32[]{:S(2)}) %copy-start.4) | copy-done | bytes 3384
  6.0 0.0 copy-start.1
  6.0 0.0 copy-start.3
  6.0 18.4 %halo.1 = (f32[113,16,128]{2,1,0:T(8,128)S(1)}, bf16[16,48,256]{2,1,0:T(8,128)(2,1)S(1)}) custom-call(s32[840]{0:T(1024)S(1)} %copy-done.4, s32[32,128]{1,0:T(8,128)S(1)} %bitcast.12, f32[2048,128]{1,0:T(8,128)S(1)} %bitcast.11), custom_call_target="tpu_custom_call" | custom-call | tf_op jit(solution)/shard_map/halo/pallas_call | solution.py:199
  24.4 0.0 copy-start.5
  24.4 0.0 copy-start.6
  24.4 0.0 copy-done.1
  24.5 0.0 copy-done.3
  24.5 0.6 copy-done.5
  25.1 0.0 copy-done.6
  25.1 31.2 %spread.1 = (f32[5,4096]{1,0:T(8,128)S(1)}, f32[2048,128]{1,0:T(8,128)S(1)}, f32[2,16,2048]{2,1,0:T(8,128)S(1)}, f32[2,4,4,8,8,128]{5,4,3,2,1,0:T(8,128)S(1)}) custom-call(s32[840]{0:T(1024)S(1)} %copy-done.4, s32[32]{0:T(128)S(1)} %copy-done.5, f32[12]{0:T(128)S(1)} %copy-done.6, f32[113,16,128]{2,1,0:T(8,128)S(1)} %get-tuple-element.12.inner_ref, ...), custom_call_target="tpu_custom_call" | custom-call | tf_op jit(solution)/shard_map/spread/pallas_call | solution.py:454
  56.3 5.2 %finish.1 = (f32[5,4096]{1,0:T(8,128)}, f32[2048,128]{1,0:T(8,128)}, f32[64,4096]{1,0:T(8,128)}) custom-call(f32[5,4096]{1,0:T(8,128)S(1)} %get-tuple-element.14.moved_ref, f32[2048,128]{1,0:T(8,128)S(1)} %get-tuple-element.15.base_ref, f32[2,16,2048]{2,1,0:T(8,128)S(1)} %get-tuple-element.16.halo_ref, f32[2,4,4,8,8,128]{5,4,3,2,1,0:T(8,128)S(1)} %get-tuple-element.17.grid_ref), custom_call_target="tpu_custom_call" | custom-call | tf_op jit(solution)/shard_map/finish/pallas_call | solution.py:569
Async XLA Ops:
  0.6 3.5 %copy-start.2 = (s32[4096]{0:T(1024)S(1)}, s32[4096]{0:T(1024)}, u32[]{:S(2)}) copy-start(s32[4096]{0:T(1024)} %cell_at.1) | copy-start | bytes 49156
  4.1 1.2 %copy-start = (f32[16,8,2048]{2,1,0:T(8,128)S(1)}, f32[16,8,2048]{2,1,0:T(8,128)}, u32[]{:S(2)}) copy-start(f32[16,8,2048]{2,1,0:T(8,128)} %param.6) | copy-start | bytes 3145732
  5.4 0.7 %copy-start.4 = (s32[840]{0:T(1024)S(1)}, s32[840]{0:T(1024)}, u32[]{:S(2)}) copy-start(s32[840]{0:T(1024)} %tables.1.table) | copy-start | bytes 10084
  6.0 18.4 %copy-start.1 = (f32[12,4096]{1,0:T(8,128)S(1)}, f32[12,4096]{1,0:T(8,128)}, u32[]{:S(2)}) copy-start(f32[12,4096]{1,0:T(8,128)} %shares_ref.1) | copy-start | bytes 589828
  6.0 18.4 %copy-start.3 = (f32[5,4096]{1,0:T(8,128)S(1)}, f32[5,4096]{1,0:T(8,128)}, u32[]{:S(2)}) copy-start(f32[5,4096]{1,0:T(8,128)} %record_ref.1) | copy-start | bytes 245764
  24.4 0.7 %copy-start.5 = (s32[32]{0:T(128)S(1)}, s32[32]{0:T(128)}, u32[]{:S(2)}) copy-start(s32[32]{0:T(128)} %count_at.1) | copy-start | bytes 388
  24.4 0.7 %copy-start.6 = (f32[12]{0:T(128)S(1)}, f32[12]{0:T(128)}, u32[]{:S(2)}) copy-start(f32[12]{0:T(128)} %steam_ref.1) | copy-start | bytes 148

commit v8 on v7

--- a/solution.py
+++ b/solution.py
@@ -30,13 +30,11 @@
 UNROLL = 16
 STEP = 8
 PAIRS = 112
-ROOM = 120
 EDGES = 48
-LAST = 2 * ROOM
-ENDS = 3 * ROOM
-EDGE_BLOCK = 4 * ROOM
-EDGE_CHUNK = 5 * ROOM
-EDGE_ENDS = 6 * ROOM
+LAST = 2
+ENDS = 3
+EDGE_BLOCK = 4
+EDGE_ENDS = 6
 LAG_MINOR = 5
 LAG_MAJOR = 5
 SPAN = 16
@@ -67,6 +65,10 @@
     return row.astype(jnp.float32).astype(jnp.bfloat16)
 
 
+def within(value, top):
+    return jnp.minimum(jnp.maximum(value, 0), top)
+
+
 def plane_rows(tile, plane):
     return pl.ds(tile * PLANES + plane, FIELDS, stride=TILES * PLANES)
 
@@ -78,56 +80,57 @@
     )
 
 
-def table_kernel(cell_at, table):
-    blocks = cell_at.shape[0] // BLOCK
+def list_pairs(cell_ref, table):
+    blocks = cell_ref.shape[0]
     chunks = (PLANES + 2) * PER_PLANE
-    inner = (PER_PLANE, (PLANES + 1) * PER_PLANE)
-    for c in range(chunks):
-        table[LAST + c] = PAIRS
-
-    def listed(b, state):
-        i, edge = state
-        first = lax.shift_right_logical(cell_at[b * BLOCK], SHIFT)
-        last = lax.shift_right_logical(cell_at[b * BLOCK + BLOCK - 1], SHIFT)
-
-        def one(c, state):
-            i, at = state
-            table[i] = b
-            table[ROOM + i] = c
-            table[LAST + c] = i
-            table[EDGE_BLOCK + at] = b
-            table[EDGE_CHUNK + at] = c
-            outer = (c < inner[0]) | (c >= inner[1])
-            return i + 1, at + jnp.where(outer, 1, 0)
-
-        i, after = lax.fori_loop(first, last + 1, one, (i, edge))
-        table[ENDS + b] = i - 1
-        table[EDGE_ENDS + b] = jnp.where(after > edge, after - 1, EDGES)
-        return i, after
-
-    pairs, edges = lax.fori_loop(0, blocks, listed, (0, 0))
-
-    def blank(start):
-        def one(i, carry):
-            table[start + i] = 0
-            table[start + ROOM + i] = -1
-            return carry
-
-        return one
-
-    lax.fori_loop(pairs, PAIRS, blank(0), 0)
-    lax.fori_loop(edges, EDGES, blank(EDGE_BLOCK), 0)
-
-
-def tables(fine_cell):
-    smem = pl.BlockSpec(memory_space=pltpu.SMEM)
-    return pl.pallas_call(
-        table_kernel,
-        out_shape=jax.ShapeDtypeStruct((7 * ROOM,), jnp.int32),
-        in_specs=[smem],
-        out_specs=smem,
-        name="tables",
-    )(fine_cell)
+    first = lax.shift_right_logical(cell_ref[:, 0:1], SHIFT).astype(jnp.float32)
+    last = lax.shift_right_logical(cell_ref[:, BLOCK - 1 : BLOCK], SHIFT).astype(jnp.float32)
+    lane = lax.broadcasted_iota(jnp.int32, (blocks, LANES), 1).astype(jnp.float32)
+    sub = lax.broadcasted_iota(jnp.int32, (blocks, LANES), 0).astype(jnp.float32)
+    spot = lane[0:1]
+
+    def over_blocks(value):
+        return jnp.sum(value, axis=0, keepdims=True)
+
+    def as_row(column):
+        return over_blocks(jnp.where(sub == lane, column, 0.0))
+
+    def starts(column):
+        return jnp.sum(jnp.where(lane < sub, as_row(column), 0.0), axis=1, keepdims=True)
+
+    def owner(start):
+        return over_blocks(jnp.where(start <= lane, 1.0, 0.0)) - 1.0
+
+    def at(block, column):
+        return over_blocks(jnp.where(sub == block, column, 0.0))
+
+    def put(row, value, low, high):
+        table[row : row + 1, :] = jnp.clip(value.astype(jnp.int32), low, high)
+
+    count = last - first + 1.0
+    start = starts(count)
+    block = owner(start)
+    real = spot < over_blocks(count)
+    put(0, jnp.where(real, block, 0.0), 0, blocks - 1)
+    put(1, jnp.where(real, spot + at(block, first - start), -1.0), -1, chunks - 1)
+    deep = owner(first)
+    held = (deep >= 0.0) & (at(deep, last) >= spot)
+    put(LAST, jnp.where(held, spot + at(deep, start - first), float(PAIRS)), 0, PAIRS)
+    put(ENDS, as_row(start + count - 1.0), 0, PAIRS)
+
+    top = float((PLANES + 1) * PER_PLANE)
+    low = jnp.maximum(jnp.minimum(last, PER_PLANE - 1.0) - first + 1.0, 0.0)
+    from_high = jnp.maximum(first, top)
+    edges = low + jnp.maximum(last - from_high + 1.0, 0.0)
+    start = starts(edges)
+    block = owner(start)
+    real = spot < over_blocks(edges)
+    inside = spot - at(block, start)
+    kept = at(block, low)
+    chunk = jnp.where(inside < kept, at(block, first) + inside, at(block, from_high) + inside - kept)
+    put(EDGE_BLOCK, jnp.where(real, block, 0.0), 0, blocks - 1)
+    put(EDGE_BLOCK + 1, jnp.where(real, chunk, -1.0), -1, chunks - 1)
+    put(EDGE_ENDS, as_row(jnp.where(edges > 0.0, start + edges - 1.0, float(EDGES))), 0, EDGES)
 
 
 def gather(table, start, steps, unroll, cell_ref, held, slots):
@@ -137,10 +140,10 @@
         total, before = carry
         for k in range(unroll):
             i = n * unroll + k
-            b = table[start + i]
-            c = table[start + ROOM + i]
+            b = within(table[start, i], cell_ref.shape[0] - 1)
+            c = table[start + 1, i]
             part = jnp.dot(
-                held(jnp.maximum(c, 0)), chosen(row, cell_ref[pl.ds(b, 1), :], c),
+                held(within(c, (PLANES + 2) * PER_PLANE - 1)), chosen(row, cell_ref[pl.ds(b, 1), :], c),
                 preferred_element_type=jnp.float32,
             )
             total = joined(part) + total * jnp.where(b == before, 1.0, 0.0)
@@ -153,7 +156,9 @@
     slots[steps] = none
 
 
-def halo_kernel(table, cell_ref, gas_ref, inner_ref, outer_ref, parts_ref, sent, got, send_sem, recv_sem):
+def halo_kernel(
+    cell_ref, gas_ref, inner_ref, outer_ref, table_ref, parts_ref, sent, got, table, table_sem, send_sem, recv_sem
+):
     slabs = 2 * RING * LINE
     slab = lax.axis_index("slab")
     cross = lax.axis_index("cross")
@@ -162,16 +167,20 @@
     barrier = pltpu.get_barrier_semaphore()
     for device in (below, above):
         pl.semaphore_signal(barrier, inc=1, device_id=device, device_id_type=pl.DeviceIdType.MESH)
+    list_pairs(cell_ref, table_ref)
+    table_ref[ROWS - 1 :, :] = jnp.zeros((1, LANES), jnp.int32)
     for side, plane in ((0, 0), (1, PLANES - 1)):
         for t in range(TILES):
             sent[side, :, t * LANES : (t + 1) * LANES] = gas_ref[plane_rows(t, plane), :]
     pl.semaphore_wait(barrier, 2)
+    table_copy = pltpu.make_async_copy(table_ref, table, table_sem)
     copies = [
         send(sent.at[0], got.at[1], send_sem.at[0], recv_sem.at[1], below),
         send(sent.at[1], got.at[0], send_sem.at[1], recv_sem.at[0], above),
     ]
     for each in copies:
         each.start()
+    table_copy.start()
     group = CHUNK // LANES
     for p in range(PLANES):
         for q in range(PER_PLANE):
@@ -181,6 +190,7 @@
     for q in range(PER_PLANE):
         parts_ref[q] = none
         parts_ref[(PLANES + 1) * PER_PLANE + q] = none
+    table_copy.wait()
     gather(table, 0, PAIRS, UNROLL, cell_ref, lambda c: parts_ref[c], inner_ref)
     for side in (0, 1):
         send(sent.at[0], got.at[side], send_sem.at[0], recv_sem.at[side], above).wait_recv()
@@ -190,9 +200,8 @@
         each.wait_send()
 
 
-def halo(table, cells, gas_rows):
+def halo(cells, gas_rows):
     vmem = pl.BlockSpec(memory_space=pltpu.VMEM)
-    smem = pl.BlockSpec(memory_space=pltpu.SMEM)
     dma = pltpu.SemaphoreType.DMA
     chunks = (PLANES + 2) * PER_PLANE
     parts = (3 * FIELDS, CHUNK)
@@ -201,25 +210,27 @@
         out_shape=(
             jax.ShapeDtypeStruct((PAIRS + 1, FIELDS, BLOCK), jnp.float32),
             jax.ShapeDtypeStruct((2 * PER_PLANE,) + parts, jnp.bfloat16),
+            jax.ShapeDtypeStruct((ROWS, LANES), jnp.int32),
         ),
-        in_specs=[smem, vmem, vmem],
-        out_specs=(vmem, vmem),
+        in_specs=[vmem, vmem],
+        out_specs=(vmem, vmem, vmem),
         scratch_shapes=[
             pltpu.VMEM((chunks,) + parts, jnp.bfloat16),
             pltpu.VMEM((2, FIELDS, TILES * LANES), jnp.float32),
             pltpu.VMEM((2, FIELDS, TILES * LANES), jnp.float32),
-            dma((2,)), dma((2,)),
+            pltpu.SMEM((ROWS, LANES), jnp.int32),
+            dma, dma((2,)), dma((2,)),
         ],
         compiler_params=pltpu.CompilerParams(
             collective_id=1, has_side_effects=True, vmem_limit_bytes=16 << 20
         ),
         name="halo",
-    )(table, cells, gas_rows)
+    )(cells, gas_rows)
 
 
 def advance(table, count_at, steam_ref, inner_ref, outer_ref, record_ref, shares_ref, cell_ref, next_ref, terms, slots):
     def held(c):
-        return outer_ref[jnp.where(c < PER_PLANE, c, jnp.maximum(c - PLANES * PER_PLANE, 0))]
+        return outer_ref[within(jnp.where(c < PER_PLANE, c, c - PLANES * PER_PLANE), 2 * PER_PLANE - 1)]
 
     blocks = cell_ref.shape[0]
     gather(table, EDGE_BLOCK, EDGES, UNROLL, cell_ref, held, slots)
@@ -233,7 +244,7 @@
         for k in range(STEP):
             b = n * STEP + k
             cols = pl.ds(pl.multiple_of(b * BLOCK, BLOCK), BLOCK)
-            gas = inner_ref[table[ENDS + b]] + slots[table[EDGE_ENDS + b]]
+            gas = inner_ref[within(table[ENDS, b], PAIRS)] + slots[within(table[EDGE_ENDS, b], EDGES)]
             record = record_ref[:, cols]
             alive = lane < count_at[b]
             gas_velocity, gas_heat, vapour = gas[0:3], gas[3:4], gas[4:]
@@ -269,8 +280,8 @@
         total, before = carry
         for k in range(UNROLL):
             i = n * UNROLL + k
-            b = table[i]
-            c = table[ROOM + i]
+            b = within(table[0, i], cell_ref.shape[0] - 1)
+            c = table[1, i]
             picked = chosen(row, cell_ref[pl.ds(b, 1), :], c)
             part = lax.dot_general(
                 parts_of(terms_ref[b]), picked, (((1,), (1,)), ((), ())),
@@ -297,13 +308,13 @@
     group = CHUNK // LANES
     for q in range(PER_PLANE):
         cols = slice(q * CHUNK, (q + 1) * CHUNK)
-        below = slots[table[2 * ROOM + q]]
-        above = slots[table[2 * ROOM + (PLANES + 1) * PER_PLANE + q]]
+        below = slots[within(table[LAST, q], PAIRS)]
+        above = slots[within(table[LAST, (PLANES + 1) * PER_PLANE + q], PAIRS)]
         edge[0, :, cols] = below
         edge[1, :, cols] = above
         inside = None
         for p in range(PLANES):
-            value = slots[table[2 * ROOM + (p + 1) * PER_PLANE + q]]
+            value = slots[within(table[LAST, (p + 1) * PER_PLANE + q], PAIRS)]
             for t in range(group):
                 base_ref[plane_rows(q * group + t, p), :] = value[:, t * LANES : (t + 1) * LANES]
             inside = value if inside is None else inside + value
@@ -592,8 +603,7 @@
 def body(gas_state, parcel_record, condensed_shares, surface_steam_factor, fine_cell, block_counts):
     rows = gas_state.reshape(FIELDS, PLANES, TILES, LANES).transpose(0, 2, 1, 3).reshape(-1, LANES)
     cells = fine_cell.reshape(-1, BLOCK)
-    table = tables(fine_cell)
-    inner, outer = halo(table, cells, rows)
+    inner, outer, table = halo(cells, rows)
     moved, base, halo_sum, grid = spread(
         table, block_counts, surface_steam_factor, inner, outer, parcel_record, condensed_shares, cells
     )

time: 61.7 us -> 57.7 us (0.935)
  Pallas kernels: 58.2 us -> 54.1 us
    pallas_call x1 -> x0, Pallas kernels: 3.47 us -> none  [tables(): pl.pallas_call(table_kernel, out_shape=jax.ShapeDtypeStruct((7 * ROOM,),...]
    unnamed x14 -> x12, local copies, waits for them, and re-layouts: 2.56 us -> 2.58 us
where the time goes in v8:
time: 57.7 us; the launch traced here: 57.4 us
  Pallas kernels  54.1 us (94%)
  local copies, waits for them, and re-layouts  2.58 us (4%)
  between operations  0.69 us (1%)
    pallas_call x1, Pallas kernels, spread(): pl.pallas_call(spread_kernel, out_shape=(jax.ShapeDtypeStruct(record.shap...  31.1 us
    pallas_call x1, Pallas kernels, halo(): pl.pallas_call(halo_kernel, out_shape=(jax.ShapeDtypeStruct((PAIRS + 1, F...  17.8 us
    pallas_call x1, Pallas kernels, finish(): pl.pallas_call(finish_kernel, out_shape=(jax.ShapeDtypeStruct(moved.shape...  5.16 us
    unnamed x12, local copies, waits for them, and re-layouts  2.58 us

profile of v8, /device:TPU:1, one launch (start us, length us, event | category | flops | bytes accessed | tf_op | source)
XLA Modules:
  0.0 57.4 jit_solution(12713483198361128319)
XLA Ops:
  0.6 0.0 copy-start
  0.6 1.2 %copy-done = f32[16,8,2048]{2,1,0:T(8,128)S(1)} copy-done((f32[16,8,2048]{2,1,0:T(8,128)S(1)}, f32[16,8,2048]{2,1,0:T(8,128)}, u32[]{:S(2)}) %copy-start) | copy-done | bytes 1048600
  1.9 0.0 copy-start.3
  1.9 0.7 %copy-done.3 = s32[4096]{0:T(1024)S(1)} copy-done((s32[4096]{0:T(1024)S(1)}, s32[4096]{0:T(1024)}, u32[]{:S(2)}) %copy-start.3) | copy-done | bytes 16408
  2.6 0.0 copy-start.1
  2.6 0.0 copy-start.2
  2.6 17.8 %halo.1 = (f32[113,16,128]{2,1,0:T(8,128)S(1)}, bf16[16,48,256]{2,1,0:T(8,128)(2,1)S(1)}, s32[8,128]{1,0:T(8,128)S(1)}) custom-call(s32[32,128]{1,0:T(8,128)S(1)} %bitcast.12, f32[2048,128]{1,0:T(8,128)S(1)} %bitcast.11), custom_call_target="tpu_custom_call" | custom-call | tf_op jit(solution)/shard_map/halo/pallas_call | solution.py:208
  20.4 0.0 copy-start.4
  20.4 0.0 copy-start.5
  20.4 0.0 copy-done.1
  20.5 0.0 copy-done.2
  20.5 0.6 %copy-done.4 = s32[32]{0:T(128)S(1)} copy-done((s32[32]{0:T(128)S(1)}, s32[32]{0:T(128)}, u32[]{:S(2)}) %copy-start.4) | copy-done | bytes 152
  21.1 0.0 copy-done.5
  21.1 31.1 %spread.1 = (f32[5,4096]{1,0:T(8,128)S(1)}, f32[2048,128]{1,0:T(8,128)S(1)}, f32[2,16,2048]{2,1,0:T(8,128)S(1)}, f32[2,4,4,8,8,128]{5,4,3,2,1,0:T(8,128)S(1)}) custom-call(s32[8,128]{1,0:T(8,128)S(1)} %get-tuple-element.13.table, s32[32]{0:T(128)S(1)} %copy-done.4, f32[12]{0:T(128)S(1)} %copy-done.5, f32[113,16,128]{2,1,0:T(8,128)S(1)} %get-tuple-element.14.inner_ref, ...), custom_call_target="tpu_custom_call" | custom-call | tf_op jit(solution)/shard_map/spread/pallas_call | solution.py:465
  52.3 5.2 %finish.1 = (f32[5,4096]{1,0:T(8,128)}, f32[2048,128]{1,0:T(8,128)}, f32[64,4096]{1,0:T(8,128)}) custom-call(f32[5,4096]{1,0:T(8,128)S(1)} %get-tuple-element.16.moved_ref, f32[2048,128]{1,0:T(8,128)S(1)} %get-tuple-element.17.base_ref, f32[2,16,2048]{2,1,0:T(8,128)S(1)} %get-tuple-element.18.halo_ref, f32[2,4,4,8,8,128]{5,4,3,2,1,0:T(8,128)S(1)} %get-tuple-element.19.grid_ref), custom_call_target="tpu_custom_call" | custom-call | tf_op jit(solution)/shard_map/finish/pallas_call | solution.py:580
Async XLA Ops:
  0.6 1.2 %copy-start = (f32[16,8,2048]{2,1,0:T(8,128)S(1)}, f32[16,8,2048]{2,1,0:T(8,128)}, u32[]{:S(2)}) copy-start(f32[16,8,2048]{2,1,0:T(8,128)} %param.6) | copy-start | bytes 3145732
  1.9 0.7 %copy-start.3 = (s32[4096]{0:T(1024)S(1)}, s32[4096]{0:T(1024)}, u32[]{:S(2)}) copy-start(s32[4096]{0:T(1024)} %param.10) | copy-start | bytes 49156
  2.6 17.9 %copy-start.1 = (f32[12,4096]{1,0:T(8,128)S(1)}, f32[12,4096]{1,0:T(8,128)}, u32[]{:S(2)}) copy-start(f32[12,4096]{1,0:T(8,128)} %shares_ref.1) | copy-start | bytes 589828
  2.6 17.9 %copy-start.2 = (f32[5,4096]{1,0:T(8,128)S(1)}, f32[5,4096]{1,0:T(8,128)}, u32[]{:S(2)}) copy-start(f32[5,4096]{1,0:T(8,128)} %record_ref.1) | copy-start | bytes 245764
  20.4 0.7 %copy-start.4 = (s32[32]{0:T(128)S(1)}, s32[32]{0:T(128)}, u32[]{:S(2)}) copy-start(s32[32]{0:T(128)} %count_at.1) | copy-start | bytes 388
  20.4 0.7 %copy-start.5 = (f32[12]{0:T(128)S(1)}, f32[12]{0:T(128)}, u32[]{:S(2)}) copy-start(f32[12]{0:T(128)} %steam_ref.1) | copy-start | bytes 148

commit v9 on v8

--- a/solution.py
+++ b/solution.py
@@ -273,7 +273,7 @@
     lax.fori_loop(0, blocks // STEP, step, 0)
 
 
-def scatter(table, cell_ref, terms_ref, base_ref, edge, slots):
+def scatter(table, cell_ref, terms_ref, edge, slots):
     row = chunk_rows()
 
     def step(n, carry):
@@ -305,7 +305,6 @@
         return [joined(jnp.dot(parts_of(kept), fold, preferred_element_type=jnp.float32))]
 
     own, low, high = [], [], []
-    group = CHUNK // LANES
     for q in range(PER_PLANE):
         cols = slice(q * CHUNK, (q + 1) * CHUNK)
         below = slots[within(table[LAST, q], PAIRS)]
@@ -315,13 +314,20 @@
         inside = None
         for p in range(PLANES):
             value = slots[within(table[LAST, (p + 1) * PER_PLANE + q], PAIRS)]
-            for t in range(group):
-                base_ref[plane_rows(q * group + t, p), :] = value[:, t * LANES : (t + 1) * LANES]
             inside = value if inside is None else inside + value
         own += mass(inside)
         low += mass(below)
         high += mass(above)
     return tuple(0.25 * jnp.concatenate(rows, axis=0) for rows in (own, low, high))
+
+
+def place_rows(table, slots, base_ref):
+    group = CHUNK // LANES
+    for q in range(PER_PLANE):
+        for p in range(PLANES):
+            value = slots[within(table[LAST, (p + 1) * PER_PLANE + q], PAIRS)]
+            for t in range(group):
+                base_ref[plane_rows(q * group + t, p), :] = value[:, t * LANES : (t + 1) * LANES]
 
 
 def spread_kernel(
@@ -381,7 +387,7 @@
         table, count_at, steam_ref, inner_ref, parts_ref, record_ref, shares_ref, cell_ref,
         next_ref, terms, edge_slots,
     )
-    own, low_tile, high_tile = scatter(table, cell_ref, terms, base_ref, edge_ref, slots)
+    own, low_tile, high_tile = scatter(table, cell_ref, terms, edge_ref, slots)
     own_ref[...] = own + jnp.where(odd == 1, low_tile, high_tile)
     outer_ref[...] = jnp.where(odd == 1, high_tile, low_tile)
     pl.semaphore_wait(barrier, len(sources))
@@ -443,6 +449,7 @@
         if step == 0:
             for each in edges:
                 each.start()
+            place_rows(table, slots, base_ref)
         if 0 <= step - LAG_MINOR < 8:
             to_majors(step - LAG_MINOR)
         if 0 <= step - LAG_MINOR - LAG_MAJOR < 8:
@@ -490,8 +497,9 @@
     )(table, block_counts, steam, inner, parts, record, shares, cells)
 
 
-def finish_kernel(moved_ref, base_ref, halo_ref, grid_ref, next_ref, fine_ref, out_ref, fine, source, even, uneven, flat, result, fine_sem, out_sem):
-    next_ref[...] = moved_ref[...]
+def finish_kernel(moved_ref, base_ref, halo_ref, grid_ref, next_ref, fine_ref, out_ref, fine, source, even, uneven, flat, result, next_sem, fine_sem, out_sem):
+    next_copy = pltpu.make_async_copy(moved_ref, next_ref, next_sem)
+    next_copy.start()
     sub = lax.broadcasted_iota(jnp.int32, (ROWS, LANES), 0)
     lane = lax.broadcasted_iota(jnp.int32, (ROWS, LANES), 1)
     first = sub == 0
@@ -570,6 +578,7 @@
     for each in copies:
         each.wait()
     fine_copy.wait()
+    next_copy.wait()
 
 
 def finish(moved, base, halo_sum, grid):
@@ -585,7 +594,7 @@
             jax.ShapeDtypeStruct((COARSE, COARSE * COARSE), jnp.float32),
         ),
         in_specs=[vmem] * 4,
-        out_specs=(vmem, hbm, hbm),
+        out_specs=(hbm, hbm, hbm),
         scratch_shapes=[
             pltpu.VMEM(base.shape, jnp.float32),
             pltpu.VMEM((COARSE, wide, LANES), jnp.float32),
@@ -593,7 +602,7 @@
             pltpu.VMEM((COARSE + 2, wide, LANES), jnp.float32),
             pltpu.VMEM((COARSE * wide, LANES), jnp.float32),
             pltpu.VMEM((COARSE, COARSE * COARSE), jnp.float32),
-            dma, dma((COARSE // ROWS,)),
+            dma, dma, dma((COARSE // ROWS,)),
         ],
         compiler_params=pltpu.CompilerParams(vmem_limit_bytes=16 << 20),
         name="finish",

time: 57.7 us -> 56.4 us (0.977)
  Pallas kernels: 54.1 us -> 52.9 us
    pallas_call x1, Pallas kernels: 5.16 us -> 4.51 us  [finish(): pl.pallas_call(finish_kernel, out_shape=(jax.ShapeDtypeStruct(moved.shape...]
    pallas_call x1, Pallas kernels: 31.1 us -> 30.5 us  [spread(): pl.pallas_call(spread_kernel, out_shape=(jax.ShapeDtypeStruct(record.shap...]
where the time goes in v9:
time: 56.4 us; the launch traced here: 56.1 us
  Pallas kernels  52.9 us (94%)
  local copies, waits for them, and re-layouts  2.58 us (5%)
  between operations  0.69 us (1%)
    pallas_call x1, Pallas kernels, spread(): pl.pallas_call(spread_kernel, out_shape=(jax.ShapeDtypeStruct(record.shap...  30.5 us
    pallas_call x1, Pallas kernels, halo(): pl.pallas_call(halo_kernel, out_shape=(jax.ShapeDtypeStruct((PAIRS + 1, F...  17.8 us
    pallas_call x1, Pallas kernels, finish(): pl.pallas_call(finish_kernel, out_shape=(jax.ShapeDtypeStruct(moved.shape...  4.51 us
    unnamed x12, local copies, waits for them, and re-layouts  2.58 us

profile of v9, /device:TPU:1, one launch (start us, length us, event | category | flops | bytes accessed | tf_op | source)
XLA Modules:
  0.0 56.1 jit_solution(14111701780059155922)
XLA Ops:
  0.6 0.0 copy-start
  0.6 1.2 %copy-done = f32[16,8,2048]{2,1,0:T(8,128)S(1)} copy-done((f32[16,8,2048]{2,1,0:T(8,128)S(1)}, f32[16,8,2048]{2,1,0:T(8,128)}, u32[]{:S(2)}) %copy-start) | copy-done | bytes 1048600
  1.9 0.0 copy-start.3
  1.9 0.7 %copy-done.3 = s32[4096]{0:T(1024)S(1)} copy-done((s32[4096]{0:T(1024)S(1)}, s32[4096]{0:T(1024)}, u32[]{:S(2)}) %copy-start.3) | copy-done | bytes 16408
  2.6 0.0 copy-start.1
  2.6 0.0 copy-start.2
  2.6 17.8 %halo.1 = (f32[113,16,128]{2,1,0:T(8,128)S(1)}, bf16[16,48,256]{2,1,0:T(8,128)(2,1)S(1)}, s32[8,128]{1,0:T(8,128)S(1)}) custom-call(s32[32,128]{1,0:T(8,128)S(1)} %bitcast.12, f32[2048,128]{1,0:T(8,128)S(1)} %bitcast.11), custom_call_target="tpu_custom_call" | custom-call | tf_op jit(solution)/shard_map/halo/pallas_call | solution.py:208
  20.4 0.0 copy-start.4
  20.4 0.0 copy-start.5
  20.4 0.0 copy-done.1
  20.5 0.0 copy-done.2
  20.5 0.6 %copy-done.4 = s32[32]{0:T(128)S(1)} copy-done((s32[32]{0:T(128)S(1)}, s32[32]{0:T(128)}, u32[]{:S(2)}) %copy-start.4) | copy-done | bytes 152
  21.1 0.0 copy-done.5
  21.1 30.5 %spread.1 = (f32[5,4096]{1,0:T(8,128)S(1)}, f32[2048,128]{1,0:T(8,128)S(1)}, f32[2,16,2048]{2,1,0:T(8,128)S(1)}, f32[2,4,4,8,8,128]{5,4,3,2,1,0:T(8,128)S(1)}) custom-call(s32[8,128]{1,0:T(8,128)S(1)} %get-tuple-element.13.table, s32[32]{0:T(128)S(1)} %copy-done.4, f32[12]{0:T(128)S(1)} %copy-done.5, f32[113,16,128]{2,1,0:T(8,128)S(1)} %get-tuple-element.14.inner_ref, ...), custom_call_target="tpu_custom_call" | custom-call | tf_op jit(solution)/shard_map/spread/pallas_call | solution.py:472
  51.6 4.5 %finish.1 = (f32[5,4096]{1,0:T(8,128)}, f32[2048,128]{1,0:T(8,128)}, f32[64,4096]{1,0:T(8,128)}) custom-call(f32[5,4096]{1,0:T(8,128)S(1)} %get-tuple-element.16.moved_ref, f32[2048,128]{1,0:T(8,128)S(1)} %get-tuple-element.17.base_ref, f32[2,16,2048]{2,1,0:T(8,128)S(1)} %get-tuple-element.18.halo_ref, f32[2,4,4,8,8,128]{5,4,3,2,1,0:T(8,128)S(1)} %get-tuple-element.19.grid_ref), custom_call_target="tpu_custom_call" | custom-call | tf_op jit(solution)/shard_map/finish/pallas_call | solution.py:589
Async XLA Ops:
  0.6 1.2 %copy-start = (f32[16,8,2048]{2,1,0:T(8,128)S(1)}, f32[16,8,2048]{2,1,0:T(8,128)}, u32[]{:S(2)}) copy-start(f32[16,8,2048]{2,1,0:T(8,128)} %param.6) | copy-start | bytes 3145732
  1.9 0.7 %copy-start.3 = (s32[4096]{0:T(1024)S(1)}, s32[4096]{0:T(1024)}, u32[]{:S(2)}) copy-start(s32[4096]{0:T(1024)} %param.10) | copy-start | bytes 49156
  2.6 17.9 %copy-start.1 = (f32[12,4096]{1,0:T(8,128)S(1)}, f32[12,4096]{1,0:T(8,128)}, u32[]{:S(2)}) copy-start(f32[12,4096]{1,0:T(8,128)} %shares_ref.1) | copy-start | bytes 589828
  2.6 17.9 %copy-start.2 = (f32[5,4096]{1,0:T(8,128)S(1)}, f32[5,4096]{1,0:T(8,128)}, u32[]{:S(2)}) copy-start(f32[5,4096]{1,0:T(8,128)} %record_ref.1) | copy-start | bytes 245764
  20.4 0.7 %copy-start.4 = (s32[32]{0:T(128)S(1)}, s32[32]{0:T(128)}, u32[]{:S(2)}) copy-start(s32[32]{0:T(128)} %count_at.1) | copy-start | bytes 388
  20.4 0.7 %copy-start.5 = (f32[12]{0:T(128)S(1)}, f32[12]{0:T(128)}, u32[]{:S(2)}) copy-start(f32[12]{0:T(128)} %steam_ref.1) | copy-start | bytes 148
